TPU v7x, 256 devices: a whole 4x4x8 slice. The times are simulated.
256 devices in a mesh: req: 64 (over y, z, core), mlp: 4 (over x).
Axes of the slice: x: 4, y: 4, z: 8, core: 2. Of those that a mesh axis runs over, the one named last changes fastest.
Arguments:
- queries: bfloat16 [64, 2, 16, 2, 1536], P('req', None, 'mlp'), may hold values from -64 to 64
- new_kv: bfloat16 [64, 2, 16, 2, 256], P('req', None, 'mlp'), may hold values from -9 to 9
- residual: bfloat16 [64, 2, 16, 2, 1536], P('req', None, 'mlp'), may hold values from -3 to 3
- prompt_kv: bfloat16 [64, 1024, 256], P('req'), may hold values from -9 to 9
- tail_kv: bfloat16 [64, 16, 64, 256], P('req', 'mlp'), may hold values from -9 to 9
- page_pool: bfloat16 [16384, 20, 256], P(('req', 'mlp')), may hold values from -9 to 9
- page_holder: int32 [256, 64], P(('req', 'mlp')), may hold values from 0 to 63, as said below
- serve_slot: int32 [256, 64], P(('req', 'mlp')), may hold values from 0 to 63
- prompt_len: int32 [64, 2], P('req'), may hold values from 512 to 32768
- tail_len: int32 [64, 2, 16], P('req', None, 'mlp'), may hold values from 1 to 62, 496 in all within a row
- w_out: bfloat16 [1536, 1536], P('mlp'), may hold values from -0.15625 to 0.15625
- norm_mlp: float32 [1536], replicated, may hold values from 0.25 to 1.75
- w_gate: bfloat16 [1536, 4608], P(None, 'mlp'), may hold values from -0.15625 to 0.15625
- w_up: bfloat16 [1536, 4608], P(None, 'mlp'), may hold values from -0.15625 to 0.15625
- w_down: bfloat16 [4608, 1536], P('mlp'), may hold values from -0.09375 to 0.09375
- norm_final: float32 [1536], replicated, may hold values from 0.25 to 1.75
- w_score: float32 [1536], replicated, may hold values from -0.15625 to 0.15625
Outputs:
- scores: float32 [64, 2, 16, 2], P('req', None, 'mlp')
- hidden_out: bfloat16 [64, 2, 16, 2, 1536], P('req', None, 'mlp')
- tails_out: bfloat16 [64, 2, 16, 64, 256], P('req', None, 'mlp')
Inputs may be any that keep to these rules, and one draw needn't show every extreme that they name: Each row of page_holder names every req index once.
All inputs are finite; a program needn't handle non-finite values. No bound on the sum of `tail_len` on one device may be relied on, other than what follows from the above.
Results may differ from a plain program's by a relative error of at most 0.015.
Values may be sent and summed in bfloat16 or wider, within the bound.
No kernel may reach another device: no remote copies, remote signals or barrier semaphores. Data moves between devices by JAX's collectives and lax.ppermute only.
A program may use at most 64 MiB of HBM per device.

v0:
```python
import jax
import jax.numpy as jnp
from jax import lax
from jax.sharding import PartitionSpec as P


def attend(query, fresh, window, tails, plen, tlen):
    count = query.shape[0]
    size = window.shape[-1] // 2
    q = query.reshape(count, 2, -1, size)
    scale = 1.0 / jnp.sqrt(jnp.float32(size))
    s_win = (
        jnp.einsum("sthd,kd->sthk", q, window[:, :size], preferred_element_type=jnp.float32) * scale
    )
    s_tail = (
        jnp.einsum("sthd,sjd->sthj", q, tails[..., :size], preferred_element_type=jnp.float32)
        * scale
    )
    s_new = (
        jnp.einsum("sthd,sud->sthu", q, fresh[..., :size], preferred_element_type=jnp.float32)
        * scale
    )
    tpos = tlen[:, None] + jnp.arange(2, dtype=jnp.int32)[None, :]
    kw = jnp.arange(window.shape[0], dtype=jnp.int32)[None, None, None, :]
    ok_win = (kw >= window.shape[0] - plen) & (kw > tpos[:, :, None, None])
    kt = jnp.arange(tails.shape[1], dtype=jnp.int32)[None, None, None, :]
    ok_tail = kt < tlen[:, None, None, None]
    steps = jnp.arange(2, dtype=jnp.int32)
    ok_new = steps[None, None, None, :] <= steps[None, :, None, None]
    s_win = jnp.where(ok_win, s_win, -1e30)
    s_tail = jnp.where(ok_tail, s_tail, -1e30)
    s_new = jnp.where(ok_new, s_new, -1e30)
    top = jnp.maximum(jnp.maximum(s_win.max(-1), s_tail.max(-1)), s_new.max(-1))[..., None]
    e_win = jnp.where(ok_win, jnp.exp(s_win - top), 0.0)
    e_tail = jnp.where(ok_tail, jnp.exp(s_tail - top), 0.0)
    e_new = jnp.where(ok_new, jnp.exp(s_new - top), 0.0)
    total = (
        e_win.sum(-1, keepdims=True) + e_tail.sum(-1, keepdims=True) + e_new.sum(-1, keepdims=True)
    )
    p_win = (e_win / total).astype(jnp.bfloat16)
    p_tail = (e_tail / total).astype(jnp.bfloat16)
    p_new = (e_new / total).astype(jnp.bfloat16)
    out = jnp.einsum("sthk,kd->sthd", p_win, window[:, size:], preferred_element_type=jnp.float32)
    out = out + jnp.einsum(
        "sthj,sjd->sthd", p_tail, tails[..., size:], preferred_element_type=jnp.float32
    )
    out = out + jnp.einsum(
        "sthu,sud->sthd", p_new, fresh[..., size:], preferred_element_type=jnp.float32
    )
    return out.reshape(count, 2, -1).astype(jnp.bfloat16)


def extend(tails, fresh, tlen):
    rows = jnp.arange(tails.shape[1], dtype=jnp.int32)[None, :, None]
    lead = tlen[:, None, None]
    out = jnp.where(rows == lead, fresh[:, 0][:, None, :], tails)
    return jnp.where(rows == lead + 1, fresh[:, 1][:, None, :], out)


def rms_scale(values):
    return values * lax.rsqrt(jnp.mean(values * values, axis=-1, keepdims=True) + 1e-06)


def on_device(
    queries,
    new_kv,
    residual,
    prompt_kv,
    tail_kv,
    page_pool,
    page_holder,
    serve_slot,
    prompt_len,
    tail_len,
    w_out,
    norm_mlp,
    w_gate,
    w_up,
    w_down,
    norm_final,
    w_score,
):
    samp_dev = queries.shape[2]
    width = residual.shape[-1]
    kv_width = new_kv.shape[-1]
    win_rows = prompt_kv.shape[1]
    tail_rows = tail_kv.shape[2]
    outgoing = jnp.take(page_pool, serve_slot[0], axis=0)
    arrived = lax.all_to_all(outgoing, "req", split_axis=0, concat_axis=0, tiled=True)
    fetched = jnp.take(arrived, page_holder[0], axis=0).reshape(-1, kv_width)
    moved_window = fetched[:win_rows]
    moved_tails = fetched[win_rows:].reshape(samp_dev, tail_rows, kv_width)
    first = attend(
        queries[0, 0], new_kv[0, 0], prompt_kv[0], tail_kv[0], prompt_len[0, 0], tail_len[0, 0]
    )
    second = attend(
        queries[0, 1], new_kv[0, 1], moved_window, moved_tails, prompt_len[0, 1], tail_len[0, 1]
    )
    attn = jnp.stack([first, second])[None]
    tails_out = jnp.stack(
        [
            extend(tail_kv[0], new_kv[0, 0], tail_len[0, 0]),
            extend(moved_tails, new_kv[0, 1], tail_len[0, 1]),
        ]
    )[None]
    block_width = w_out.shape[0]
    position = lax.axis_index("mlp")
    every = lax.all_gather(attn, "mlp", axis=2, tiled=True)
    block = lax.dynamic_slice_in_dim(every, position * block_width, block_width, 4)
    partial_sum = jnp.dot(block.reshape(-1, block_width), w_out, preferred_element_type=jnp.float32)
    mixed = lax.psum(partial_sum, "mlp")
    res_all = lax.all_gather(residual, "mlp", axis=2, tiled=True).reshape(-1, width)
    h1_all = (res_all.astype(jnp.float32) + mixed).astype(jnp.bfloat16)
    h1_own = lax.dynamic_slice_in_dim(
        h1_all.reshape(2, -1, 2, width), position * samp_dev, samp_dev, 1
    )
    normed = (rms_scale(h1_all.astype(jnp.float32)) * norm_mlp).astype(jnp.bfloat16)
    gate = jnp.dot(normed, w_gate, preferred_element_type=jnp.float32)
    up = jnp.dot(normed, w_up, preferred_element_type=jnp.float32)
    act = (jax.nn.gelu(gate, approximate=True) * up).astype(jnp.bfloat16)
    down_terms = jnp.dot(act, w_down, preferred_element_type=jnp.float32).reshape(2, -1, 2, width)
    down_own = lax.psum_scatter(
        down_terms.astype(jnp.bfloat16), "mlp", scatter_dimension=1, tiled=True
    ).astype(jnp.float32)
    h2 = h1_own.astype(jnp.float32) + down_own
    scores = jnp.sum(rms_scale(h2) * norm_final * w_score, axis=-1)
    return (scores[None], h2.astype(jnp.bfloat16)[None], tails_out)


def solution(mesh):
    placed = (
        P("req", None, "mlp", None, None),
        P("req", None, "mlp", None, None),
        P("req", None, "mlp", None, None),
        P("req", None, None),
        P("req", "mlp", None, None),
        P(("req", "mlp"), None, None),
        P(("req", "mlp"), None),
        P(("req", "mlp"), None),
        P("req", None),
        P("req", None, "mlp"),
        P("mlp", None),
        P(),
        P(None, "mlp"),
        P(None, "mlp"),
        P("mlp", None),
        P(),
        P(),
    )
    return jax.shard_map(
        on_device,
        mesh=mesh,
        in_specs=placed,
        out_specs=(
            P("req", None, "mlp", None),
            P("req", None, "mlp", None, None),
            P("req", None, "mlp", None, None),
        ),
        check_vma=False,
    )
```

profile of v0, /device:TPU:32, one launch (start us, length us, event | category | flops | bytes accessed | tf_op | source)
XLA Modules:
  0.0 237.1 jit_solution(120826959070692707)
XLA Ops:
  7.2 0.8 compare_select_fusion.1
  8.0 1.3 compare_and_fusion.3
  9.3 3.7 %gather_fusion = bf16[64,20,256]{2,0,1:T(8,128)(2,1)} fusion(bf16[64,20,256]{2,0,1:T(8,128)(2,1)} %param.24, s32[1024]{0:T(1024)S(1)} %pad_clamp_fusion.1), kind=kCustom, calls=%fused_computation.clone | custom fusion | bytes 1310976 | tf_op jit(solution)/shard_map/jit(_take)/gather | solution.py:88
  13.1 1.3 broadcast_select_fusion.1
  14.4 1.3 copy.22
  15.6 12.0 %all-to-all-start = ((bf16[64,20,256]{2,1,0:T(8,128)(2,1)}), bf16[64,20,256]{2,1,0:T(8,128)(2,1)}, u32[]{:S(2)}, u32[]{:S(2)}) async-start(bf16[64,20,256]{2,1,0:T(8,128)(2,1)} %copy.22), calls=%async_computation | async-start | bytes 1572864 | tf_op jit(solution)/shard_map/all_to_all | solution.py:89
  30.8 1.4 fusion.62
  34.0 1.4 reshape_squeeze.6
  36.6 1.6 fusion.66
  38.2 1.1 fusion.68
  39.3 0.8 compare_and_fusion.1
  40.1 2.0 fusion.67
  42.1 1.3 fusion.32
  43.5 13.9 %all_gather.6 = bf16[1,2,16,2,1536]{4,3,2,1,0:T(2,128)(2,1)} all-gather(bf16[1,2,4,2,1536]{4,3,2,1,0:T(2,128)(2,1)} %param.21), channel_id=1, replica_groups=mesh['req'=64,'mlp'=4] {'mlp'}, dimensions={2}, use_global_device_ids=true | all-gather | bytes 245760 | tf_op jit(solution)/shard_map/all_gather | solution.py:112
  57.4 1.4 reshape_squeeze.7
  58.8 1.7 reshape.390
  60.5 1.3 copy.46
  61.8 1.3 copy.47
  63.0 1.3 copy.48
  64.3 1.3 copy.49
  65.5 1.3 dynamic-slice.1
  67.5 1.9 fusion.11
  69.3 1.2 compare_and_fusion.2
  70.5 1.3 broadcast_add_fusion.1
  71.8 0.7 iota_add_fusion
  72.5 1.4 compare_and_fusion
  73.8 2.1 fusion.69
  76.0 2.8 %gather_fusion.1 = bf16[64,20,256]{2,1,0:T(8,128)(2,1)} fusion(bf16[64,20,256]{2,1,0:T(8,128)(2,1)} %all-to-all-done, s32[1024]{0:T(1024)} %pad_clamp_fusion), kind=kCustom, calls=%fused_computation.1.clone | custom fusion | bytes 1310976 | tf_op jit(solution)/shard_map/jit(_take)/gather | solution.py:90
  78.7 2.2 broadcast_select_fusion
  80.9 2.0 reshape.385
  83.0 1.0 slice.118
  84.0 2.1 fusion.70
  86.0 1.5 fusion.71
  87.6 0.7 maximum_maximum_fusion
  88.8 1.4 fusion.50
  90.3 0.7 add_add_fusion.1
  90.9 1.4 fusion.25
  92.7 0.9 fusion.7
  93.6 1.4 convert_element_type.83
  94.9 1.0 fusion.33
  96.0 1.3 fusion.12
  97.3 0.7 add_add_fusion
  98.0 1.5 fusion.24
  99.4 1.1 convolution_add_fusion.1
  100.5 1.6 fusion.8
  102.1 1.4 convert_element_type.88
  103.5 0.8 pad_maximum_fusion
  104.3 12.1 %all-gather = bf16[2,16,2,1536]{3,2,1,0:T(2,128)(2,1)S(1)} all-gather(bf16[2,4,2,1536]{3,2,1,0:T(2,128)(2,1)S(1)} %pad_maximum_fusion), channel_id=2, replica_groups=mesh['req'=64,'mlp'=4] {'mlp'}, dimensions={1}, use_global_device_ids=true | all-gather | bytes 245760 | tf_op jit(solution)/shard_map/all_gather | solution.py:108
  117.1 1.4 reshape.387
  118.6 2.4 %fusion.72 = f32[64,1536]{1,0:T(8,128)} fusion(bf16[64,384]{1,0:T(8,128)(2,1)} %reshape.387, bf16[384,1536]{1,0:T(8,128)(2,1)} %param.29), kind=kOutput, calls=%fused_computation.155 | convolution fusion | flops 75497472 | bytes 1622016 | tf_op jit(solution)/shard_map/dot_general | solution.py:110
  121.0 1.3 iota_compare_fusion.3
  122.3 1.7 select_select_fusion.1
  124.0 44.4 %all-reduce.4.cloned.1.call-done = f32[64,1536]{1,0:T(8,128)} async-done(((f32[64,1536]{1,0:T(8,128)}), f32[64,1536]{1,0:T(8,128)}) %all-reduce.4.cloned.1.call-update) | async-done | bytes 393232 | tf_op jit(solution)/shard_map/psum | solution.py:111
  168.4 1.3 fusion.13
  170.3 3.5 %fusion.36 = f32[64,1152]{1,0:T(8,128)} fusion(bf16[1536,1152]{1,0:T(8,128)(2,1)} %param.31, bf16[64,1536]{1,0:T(8,128)(2,1)S(1)} %get-tuple-element.7, f32[1536]{0:T(1024)S(1)} %copy-done.14, f32[64]{0:T(128)S(1)} %add_rsqrt_fusion.1), kind=kOutput, calls=%fused_computation.77 | convolution fusion | flops 226885632 | bytes 4036864 | tf_op jit(solution)/shard_map/dot_general | solution.py:118
  173.8 4.2 %convolution_convert_fusion = bf16[64,1536]{1,0:T(8,128)(2,1)} fusion(bf16[1152,1536]{1,0:T(8,128)(2,1)S(1)} %copy-done, bf16[1536,1152]{1,0:T(8,128)(2,1)} %param.32, f32[64,1152]{1,0:T(8,128)} %fusion.36, bf16[64,1536]{1,0:T(8,128)(2,1)} %copy-done.1, f32[1536]{0:T(1024)S(1)} %copy-done.14, f32[64]{0:T(128)} %copy-done.22), kind=kOutput, calls=%fused_computation.4 | convolution fusion | flops 454213632 | bytes 7772416 | tf_op jit(solution)/shard_map/dot_general | solution.py:121
  178.1 1.7 convert_element_type.95
  179.8 1.0 select_select_fusion
  180.8 1.6 maximum_bitcast_fusion
  182.5 1.7 reshape.388
  184.1 42.9 %all-reduce.6.cloned.1.call-done = bf16[2,16,2,1536]{3,2,1,0:T(2,128)(2,1)} async-done(((bf16[2,16,2,1536]{3,2,1,0:T(2,128)(2,1)}), bf16[2,16,2,1536]{3,2,1,0:T(2,128)(2,1)}) %all-reduce.6.cloned.1.call-update) | async-done | bytes 196624
  227.1 1.0 multiply_reduce_fusion.1
  228.1 1.5 fusion.39
  229.6 0.7 copy.23
  (72 shorter events, 7.2 us)
Async XLA Ops:
  7.2 166.7 %copy-start = (bf16[1152,1536]{1,0:T(8,128)(2,1)S(1)}, bf16[1152,1536]{1,0:T(8,128)(2,1)}, u32[]{:S(2)}) copy-start(bf16[1152,1536]{1,0:T(8,128)(2,1)} %param.33) | copy-start | bytes 10616836
  13.1 15.1 %copy-start.21 = (s32[1,2,4]{2,1,0:T(2,128)S(1)}, s32[1,2,4]{2,1,0:T(2,128)}, u32[]{:S(2)}) copy-start(s32[1,2,4]{2,1,0:T(2,128)} %param.28) | copy-start | bytes 100
  13.1 19.1 %copy-start.23 = (s32[1,2]{1,0:T(1,128)S(1)}, s32[1,2]{1,0:T(1,128)}, u32[]{:S(2)}) copy-start(s32[1,2]{1,0:T(1,128)} %param.27) | copy-start | bytes 28
  13.1 20.9 %copy-start.17 = (bf16[1,2,4,2,256]{4,3,2,1,0:T(2,128)(2,1)S(1)}, bf16[1,2,4,2,256]{4,3,2,1,0:T(2,128)(2,1)}, u32[]{:S(2)}) copy-start(bf16[1,2,4,2,256]{4,3,2,1,0:T(2,128)(2,1)} %param.20) | copy-start | bytes 24580
  15.6 60.3 %all-to-all-start = ((bf16[64,20,256]{2,1,0:T(8,128)(2,1)}), bf16[64,20,256]{2,1,0:T(8,128)(2,1)}, u32[]{:S(2)}, u32[]{:S(2)}) async-start(bf16[64,20,256]{2,1,0:T(8,128)(2,1)} %copy.22), calls=%async_computation | async-start | bytes 1572864 | tf_op jit(solution)/shard_map/all_to_all | solution.py:89
  27.6 140.7 %all-reduce.4.cloned.1.call-start = ((), (), s32[]{:S(2)}) async-start(), calls=%async_computation.1 | async-start | bytes 786432 | tf_op jit(solution)/shard_map/psum | solution.py:111
  28.2 5.8 %copy-start.20 = (s32[4]{0:T(128)}, s32[4]{0:T(128)S(1)}, u32[]{:S(2)}) copy-start(s32[4]{0:T(128)S(1)} %get-tuple-element.21) | copy-start | bytes 52
  34.0 4.2 %copy-start.10 = (bf16[4,2,256]{2,1,0:T(2,128)(2,1)}, bf16[4,2,256]{2,1,0:T(2,128)(2,1)S(1)}, u32[]{:S(2)}) copy-start(bf16[4,2,256]{2,1,0:T(2,128)(2,1)S(1)} %get-tuple-element.12) | copy-start | bytes 12292
  34.0 4.1 %copy-start.12 = (bf16[4,2,256]{2,1,0:T(2,128)(2,1)}, bf16[4,2,256]{2,1,0:T(2,128)(2,1)S(1)}, u32[]{:S(2)}) copy-start(bf16[4,2,256]{2,1,0:T(2,128)(2,1)S(1)} %get-tuple-element.13) | copy-start | bytes 12292
  39.2 2.9 %copy-start.4 = (f32[4,2,12,64]{3,2,1,0:T(8,128)}, f32[4,2,12,64]{3,2,1,0:T(8,128)S(1)}, u32[]{:S(2)}) copy-start(f32[4,2,12,64]{3,2,1,0:T(8,128)S(1)} %get-tuple-element.33) | copy-start | bytes 73732
  42.1 1.4 copy-start.6
  82.9 9.4 %copy-start.3 = (bf16[1,4,64,256]{3,2,1,0:T(8,128)(2,1)S(1)}, bf16[1,4,64,256]{3,2,1,0:T(8,128)(2,1)}, u32[]{:S(2)}) copy-start(bf16[1,4,64,256]{3,2,1,0:T(8,128)(2,1)} %param.23) | copy-start | bytes 393220
  82.9 9.4 %copy-start.5 = (f32[4,2,12,64]{3,2,1,0:T(8,128)S(1)}, f32[4,2,12,64]{3,2,1,0:T(8,128)}, u32[]{:S(2)}) copy-start(f32[4,2,12,64]{3,2,1,0:T(8,128)} %copy-done.4) | copy-start | bytes 73732
  82.9 9.5 %copy-start.7 = (f32[1,8,12]{2,1,0:T(8,128)S(1)}, f32[1,8,12]{2,1,0:T(8,128)}, u32[]{:S(2)}) copy-start(f32[1,8,12]{2,1,0:T(8,128)} %copy-done.6) | copy-start | bytes 1156
  82.9 9.5 %copy-start.19 = (pred[4,64]{1,0:T(4,128)(4,1)S(1)}, pred[4,64]{1,0:T(4,128)(4,1)}, u32[]{:S(2)}) copy-start(pred[4,64]{1,0:T(4,128)(4,1)} %get-tuple-element.40) | copy-start | bytes 772
  82.9 9.7 %copy-start.13 = (bf16[4,2,256]{2,1,0:T(2,128)(2,1)S(1)}, bf16[4,2,256]{2,1,0:T(2,128)(2,1)}, u32[]{:S(2)}) copy-start(bf16[4,2,256]{2,1,0:T(2,128)(2,1)} %copy-done.12) | copy-start | bytes 12292
  82.9 9.7 %copy-start.18 = (f32[4,2,12,2]{2,3,1,0:T(2,128)S(1)}, f32[4,2,12,2]{2,3,1,0:T(2,128)}, u32[]{:S(2)}) copy-start(f32[4,2,12,2]{2,3,1,0:T(2,128)} %get-tuple-element.29) | copy-start | bytes 2308
  83.0 9.7 %copy-start.24 = (pred[2,2]{1,0:T(4,128)(4,1)S(1)}, pred[2,2]{1,0:T(4,128)(4,1)}, u32[]{:S(2)}) copy-start(pred[2,2]{1,0:T(4,128)(4,1)} %iota_compare_fusion.8) | copy-start | bytes 16
  84.0 2.1 copy-start.2
  88.3 0.6 copy-start.8
  92.4 7.0 %copy-start.9 = (f32[1,8,12]{2,1,0:T(8,128)S(1)}, f32[1,8,12]{2,1,0:T(8,128)}, u32[]{:S(2)}) copy-start(f32[1,8,12]{2,1,0:T(8,128)} %copy-done.8) | copy-start | bytes 1156
  92.4 8.1 %copy-start.11 = (bf16[4,2,256]{2,1,0:T(2,128)(2,1)S(1)}, bf16[4,2,256]{2,1,0:T(2,128)(2,1)}, u32[]{:S(2)}) copy-start(bf16[4,2,256]{2,1,0:T(2,128)(2,1)} %copy-done.10) | copy-start | bytes 12292
  98.0 72.4 %copy-start.14 = (f32[1536]{0:T(1024)S(1)}, f32[1536]{0:T(1024)}, u32[]{:S(2)}) copy-start(f32[1536]{0:T(1024)} %param.30) | copy-start | bytes 18436
  121.0 106.1 %all-reduce.6.cloned.1.call-start = ((), (), s32[]{:S(2)}) async-start(), calls=%async_computation.2 | async-start | bytes 393216
  169.6 0.7 copy-start.1
  169.7 0.7 copy-start.22
  173.8 5.9 %copy-start.15 = (bf16[4,1,256]{2,0,1:T(4,128)(2,1)S(1)}, bf16[4,1,256]{2,0,1:T(4,128)(2,1)}, u32[]{:S(2)}) copy-start(bf16[4,1,256]{2,0,1:T(4,128)(2,1)} %copy.46) | copy-start | bytes 6148
  173.8 6.0 %copy-start.16 = (bf16[4,1,256]{2,0,1:T(4,128)(2,1)S(1)}, bf16[4,1,256]{2,0,1:T(4,128)(2,1)}, u32[]{:S(2)}) copy-start(bf16[4,1,256]{2,0,1:T(4,128)(2,1)} %copy.47) | copy-start | bytes 6148
Sparse Core Ops, SparseCore 0:
  121.1 47.2 all-reduce.3
  179.9 47.1 all-reduce.5
where the time goes:
time: 240 us; the launch traced here: 237 us
  waiting for transfers between devices  87.4 us (36%)
  local copies, waits for them, and re-layouts  34.4 us (14%)
  other arithmetic  33.8 us (14%)
  matrix products  27.1 us (11%)
  blocking collectives  26.1 us (11%)
  between operations  16.2 us (7%)
  starting transfers between devices  12.1 us (5%)
    psum x1, waiting for transfers between devices, on_device(): mixed = lax.psum(partial_sum, 'mlp')  44.4 us
    unnamed x3, waiting for transfers between devices  42.9 us
    all_gather x1, blocking collectives, on_device(): lax.all_gather(residual, 'mlp', axis=2, tiled=True).reshape(-1, width)  13.9 us
    all_gather x1, blocking collectives, on_device(): every = lax.all_gather(attn, 'mlp', axis=2, tiled=True)  12.1 us
    all_to_all x1, starting transfers between devices, on_device(): lax.all_to_all(outgoing, 'req', split_axis=0, concat_axis=0, tiled=True)  12 us
    unnamed x56, local copies, waits for them, and re-layouts  8.28 us
  transfers between devices with their start and end apart: 3, of which 2 were waited for; matrix products, arithmetic and copies ran while one was open for 17% of the time, Pallas kernels for 0%

commit v1 on v0

v1 whole, which is shorter than its diff:
```python
import functools

import jax
import jax.numpy as jnp
from jax import lax
from jax.experimental import pallas as pl
from jax.experimental.pallas import tpu as pltpu
from jax.sharding import PartitionSpec as P

BF = jnp.bfloat16
F32 = jnp.float32
NEG = -1e30
VMEM = pl.BlockSpec(memory_space=pltpu.VMEM)
SMEM = pl.BlockSpec(memory_space=pltpu.SMEM)
HBM = pl.BlockSpec(memory_space=pltpu.HBM)


def call(body, outs, operands, specs, scratch=(), flops=0, nbytes=0, limit=8):
    return pl.pallas_call(
        body,
        out_shape=outs,
        in_specs=specs,
        out_specs=jax.tree.map(lambda _: VMEM, outs),
        scratch_shapes=scratch,
        cost_estimate=pl.CostEstimate(flops=flops, bytes_accessed=nbytes, transcendentals=0),
        compiler_params=pltpu.CompilerParams(vmem_limit_bytes=limit << 20),
    )(*operands)


def iota(shape, axis):
    return lax.broadcasted_iota(jnp.int32, shape, axis)


def pick_pages(pool_ref, slot_ref, out_ref, scr):
    rows, slots, width = pool_ref.shape
    dests = slot_ref.shape[1]
    half = width // 2
    hot = (iota((slots, dests), 0) == slot_ref[...]).astype(F32).T.astype(BF)
    for i in range(rows):
        got = jnp.dot(hot, pool_ref[i], preferred_element_type=F32)
        scr[pl.ds(i, dests, stride=2 * rows), :] = got[:, :half]
        scr[pl.ds(rows + i, dests, stride=2 * rows), :] = got[:, half:]
    out_ref[...] = scr[...].astype(BF)


def load_rows(ref, q, lanes=None):
    parts = [ref[0, q, s].astype(F32) for s in range(ref.shape[2])]
    return jnp.concatenate(parts, axis=0)


def stack_heads(q8, size):
    heads = q8.shape[1] // size
    parts = [q8[:, h * size : (h + 1) * size] for h in range(heads)]
    return jnp.concatenate(parts, axis=0).astype(BF)


def row_lengths(tlen_ref, q, count):
    r = iota((2 * count, 1), 0)
    sample, token = r >> 1, r & 1
    length = jnp.zeros((2 * count, 1), jnp.int32)
    for s in range(count):
        length = jnp.where(sample == s, tlen_ref[0, q, s], length)
    return sample, token, length


def to_bias(visible):
    return jnp.where(visible, 0.0, NEG).astype(F32)


def window_bias(pos, plen, win, tail, sample, token, length):
    back = pos - win
    in_win = (pos < win) & (pos >= win - plen) & (pos > length + token)
    first = sample * tail
    in_tail = (back >= first) & (back < first + length)
    return to_bias(in_win | in_tail)


def new_bias(sample, token, count):
    c = iota((1, 2 * count), 1)
    return to_bias(((c >> 1) == sample) & ((c & 1) <= token))


def attend(qh, segments, rows, size):
    scale = 1.0 / jnp.sqrt(F32(size))
    heads = qh.shape[0] // rows
    scored = []
    top = None
    for keys, _, bias, _ in segments:
        s = lax.dot_general(qh, keys, (((1,), (1,)), ((), ())), preferred_element_type=F32)
        n = s.shape[1]
        s = s.reshape(heads, rows, n) * scale + bias[None]
        s = s.reshape(heads * rows, n)
        scored.append(s)
        m = s.max(axis=1, keepdims=True)
        top = m if top is None else jnp.maximum(top, m)
    total = None
    acc = None
    for s, (_, values, _, shift) in zip(scored, segments):
        e = jnp.exp(s - top)
        t = e.sum(axis=1, keepdims=True)
        if shift:
            e = pltpu.roll(e, shift, axis=1)
        o = jnp.dot(e.astype(BF), values, preferred_element_type=F32)
        total = t if total is None else total + t
        acc = o if acc is None else acc + o
    acc = acc / total
    return jnp.concatenate([acc[h * rows : (h + 1) * rows] for h in range(heads)], axis=1)


def resident(win, tail, size, page, q_ref, new_ref, kv_ref, tails_ref, holder_ref, plen_ref, tlen_ref, out_ref, bias_ref):
    count = q_ref.shape[2]
    rows = 2 * count
    sample, token, length = row_lengths(tlen_ref, 0, count)
    q8 = load_rows(q_ref, 0)
    qh = stack_heads(q8, size)
    fresh = load_rows(new_ref, 0).astype(BF)
    tails = tails_ref[0].reshape(count * tail, 2 * size)
    window = kv_ref[0]
    wb = window_bias(iota((1, win), 1), plen_ref[0, 0], win, tail, sample, token, length)
    tb = window_bias(win + iota((1, count * tail), 1), plen_ref[0, 0], win, tail, sample, token, length)
    nb = new_bias(sample, token, count)
    out = attend(
        qh,
        [
            (window[:, :size], window[:, size:], wb, 0),
            (tails[:, :size], tails[:, size:], tb, 0),
            (fresh[:, :size], fresh[:, size:], nb, 0),
        ],
        rows,
        size,
    )
    out_ref[...] = out.astype(BF)
    n = bias_ref.shape[1]
    c = iota((1, n), 1)
    pages = holder_ref.shape[1]
    per = n // pages
    origin = (c * (-(-(1 << 21) // per))) >> 21
    inside = c - origin * per
    base = jnp.zeros((1, n), jnp.int32)
    for p in range(pages):
        base = jnp.where(origin == holder_ref[0, p], p * page, base)
    pos = jnp.where(inside < page, base + inside, 1 << 20)
    sample, token, length = row_lengths(tlen_ref, 1, count)
    bias_ref[...] = window_bias(pos, plen_ref[0, 1], win, tail, sample, token, length)


def moved(size, page, where_ref, q_ref, new_ref, arr_ref, bias_ref, first_ref, res_ref, norm_ref, own_hbm, a1, a2, a3, b1, b2, b3, h1_ref, normed_ref, wown, attn, sem):
    fetch = pltpu.make_async_copy(own_hbm, wown, sem)
    fetch.start()
    wa, wb = (a1, a2, a3), (b1, b2, b3)
    count = q_ref.shape[2]
    rows = 2 * count
    r = iota((rows, 1), 0)
    qh = stack_heads(load_rows(q_ref, 1), size)
    fresh = load_rows(new_ref, 1).astype(BF)
    nb = new_bias(r >> 1, r & 1, count)
    arr = arr_ref[...]
    second = attend(
        qh,
        [(arr, arr, bias_ref[...], page), (fresh[:, :size], fresh[:, size:], nb, 0)],
        rows,
        size,
    )
    attn[...] = jnp.concatenate([first_ref[...].astype(F32), second], axis=0).astype(BF)
    me, core = where_ref[0, 0], where_ref[0, 1]
    block = wown.shape[0]
    n_mlp = len(wa) + 1

    def piece(k):
        rb = lax.rem(me - k + n_mlp, n_mlp)
        return attn[:, pl.ds(pl.multiple_of(rb * block, 128), block)]

    same = other = None
    for k in range(1, n_mlp):
        x = piece(k)
        s = jnp.dot(x, wa[k - 1][...], preferred_element_type=F32)
        o = jnp.dot(x, wb[k - 1][...], preferred_element_type=F32)
        same = s if same is None else same + s
        other = o if other is None else other + o
    fetch.wait()
    own = jnp.dot(piece(0), wown[...], preferred_element_type=F32)
    low = core == 0
    left = jnp.where(low, same, other)
    right = jnp.where(low, other, same)
    mixed = own + jnp.concatenate([left, right], axis=1)
    res = jnp.concatenate([load_rows(res_ref, 0), load_rows(res_ref, 1)], axis=0)
    h1 = (res + mixed).astype(BF)
    h1_ref[...] = h1
    f = h1.astype(F32)
    inv = lax.rsqrt(jnp.mean(f * f, axis=1, keepdims=True) + 1e-6)
    normed_ref[...] = (f * inv * norm_ref[...]).astype(BF)


def write_tails(win, page, arr_ref, tails_ref, new_ref, holder_ref, tlen_ref, out_ref, scr):
    count, tail, width = tails_ref.shape[1:]
    half = width // 2
    pages = holder_ref.shape[1]
    start = win // page
    lead = win - start * page
    for p in range(start, pages):
        block = arr_ref[holder_ref[0, p]].astype(F32)
        off = (p - start) * page
        scr[off : off + page, :half] = block[:page]
        scr[off : off + page, half:] = block[page:]
    row = iota((tail, 1), 0)
    for q in range(2):
        for s in range(count):
            if q == 0:
                old = tails_ref[0, s].astype(F32)
            else:
                old = scr[lead + s * tail : lead + (s + 1) * tail, :]
            fresh = new_ref[0, q, s].astype(F32)
            length = tlen_ref[0, q, s]
            t = jnp.where(row == length, fresh[0:1], old)
            t = jnp.where(row == length + 1, fresh[1:2], t)
            out_ref[0, q, s] = t.astype(BF)


def mlp(x0, x1, x2, x3, wg_hbm, wu_hbm, wd_hbm, y0, y1, y2, y3, wg, wu, wd, sems):
    cuts = 3
    kin, kout = wg.shape[0] // cuts, wd.shape[0] // cuts
    ups, downs = [], []
    for c in range(cuts):
        at = pl.ds(c * kin, kin)
        ups.append(
            (
                pltpu.make_async_copy(wg_hbm.at[at], wg.at[at], sems.at[3 * c]),
                pltpu.make_async_copy(wu_hbm.at[at], wu.at[at], sems.at[3 * c + 1]),
            )
        )
        at = pl.ds(c * kout, kout)
        downs.append(pltpu.make_async_copy(wd_hbm.at[at], wd.at[at], sems.at[3 * c + 2]))
    for g, u in ups:
        g.start()
        u.start()
    for d in downs:
        d.start()
    x = jnp.concatenate([x0[...], x1[...], x2[...], x3[...]], axis=0)
    gate = up = None
    for c, (g, u) in enumerate(ups):
        part = x[:, c * kin : (c + 1) * kin]
        g.wait()
        t = jnp.dot(part, wg[c * kin : (c + 1) * kin], preferred_element_type=F32)
        gate = t if gate is None else gate + t
        u.wait()
        t = jnp.dot(part, wu[c * kin : (c + 1) * kin], preferred_element_type=F32)
        up = t if up is None else up + t
    act = (jax.nn.gelu(gate, approximate=True) * up).astype(BF)
    y = None
    for c, d in enumerate(downs):
        d.wait()
        t = jnp.dot(act[:, c * kout : (c + 1) * kout], wd[c * kout : (c + 1) * kout], preferred_element_type=F32)
        y = t if y is None else y + t
    n = x0.shape[0]
    y0[...] = y[:n]
    y1[...] = y[n : 2 * n].astype(BF)
    y2[...] = y[2 * n : 3 * n].astype(BF)
    y3[...] = y[3 * n :].astype(BF)


def finish(h1_ref, y0, y1, y2, y3, nf_ref, ws_ref, score_ref, hid_ref):
    h2 = h1_ref[...].astype(F32) + (y0[...] + y1[...].astype(F32) + y2[...].astype(F32) + y3[...].astype(F32))
    inv = lax.rsqrt(jnp.mean(h2 * h2, axis=1, keepdims=True) + 1e-6)
    sc = jnp.sum(h2 * inv * nf_ref[...] * ws_ref[...], axis=1, keepdims=True)
    n = h2.shape[0]
    count = n // 4
    row, col = iota((n, count), 0), iota((n, count), 1)
    for q in range(2):
        for t in range(2):
            hit = row == q * 2 * count + col * 2 + t
            score_ref[0, q, t : t + 1, :] = jnp.sum(jnp.where(hit, sc, 0.0), axis=0, keepdims=True)
        for s in range(count):
            r = q * 2 * count + s * 2
            hid_ref[0, q, s] = h2[r : r + 2].astype(BF)


def on_device(
    n_req,
    n_mlp,
    queries,
    new_kv,
    residual,
    prompt_kv,
    tail_kv,
    page_pool,
    page_holder,
    serve_slot,
    prompt_len,
    tail_len,
    w_out,
    norm_mlp,
    w_gate,
    w_up,
    w_down,
    norm_final,
    w_score,
):
    samp, width = residual.shape[2], residual.shape[-1]
    size = new_kv.shape[-1] // 2
    win, tail = prompt_kv.shape[1], tail_kv.shape[2]
    slots, page = page_pool.shape[:2]
    rows = 4 * samp
    me = lax.axis_index("mlp")
    core = lax.rem(lax.axis_index("req"), 2)
    place = jnp.stack([me, core]).astype(jnp.int32)[None]
    arrived_rows = n_req * 2 * page

    def shift(x, k):
        return lax.ppermute(x, "mlp", [(i, (i + k) % n_mlp) for i in range(n_mlp)])

    half = width // 2
    mine = lax.dynamic_slice_in_dim(w_out, core * half, half, 1)
    slot, mine = lax.optimization_barrier((serve_slot, mine))
    same = [shift(mine, k) for k in range(1, n_mlp)]

    outgoing = call(
        pick_pages,
        jax.ShapeDtypeStruct((arrived_rows, size), BF),
        (jnp.transpose(page_pool, (1, 0, 2)), slot),
        [VMEM, VMEM],
        [pltpu.VMEM((arrived_rows, size), F32)],
        flops=100_000_000,
        nbytes=1_400_000,
    )
    arrived = lax.all_to_all(
        outgoing.reshape(n_req, 2 * page, size), "req", split_axis=0, concat_axis=0, tiled=True
    )
    q_late, outgoing = lax.optimization_barrier((queries, outgoing))
    first, bias = call(
        functools.partial(resident, win, tail, size, page),
        (jax.ShapeDtypeStruct((2 * samp, width), BF), jax.ShapeDtypeStruct((2 * samp, arrived_rows), F32)),
        (q_late, new_kv, prompt_kv, tail_kv, page_holder, prompt_len, tail_len),
        [VMEM, VMEM, VMEM, VMEM, SMEM, SMEM, SMEM],
        flops=100_000_000,
        nbytes=1_000_000,
    )
    *same, first = lax.optimization_barrier((*same, first))
    other = [lax.ppermute(a, "req", [(i, i ^ 1) for i in range(n_req)]) for a in same]
    tails_out = call(
        functools.partial(write_tails, win, page),
        jax.ShapeDtypeStruct((1, 2) + tail_kv.shape[1:], BF),
        (arrived, tail_kv, new_kv, page_holder, tail_len),
        [VMEM, VMEM, VMEM, SMEM, SMEM],
        [pltpu.VMEM(((n_req - win // page) * page, 2 * size), F32)],
        flops=1_000_000,
        nbytes=1_500_000,
    )
    block = w_out.shape[0]
    h1, normed = call(
        functools.partial(moved, size, page),
        (jax.ShapeDtypeStruct((rows, width), BF), jax.ShapeDtypeStruct((rows, width), BF)),
        (
            place,
            queries,
            new_kv,
            arrived.reshape(arrived_rows, size),
            bias,
            first,
            residual,
            norm_mlp[None],
            w_out,
            *same,
            *other,
        ),
        [SMEM] + [VMEM] * 7 + [HBM] + [VMEM] * 6,
        [
            pltpu.VMEM((block, width), BF),
            pltpu.VMEM((rows, width), BF),
            pltpu.SemaphoreType.DMA,
        ],
        limit=14,
        flops=200_000_000,
        nbytes=6_000_000,
    )
    others = [shift(normed, k) for k in range(1, n_mlp)]
    row_bf = jax.ShapeDtypeStruct((rows, width), BF)
    hid = w_gate.shape[1]
    ys = call(
        mlp,
        (jax.ShapeDtypeStruct((rows, width), F32), row_bf, row_bf, row_bf),
        (normed, *others, w_gate, w_up, w_down),
        [VMEM] * 4 + [HBM] * 3,
        [
            pltpu.VMEM((width, hid), BF),
            pltpu.VMEM((width, hid), BF),
            pltpu.VMEM((hid, width), BF),
            pltpu.SemaphoreType.DMA((9,)),
        ],
        flops=700_000_000,
        nbytes=11_000_000,
        limit=16,
    )
    back = [shift(ys[k], -k) for k in range(1, n_mlp)]
    scores, hidden = call(
        finish,
        (jax.ShapeDtypeStruct((1, 2, 2, samp), F32), jax.ShapeDtypeStruct(residual.shape, BF)),
        (h1, ys[0], *back, norm_final[None], w_score[None]),
        [VMEM] * 7,
        flops=1_000_000,
        nbytes=500_000,
    )
    return (jnp.transpose(scores, (0, 1, 3, 2)), hidden, tails_out)


def solution(mesh):
    placed = (
        P("req", None, "mlp", None, None),
        P("req", None, "mlp", None, None),
        P("req", None, "mlp", None, None),
        P("req", None, None),
        P("req", "mlp", None, None),
        P(("req", "mlp"), None, None),
        P(("req", "mlp"), None),
        P(("req", "mlp"), None),
        P("req", None),
        P("req", None, "mlp"),
        P("mlp", None),
        P(),
        P(None, "mlp"),
        P(None, "mlp"),
        P("mlp", None),
        P(),
        P(),
    )
    return jax.shard_map(
        functools.partial(on_device, mesh.shape["req"], mesh.shape["mlp"]),
        mesh=mesh,
        in_specs=placed,
        out_specs=(
            P("req", None, "mlp", None),
            P("req", None, "mlp", None, None),
            P("req", None, "mlp", None, None),
        ),
        check_vma=False,
    )
```

time: 240 us -> 85.1 us (0.35)
  waiting for transfers between devices: 87.4 us -> 30 us
  other arithmetic: 33.8 us -> 0.08 us
  matrix products: 27.1 us -> 0 us
  blocking collectives: 26.1 us -> 0 us
  local copies, waits for them, and re-layouts: 34.4 us -> 12.4 us
  between operations: 16.2 us -> 0.8 us
  starting transfers between devices: 12.1 us -> 27.3 us
  Pallas kernels: 0 us -> 13.6 us
    psum x1 -> x0, waiting for transfers between devices: 44.4 us -> none  [on_device(): mixed = lax.psum(partial_sum, 'mlp')]
    unnamed x3 -> x0, waiting for transfers between devices: 42.9 us -> none
    ppermute x0 -> x12, waiting for transfers between devices: none -> 30 us  [the longest x9 26.6 us: shift(): return lax.ppermute(x, 'mlp', [(i, (i + k) % n_mlp) for i in range(n_mlp)])]
    dot_general x15 -> x0, matrix products: 27.1 us -> none  [the longest x1 4.23 us: on_device(): jnp.dot(act, w_down, preferred_element_type=jnp.float32)]
    all_gather x2 -> x0, blocking collectives: 26.1 us -> none  [the longest x1 13.9 us: on_device(): lax.all_gather(residual, 'mlp', axis=2, tiled=True).reshape(-1, width)]
    ppermute x0 -> x12, starting transfers between devices: none -> 15.5 us  [the longest x9 15 us: shift(): return lax.ppermute(x, 'mlp', [(i, (i + k) % n_mlp) for i in range(n_mlp)])]
    pallas_call x0 -> x6, Pallas kernels: none -> 13.6 us  [call(): pl.pallas_call(body, out_shape=outs, in_specs=specs, out_specs=jax.tree.m...]
    reduce_sum x7 -> x0, other arithmetic: 9.22 us -> none  [the longest x2 3.19 us: attend(): e_win.sum(-1, keepdims=True) + e_tail.sum(-1, keepdims=True)]
  transfers between devices with their start and end apart: 3 -> 13, of which waited for: 2 -> 9; matrix products, arithmetic and copies ran while one was open for 17% -> 0% of each run, Pallas kernels for 0% -> 3%
where the time goes in v1:
time: 85.1 us; the launch traced here: 84.2 us
  waiting for transfers between devices  30 us (35%)
  starting transfers between devices  27.3 us (32%)
  Pallas kernels  13.6 us (16%)
  local copies, waits for them, and re-layouts  12.4 us (15%)
    ppermute x9, waiting for transfers between devices, shift(): return lax.ppermute(x, 'mlp', [(i, (i + k) % n_mlp) for i in range(n_mlp)])  26.6 us
    ppermute x9, starting transfers between devices, shift(): return lax.ppermute(x, 'mlp', [(i, (i + k) % n_mlp) for i in range(n_mlp)])  15 us
    pallas_call x6, Pallas kernels, call(): pl.pallas_call(body, out_shape=outs, in_specs=specs, out_specs=jax.tree.m...  13.6 us
    all_to_all x1, starting transfers between devices, on_device(): lax.all_to_all(outgoing.reshape(n_req, 2 * page, size), 'req', split_axis...  11.8 us
    unnamed x38, local copies, waits for them, and re-layouts  10.4 us
    ppermute x3, waiting for transfers between devices, on_device(): lax.ppermute(a, 'req', [(i, i ^ 1) for i in range(n_req)])  3.43 us
    dynamic_slice x1, local copies, waits for them, and re-layouts, on_device(): mine = lax.dynamic_slice_in_dim(w_out, core * half, half, 1)  2.03 us
  transfers between devices with their start and end apart: 13, of which 9 were waited for; matrix products, arithmetic and copies ran while one was open for 0% of the time, Pallas kernels for 3%

profile of v1, /device:TPU:32, one launch (start us, length us, event | category | flops | bytes accessed | tf_op | source)
XLA Modules:
  0.0 84.2 jit_solution(12159043990675980411)
XLA Ops:
  0.6 0.0 copy-start.3
  0.6 0.0 copy-start.10
  0.7 0.0 copy-start.13
  0.7 0.0 copy-start.15
  0.7 0.0 copy-start.12
  0.7 0.0 copy-start.16
  0.7 2.0 %constant_dynamic-slice_fusion = bf16[384,768]{1,0:T(8,128)(2,1)} fusion(bf16[384,1536]{1,0:T(8,128)(2,1)} %own_hbm.1, s32[]{:T(128)S(6)} %select_n.3), kind=kLoop, calls=%fused_computation.1 | loop fusion | bytes 1179652 | tf_op jit(solution)/shard_map/dynamic_slice | solution.py:312
  2.7 0.0 copy-start.4
  2.7 1.1 %copy-done.4 = bf16[64,20,256]{2,0,1:T(8,128)(2,1)S(1)} copy-done((bf16[64,20,256]{2,0,1:T(8,128)(2,1)S(1)}, bf16[64,20,256]{2,0,1:T(8,128)(2,1)}, u32[]{:S(2)}) %copy-start.4) | copy-done | bytes 655384
  3.8 0.0 copy-start.14
  3.8 0.7 copy-done.14
  4.5 1.4 %shard_map.184 = bf16[2560,128]{1,0:T(8,128)(2,1)} custom-call(bf16[20,64,256]{2,1,0:T(8,128)(2,1)S(1)} %bitcast.9, s32[1,64]{1,0:T(1,128)S(1)} %copy-done.14), custom_call_target="tpu_custom_call" | custom-call | flops 100000000 | bytes 1400000 | tf_op jit(solution)/shard_map/pallas_call | solution.py:19
  5.8 11.8 %all-to-all-start = ((bf16[64,40,128]{2,1,0:T(8,128)(2,1)}), bf16[64,40,128]{2,1,0:T(8,128)(2,1)S(1)}, u32[]{:S(2)}, u32[]{:S(2)}) async-start(bf16[64,40,128]{2,1,0:T(8,128)(2,1)} %bitcast.4), calls=%async_computation | async-start | bytes 1310720 | tf_op jit(solution)/shard_map/all_to_all | solution.py:325
  17.6 1.6 %collective-permute-start = (bf16[384,768]{1,0:T(8,128)(2,1)}, bf16[384,768]{1,0:T(8,128)(2,1)S(1)}, u32[]{:S(2)}, u32[]{:S(2)}) collective-permute-start(bf16[384,768]{1,0:T(8,128)(2,1)} %constant_dynamic-slice_fusion), channel_id=1, source_target_pairs={{0,1},{1,2},{2,3},{3,0},{4,5},{5,6},{6,7},{7,4},{8,9},{9,10},{10,1... | collective-permute-start | bytes 1769480 | tf_op jit(solution)/shard_map/ppermute | solution.py:309
  19.2 2.7 %collective-permute-start.1 = (bf16[384,768]{1,0:T(8,128)(2,1)}, bf16[384,768]{1,0:T(8,128)(2,1)S(1)}, u32[]{:S(2)}, u32[]{:S(2)}) collective-permute-start(bf16[384,768]{1,0:T(8,128)(2,1)} %constant_dynamic-slice_fusion), channel_id=1, source_target_pairs={{0,2},{1,3},{2,0},{3,1},{4,6},{5,7},{6,4},{7,5},{8,10},{9,11},{10,... | collective-permute-start | bytes 1769480 | tf_op jit(solution)/shard_map/ppermute | solution.py:309
  21.9 1.4 %collective-permute-start.2 = (bf16[384,768]{1,0:T(8,128)(2,1)}, bf16[384,768]{1,0:T(8,128)(2,1)}, u32[]{:S(2)}, u32[]{:S(2)}) collective-permute-start(bf16[384,768]{1,0:T(8,128)(2,1)} %constant_dynamic-slice_fusion), channel_id=1, source_target_pairs={{0,3},{1,0},{2,1},{3,2},{4,7},{5,4},{6,5},{7,6},{8,11},{9,8},{10,9... | collective-permute-start | bytes 1769480 | tf_op jit(solution)/shard_map/ppermute | solution.py:309
  23.3 0.0 copy-done.10
  23.3 0.0 copy-done.13
  23.3 0.0 copy-done.15
  23.3 0.0 copy-done.12
  23.4 0.0 copy-start.5
  23.4 1.0 %copy-done.5 = bf16[1,1024,256]{2,1,0:T(8,128)(2,1)S(1)} copy-done((bf16[1,1024,256]{2,1,0:T(8,128)(2,1)S(1)}, bf16[1,1024,256]{2,1,0:T(8,128)(2,1)}, u32[]{:S(2)}) %copy-start.5) | copy-done | bytes 524312
  24.4 0.0 copy-start.6
  24.4 0.9 %copy-done.6 = bf16[1,4,64,256]{3,2,1,0:T(8,128)(2,1)S(1)} copy-done((bf16[1,4,64,256]{3,2,1,0:T(8,128)(2,1)S(1)}, bf16[1,4,64,256]{3,2,1,0:T(8,128)(2,1)}, u32[]{:S(2)}) %copy-start.6) | copy-done | bytes 131096
  25.3 0.8 copy-done.8
  26.1 1.5 %shard_map.185 = (bf16[8,1536]{1,0:T(8,128)(2,1)S(1)}, f32[8,2560]{1,0:T(8,128)S(1)}) custom-call(bf16[1,2,4,2,1536]{4,3,2,1,0:T(2,128)(2,1)S(1)} %copy-done.8, bf16[1,2,4,2,256]{4,3,2,1,0:T(2,128)(2,1)S(1)} %copy-done.10, bf16[1,1024,256]{2,1,0:T(8,128)(2,1)S(1)} %copy-done.5, bf16[1,4,64,256]{3,2,1,0:T(8,128)(2,1)S(1)} %copy-done.6, ...), custom_call_target="tpu_custom_call" | custom-call | flops 100000000 | bytes 1000000 | tf_op jit(solution)/shard_map/pallas_call | solution.py:19
  27.6 6.9 %collective-permute-done.a1 = bf16[384,768]{1,0:T(8,128)(2,1)S(1)} collective-permute-done((bf16[384,768]{1,0:T(8,128)(2,1)}, bf16[384,768]{1,0:T(8,128)(2,1)S(1)}, u32[]{:S(2)}, u32[]{:S(2)}) %collective-permute-start) | collective-permute-done | bytes 589856 | tf_op jit(solution)/shard_map/ppermute | solution.py:309
  34.5 13.6 %collective-permute-done.1.a2 = bf16[384,768]{1,0:T(8,128)(2,1)S(1)} collective-permute-done((bf16[384,768]{1,0:T(8,128)(2,1)}, bf16[384,768]{1,0:T(8,128)(2,1)S(1)}, u32[]{:S(2)}, u32[]{:S(2)}) %collective-permute-start.1) | collective-permute-done | bytes 589856 | tf_op jit(solution)/shard_map/ppermute | solution.py:309
  48.1 0.0 collective-permute-done.2.a3
  48.1 0.0 collective-permute-start.3
  48.1 0.5 collective-permute-start.4
  48.6 0.0 collective-permute-start.5
  48.6 0.0 copy-done.16
  48.6 0.1 add_bitcast_fusion.where_ref
  48.7 1.5 %collective-permute-done.3.b1 = bf16[384,768]{1,0:T(8,128)(2,1)} collective-permute-done((bf16[384,768]{1,0:T(8,128)(2,1)S(1)}, bf16[384,768]{1,0:T(8,128)(2,1)}, u32[]{:S(2)}, u32[]{:S(2)}) %collective-permute-start.3) | collective-permute-done | bytes 589856 | tf_op jit(solution)/shard_map/ppermute | solution.py:338
  50.3 1.7 %collective-permute-done.4.b2 = bf16[384,768]{1,0:T(8,128)(2,1)} collective-permute-done((bf16[384,768]{1,0:T(8,128)(2,1)S(1)}, bf16[384,768]{1,0:T(8,128)(2,1)}, u32[]{:S(2)}, u32[]{:S(2)}) %collective-permute-start.4) | collective-permute-done | bytes 589856 | tf_op jit(solution)/shard_map/ppermute | solution.py:338
  51.9 0.2 collective-permute-done.5.b3
  52.2 0.0 all-to-all-done.arr_ref
  52.2 0.0 copy-done.3
  52.2 0.0 copy-start.9
  52.2 0.9 %copy-done.9 = bf16[1,2,4,2,1536]{4,3,2,1,0:T(2,128)(2,1)S(1)} copy-done((bf16[1,2,4,2,1536]{4,3,2,1,0:T(2,128)(2,1)S(1)}, bf16[1,2,4,2,1536]{4,3,2,1,0:T(2,128)(2,1)}, u32[]{:S(2)}) %copy-start.9) | copy-done | bytes 49176
  53.1 0.9 %copy-done.11 = bf16[1,2,4,2,1536]{4,3,2,1,0:T(2,128)(2,1)S(1)} copy-done((bf16[1,2,4,2,1536]{4,3,2,1,0:T(2,128)(2,1)S(1)}, bf16[1,2,4,2,1536]{4,3,2,1,0:T(2,128)(2,1)}, u32[]{:S(2)}) %copy-start.11) | copy-done | bytes 49176
  54.1 3.6 %shard_map.186 = (bf16[16,1536]{1,0:T(8,128)(2,1)S(1)}, bf16[16,1536]{1,0:T(8,128)(2,1)S(1)}) custom-call(s32[1,2]{1,0:T(1,128)S(1)} %add_bitcast_fusion.where_ref, bf16[1,2,4,2,1536]{4,3,2,1,0:T(2,128)(2,1)S(1)} %copy-done.9, bf16[1,2,4,2,256]{4,3,2,1,0:T(2,128)(2,1)S(1)} %copy-done.10, bf16[2560,128]{1,0:T(8,128)(2,1)S(1)} %bitcast.8, ...), custom_call_target="tpu_custom_call" | custom-call | flops 200000000 | bytes 6000000 | tf_op jit(solution)/shard_map/pallas_call | solution.py:19
  57.7 1.5 %collective-permute-start.6 = (bf16[16,1536]{1,0:T(8,128)(2,1)S(1)}, bf16[16,1536]{1,0:T(8,128)(2,1)S(1)}, u32[]{:S(2)}, u32[]{:S(2)}) collective-permute-start(bf16[16,1536]{1,0:T(8,128)(2,1)S(1)} %get-tuple-element.30.x0), channel_id=1, source_target_pairs={{0,1},{1,2},{2,3},{3,0},{4,5},{5,6},{6,7},{7,4},{8,9},{9,10},{10,1... | collective-permute-start | bytes 147464 | tf_op jit(solution)/shard_map/ppermute | solution.py:309
  59.2 2.4 %collective-permute-start.7 = (bf16[16,1536]{1,0:T(8,128)(2,1)S(1)}, bf16[16,1536]{1,0:T(8,128)(2,1)S(1)}, u32[]{:S(2)}, u32[]{:S(2)}) collective-permute-start(bf16[16,1536]{1,0:T(8,128)(2,1)S(1)} %get-tuple-element.30.x0), channel_id=1, source_target_pairs={{0,2},{1,3},{2,0},{3,1},{4,6},{5,7},{6,4},{7,5},{8,10},{9,11},{10,... | collective-permute-start | bytes 147464 | tf_op jit(solution)/shard_map/ppermute | solution.py:309
  61.6 1.6 %collective-permute-start.8 = (bf16[16,1536]{1,0:T(8,128)(2,1)S(1)}, bf16[16,1536]{1,0:T(8,128)(2,1)S(1)}, u32[]{:S(2)}, u32[]{:S(2)}) collective-permute-start(bf16[16,1536]{1,0:T(8,128)(2,1)S(1)} %get-tuple-element.30.x0), channel_id=1, source_target_pairs={{0,3},{1,0},{2,1},{3,2},{4,7},{5,4},{6,5},{7,6},{8,11},{9,8},{10,9... | collective-permute-start | bytes 147464 | tf_op jit(solution)/shard_map/ppermute | solution.py:309
  63.1 0.0 collective-permute-done.6.x1
  63.2 1.6 %collective-permute-done.7.x2 = bf16[16,1536]{1,0:T(8,128)(2,1)S(1)} collective-permute-done((bf16[16,1536]{1,0:T(8,128)(2,1)S(1)}, bf16[16,1536]{1,0:T(8,128)(2,1)S(1)}, u32[]{:S(2)}, u32[]{:S(2)}) %collective-permute-start.7) | collective-permute-done | bytes 49184 | tf_op jit(solution)/shard_map/ppermute | solution.py:309
  64.8 0.9 %collective-permute-done.8.x3 = bf16[16,1536]{1,0:T(8,128)(2,1)S(1)} collective-permute-done((bf16[16,1536]{1,0:T(8,128)(2,1)S(1)}, bf16[16,1536]{1,0:T(8,128)(2,1)S(1)}, u32[]{:S(2)}, u32[]{:S(2)}) %collective-permute-start.8) | collective-permute-done | bytes 49184 | tf_op jit(solution)/shard_map/ppermute | solution.py:309
  65.7 0.0 copy-done
  65.7 2.0 %copy-done.1 = bf16[1536,1152]{1,0:T(8,128)(2,1)S(1)} copy-done((bf16[1536,1152]{1,0:T(8,128)(2,1)S(1)}, bf16[1536,1152]{1,0:T(8,128)(2,1)}, u32[]{:S(2)}) %copy-start.1) | copy-done | bytes 3538968
  67.7 2.0 %copy-done.2 = bf16[1152,1536]{1,0:T(8,128)(2,1)S(1)} copy-done((bf16[1152,1536]{1,0:T(8,128)(2,1)S(1)}, bf16[1152,1536]{1,0:T(8,128)(2,1)}, u32[]{:S(2)}) %copy-start.2) | copy-done | bytes 3538968
  69.7 5.0 %shard_map.187 = (f32[16,1536]{1,0:T(8,128)S(1)}, bf16[16,1536]{1,0:T(8,128)(2,1)S(1)}, bf16[16,1536]{1,0:T(8,128)(2,1)S(1)}, bf16[16,1536]{1,0:T(8,128)(2,1)S(1)}) custom-call(bf16[16,1536]{1,0:T(8,128)(2,1)S(1)} %get-tuple-element.30.x0, bf16[16,1536]{1,0:T(8,128)(2,1)S(1)} %collective-permute-done.6.x1, bf16[16,1536]{1,0:T(8,128)(2,1)S(1)} %collective-permute-done.7.x2, ...), custom_call_target="tpu_custom_call" | custom-call | flops 700000000 | bytes 11000000 | tf_op jit(solution)/shard_map/pallas_call | solution.py:19
  74.7 2.9 %collective-permute-start.9 = (bf16[16,1536]{1,0:T(8,128)(2,1)S(1)}, bf16[16,1536]{1,0:T(8,128)(2,1)S(1)}, u32[]{:S(2)}, u32[]{:S(2)}) collective-permute-start(bf16[16,1536]{1,0:T(8,128)(2,1)S(1)} %get-tuple-element.32), channel_id=1, source_target_pairs={{0,3},{1,0},{2,1},{3,2},{4,7},{5,4},{6,5},{7,6},{8,11},{9,8},{10,9... | collective-permute-start | bytes 147464 | tf_op jit(solution)/shard_map/ppermute | solution.py:309
  77.5 0.1 collective-permute-start.10
  77.6 0.9 %collective-permute-start.11 = (bf16[16,1536]{1,0:T(8,128)(2,1)S(1)}, bf16[16,1536]{1,0:T(8,128)(2,1)S(1)}, u32[]{:S(2)}, u32[]{:S(2)}) collective-permute-start(bf16[16,1536]{1,0:T(8,128)(2,1)S(1)} %get-tuple-element.34), channel_id=1, source_target_pairs={{0,1},{1,2},{2,3},{3,0},{4,5},{5,6},{6,7},{7,4},{8,9},{9,10},{10,1... | collective-permute-start | bytes 147464 | tf_op jit(solution)/shard_map/ppermute | solution.py:309
  78.5 0.0 copy-done.17
  78.5 0.0 copy-done.18
  78.5 0.0 copy-done.7
  78.5 1.4 %shard_map.189 = bf16[1,2,4,64,256]{4,3,2,1,0:T(8,128)(2,1)} custom-call(bf16[64,40,128]{2,1,0:T(8,128)(2,1)S(1)} %all-to-all-done.arr_ref, bf16[1,4,64,256]{3,2,1,0:T(8,128)(2,1)S(1)} %copy-done.7, bf16[1,2,4,2,256]{4,3,2,1,0:T(2,128)(2,1)S(1)} %copy-done.10, s32[1,64]{1,0:T(1,128)S(1)} %copy-done.13, s32[1,2,4]{2,1,0:T(2,128)S(1)} %copy-done.12), custom_call_target="tpu_custom_call" | custom-call | flops 1000000 | bytes 1500000 | tf_op jit(solution)/shard_map/pallas_call | solution.py:19
  79.9 0.0 collective-permute-done.9.y1
  79.9 3.3 %collective-permute-done.10.y2 = bf16[16,1536]{1,0:T(8,128)(2,1)S(1)} collective-permute-done((bf16[16,1536]{1,0:T(8,128)(2,1)S(1)}, bf16[16,1536]{1,0:T(8,128)(2,1)S(1)}, u32[]{:S(2)}, u32[]{:S(2)}) %collective-permute-start.10) | collective-permute-done | bytes 49184 | tf_op jit(solution)/shard_map/ppermute | solution.py:309
  83.2 0.2 collective-permute-done.11.y3
  83.4 0.8 shard_map.188
  (11 shorter events, 0.0 us)
Async XLA Ops:
  0.6 51.5 %copy-start.3 = (bf16[384,1536]{1,0:T(8,128)(2,1)S(1)}, bf16[384,1536]{1,0:T(8,128)(2,1)}, u32[]{:S(2)}) copy-start(bf16[384,1536]{1,0:T(8,128)(2,1)} %own_hbm.1) | copy-start | bytes 3538948
  0.6 22.7 %copy-start.10 = (bf16[1,2,4,2,256]{4,3,2,1,0:T(2,128)(2,1)S(1)}, bf16[1,2,4,2,256]{4,3,2,1,0:T(2,128)(2,1)}, u32[]{:S(2)}) copy-start(bf16[1,2,4,2,256]{4,3,2,1,0:T(2,128)(2,1)} %new_ref.5) | copy-start | bytes 24580
  0.7 22.7 %copy-start.13 = (s32[1,64]{1,0:T(1,128)S(1)}, s32[1,64]{1,0:T(1,128)}, u32[]{:S(2)}) copy-start(s32[1,64]{1,0:T(1,128)} %holder_ref.3) | copy-start | bytes 772
  0.7 22.7 %copy-start.15 = (s32[1,2]{1,0:T(1,128)S(1)}, s32[1,2]{1,0:T(1,128)}, u32[]{:S(2)}) copy-start(s32[1,2]{1,0:T(1,128)} %plen_ref.1) | copy-start | bytes 28
  0.7 22.7 %copy-start.12 = (s32[1,2,4]{2,1,0:T(2,128)S(1)}, s32[1,2,4]{2,1,0:T(2,128)}, u32[]{:S(2)}) copy-start(s32[1,2,4]{2,1,0:T(2,128)} %tlen_ref.3) | copy-start | bytes 100
  0.7 48.0 %copy-start.16 = (f32[1536]{0:T(1024)S(1)}, f32[1536]{0:T(1024)}, u32[]{:S(2)}) copy-start(f32[1536]{0:T(1024)} %param.28) | copy-start | bytes 18436
  2.7 1.1 %copy-start.4 = (bf16[64,20,256]{2,0,1:T(8,128)(2,1)S(1)}, bf16[64,20,256]{2,0,1:T(8,128)(2,1)}, u32[]{:S(2)}) copy-start(bf16[64,20,256]{2,0,1:T(8,128)(2,1)} %param.22) | copy-start | bytes 1966084
  3.8 0.7 copy-start.14
  5.8 46.3 %all-to-all-start = ((bf16[64,40,128]{2,1,0:T(8,128)(2,1)}), bf16[64,40,128]{2,1,0:T(8,128)(2,1)S(1)}, u32[]{:S(2)}, u32[]{:S(2)}) async-start(bf16[64,40,128]{2,1,0:T(8,128)(2,1)} %bitcast.4), calls=%async_computation | async-start | bytes 1310720 | tf_op jit(solution)/shard_map/all_to_all | solution.py:325
  17.6 16.9 %collective-permute-start = (bf16[384,768]{1,0:T(8,128)(2,1)}, bf16[384,768]{1,0:T(8,128)(2,1)S(1)}, u32[]{:S(2)}, u32[]{:S(2)}) collective-permute-start(bf16[384,768]{1,0:T(8,128)(2,1)} %constant_dynamic-slice_fusion), channel_id=1, source_target_pairs={{0,1},{1,2},{2,3},{3,0},{4,5},{5,6},{6,7},{7,4},{8,9},{9,10},{10,1... | collective-permute-start | bytes 1769480 | tf_op jit(solution)/shard_map/ppermute | solution.py:309
  19.2 28.9 %collective-permute-start.1 = (bf16[384,768]{1,0:T(8,128)(2,1)}, bf16[384,768]{1,0:T(8,128)(2,1)S(1)}, u32[]{:S(2)}, u32[]{:S(2)}) collective-permute-start(bf16[384,768]{1,0:T(8,128)(2,1)} %constant_dynamic-slice_fusion), channel_id=1, source_target_pairs={{0,2},{1,3},{2,0},{3,1},{4,6},{5,7},{6,4},{7,5},{8,10},{9,11},{10,... | collective-permute-start | bytes 1769480 | tf_op jit(solution)/shard_map/ppermute | solution.py:309
  21.9 26.2 %collective-permute-start.2 = (bf16[384,768]{1,0:T(8,128)(2,1)}, bf16[384,768]{1,0:T(8,128)(2,1)}, u32[]{:S(2)}, u32[]{:S(2)}) collective-permute-start(bf16[384,768]{1,0:T(8,128)(2,1)} %constant_dynamic-slice_fusion), channel_id=1, source_target_pairs={{0,3},{1,0},{2,1},{3,2},{4,7},{5,4},{6,5},{7,6},{8,11},{9,8},{10,9... | collective-permute-start | bytes 1769480 | tf_op jit(solution)/shard_map/ppermute | solution.py:309
  23.4 1.0 %copy-start.5 = (bf16[1,1024,256]{2,1,0:T(8,128)(2,1)S(1)}, bf16[1,1024,256]{2,1,0:T(8,128)(2,1)}, u32[]{:S(2)}) copy-start(bf16[1,1024,256]{2,1,0:T(8,128)(2,1)} %kv_ref.1) | copy-start | bytes 1572868
  24.4 0.9 %copy-start.6 = (bf16[1,4,64,256]{3,2,1,0:T(8,128)(2,1)S(1)}, bf16[1,4,64,256]{3,2,1,0:T(8,128)(2,1)}, u32[]{:S(2)}) copy-start(bf16[1,4,64,256]{3,2,1,0:T(8,128)(2,1)} %tails_ref.3) | copy-start | bytes 393220
  25.3 0.8 copy-start.8
  48.1 2.1 %collective-permute-start.3 = (bf16[384,768]{1,0:T(8,128)(2,1)S(1)}, bf16[384,768]{1,0:T(8,128)(2,1)}, u32[]{:S(2)}, u32[]{:S(2)}) collective-permute-start(bf16[384,768]{1,0:T(8,128)(2,1)S(1)} %collective-permute-done.a1), channel_id=1, source_target_pairs={{0,4},{4,0},{8,12},{12,8},{16,20},{20,16},{24,28},{28,24},{32,36},... | collective-permute-start | bytes 1769480 | tf_op jit(solution)/shard_map/ppermute | solution.py:338
  48.1 3.8 %collective-permute-start.4 = (bf16[384,768]{1,0:T(8,128)(2,1)S(1)}, bf16[384,768]{1,0:T(8,128)(2,1)}, u32[]{:S(2)}, u32[]{:S(2)}) collective-permute-start(bf16[384,768]{1,0:T(8,128)(2,1)S(1)} %collective-permute-done.1.a2), channel_id=1, source_target_pairs={{0,4},{4,0},{8,12},{12,8},{16,20},{20,16},{24,28},{28,24},{32,36},... | collective-permute-start | bytes 1769480 | tf_op jit(solution)/shard_map/ppermute | solution.py:338
  48.6 3.5 %collective-permute-start.5 = (bf16[384,768]{1,0:T(8,128)(2,1)}, bf16[384,768]{1,0:T(8,128)(2,1)}, u32[]{:S(2)}, u32[]{:S(2)}) collective-permute-start(bf16[384,768]{1,0:T(8,128)(2,1)} %collective-permute-done.2.a3), channel_id=1, source_target_pairs={{0,4},{4,0},{8,12},{12,8},{16,20},{20,16},{24,28},{28,24},{32,36},... | collective-permute-start | bytes 1769480 | tf_op jit(solution)/shard_map/ppermute | solution.py:338
  52.2 13.5 %copy-start = (bf16[1536,1152]{1,0:T(8,128)(2,1)S(1)}, bf16[1536,1152]{1,0:T(8,128)(2,1)}, u32[]{:S(2)}) copy-start(bf16[1536,1152]{1,0:T(8,128)(2,1)} %wg_hbm.1) | copy-start | bytes 10616836
  52.2 1.0 %copy-start.9 = (bf16[1,2,4,2,1536]{4,3,2,1,0:T(2,128)(2,1)S(1)}, bf16[1,2,4,2,1536]{4,3,2,1,0:T(2,128)(2,1)}, u32[]{:S(2)}) copy-start(bf16[1,2,4,2,1536]{4,3,2,1,0:T(2,128)(2,1)} %q_ref.2) | copy-start | bytes 147460
  53.1 0.9 %copy-start.11 = (bf16[1,2,4,2,1536]{4,3,2,1,0:T(2,128)(2,1)S(1)}, bf16[1,2,4,2,1536]{4,3,2,1,0:T(2,128)(2,1)}, u32[]{:S(2)}) copy-start(bf16[1,2,4,2,1536]{4,3,2,1,0:T(2,128)(2,1)} %res_ref.1) | copy-start | bytes 147460
  54.0 24.4 %copy-start.17 = (f32[1536]{0:T(1024)S(1)}, f32[1536]{0:T(1024)}, u32[]{:S(2)}) copy-start(f32[1536]{0:T(1024)} %param.32) | copy-start | bytes 18436
  54.0 24.4 %copy-start.18 = (f32[1536]{0:T(1024)S(1)}, f32[1536]{0:T(1024)}, u32[]{:S(2)}) copy-start(f32[1536]{0:T(1024)} %param.33) | copy-start | bytes 18436
  54.1 24.5 %copy-start.7 = (bf16[1,4,64,256]{3,2,1,0:T(8,128)(2,1)S(1)}, bf16[1,4,64,256]{3,2,1,0:T(8,128)(2,1)}, u32[]{:S(2)}) copy-start(bf16[1,4,64,256]{3,2,1,0:T(8,128)(2,1)} %tails_ref.3) | copy-start | bytes 393220
  57.7 5.5 %collective-permute-start.6 = (bf16[16,1536]{1,0:T(8,128)(2,1)S(1)}, bf16[16,1536]{1,0:T(8,128)(2,1)S(1)}, u32[]{:S(2)}, u32[]{:S(2)}) collective-permute-start(bf16[16,1536]{1,0:T(8,128)(2,1)S(1)} %get-tuple-element.30.x0), channel_id=1, source_target_pairs={{0,1},{1,2},{2,3},{3,0},{4,5},{5,6},{6,7},{7,4},{8,9},{9,10},{10,1... | collective-permute-start | bytes 147464 | tf_op jit(solution)/shard_map/ppermute | solution.py:309
  59.2 5.6 %collective-permute-start.7 = (bf16[16,1536]{1,0:T(8,128)(2,1)S(1)}, bf16[16,1536]{1,0:T(8,128)(2,1)S(1)}, u32[]{:S(2)}, u32[]{:S(2)}) collective-permute-start(bf16[16,1536]{1,0:T(8,128)(2,1)S(1)} %get-tuple-element.30.x0), channel_id=1, source_target_pairs={{0,2},{1,3},{2,0},{3,1},{4,6},{5,7},{6,4},{7,5},{8,10},{9,11},{10,... | collective-permute-start | bytes 147464 | tf_op jit(solution)/shard_map/ppermute | solution.py:309
  61.6 4.1 %collective-permute-start.8 = (bf16[16,1536]{1,0:T(8,128)(2,1)S(1)}, bf16[16,1536]{1,0:T(8,128)(2,1)S(1)}, u32[]{:S(2)}, u32[]{:S(2)}) collective-permute-start(bf16[16,1536]{1,0:T(8,128)(2,1)S(1)} %get-tuple-element.30.x0), channel_id=1, source_target_pairs={{0,3},{1,0},{2,1},{3,2},{4,7},{5,4},{6,5},{7,6},{8,11},{9,8},{10,9... | collective-permute-start | bytes 147464 | tf_op jit(solution)/shard_map/ppermute | solution.py:309
  65.7 2.0 %copy-start.1 = (bf16[1536,1152]{1,0:T(8,128)(2,1)S(1)}, bf16[1536,1152]{1,0:T(8,128)(2,1)}, u32[]{:S(2)}) copy-start(bf16[1536,1152]{1,0:T(8,128)(2,1)} %wu_hbm.1) | copy-start | bytes 10616836
  67.7 2.0 %copy-start.2 = (bf16[1152,1536]{1,0:T(8,128)(2,1)S(1)}, bf16[1152,1536]{1,0:T(8,128)(2,1)}, u32[]{:S(2)}) copy-start(bf16[1152,1536]{1,0:T(8,128)(2,1)} %wd_hbm.1) | copy-start | bytes 10616836
  74.7 5.2 %collective-permute-start.9 = (bf16[16,1536]{1,0:T(8,128)(2,1)S(1)}, bf16[16,1536]{1,0:T(8,128)(2,1)S(1)}, u32[]{:S(2)}, u32[]{:S(2)}) collective-permute-start(bf16[16,1536]{1,0:T(8,128)(2,1)S(1)} %get-tuple-element.32), channel_id=1, source_target_pairs={{0,3},{1,0},{2,1},{3,2},{4,7},{5,4},{6,5},{7,6},{8,11},{9,8},{10,9... | collective-permute-start | bytes 147464 | tf_op jit(solution)/shard_map/ppermute | solution.py:309
  77.5 5.7 %collective-permute-start.10 = (bf16[16,1536]{1,0:T(8,128)(2,1)S(1)}, bf16[16,1536]{1,0:T(8,128)(2,1)S(1)}, u32[]{:S(2)}, u32[]{:S(2)}) collective-permute-start(bf16[16,1536]{1,0:T(8,128)(2,1)S(1)} %get-tuple-element.33), channel_id=1, source_target_pairs={{0,2},{1,3},{2,0},{3,1},{4,6},{5,7},{6,4},{7,5},{8,10},{9,11},{10,... | collective-permute-start | bytes 147464 | tf_op jit(solution)/shard_map/ppermute | solution.py:309
  77.6 5.8 %collective-permute-start.11 = (bf16[16,1536]{1,0:T(8,128)(2,1)S(1)}, bf16[16,1536]{1,0:T(8,128)(2,1)S(1)}, u32[]{:S(2)}, u32[]{:S(2)}) collective-permute-start(bf16[16,1536]{1,0:T(8,128)(2,1)S(1)} %get-tuple-element.34), channel_id=1, source_target_pairs={{0,1},{1,2},{2,3},{3,0},{4,5},{5,6},{6,7},{7,4},{8,9},{9,10},{10,1... | collective-permute-start | bytes 147464 | tf_op jit(solution)/shard_map/ppermute | solution.py:309

commit v2 on v1

--- a/solution.py
+++ b/solution.py
@@ -43,7 +43,15 @@
     out_ref[...] = scr[...].astype(BF)
 
 
-def load_rows(ref, q, lanes=None):
+def take_half(w_hbm, out_ref, sem):
+    half = out_ref.shape[1]
+    core = lax.rem(lax.axis_index("req"), 2)
+    copy = pltpu.make_async_copy(w_hbm.at[:, pl.ds(pl.multiple_of(core * half, 128), half)], out_ref, sem)
+    copy.start()
+    copy.wait()
+
+
+def load_rows(ref, q):
     parts = [ref[0, q, s].astype(F32) for s in range(ref.shape[2])]
     return jnp.concatenate(parts, axis=0)
 
@@ -107,7 +115,7 @@
     return jnp.concatenate([acc[h * rows : (h + 1) * rows] for h in range(heads)], axis=1)
 
 
-def resident(win, tail, size, page, q_ref, new_ref, kv_ref, tails_ref, holder_ref, plen_ref, tlen_ref, out_ref, bias_ref):
+def resident(win, tail, size, page, n, q_ref, new_ref, kv_ref, tails_ref, holder_ref, plen_ref, tlen_ref, res_ref, out_ref):
     count = q_ref.shape[2]
     rows = 2 * count
     sample, token, length = row_lengths(tlen_ref, 0, count)
@@ -129,8 +137,6 @@
         rows,
         size,
     )
-    out_ref[...] = out.astype(BF)
-    n = bias_ref.shape[1]
     c = iota((1, n), 1)
     pages = holder_ref.shape[1]
     per = n // pages
@@ -141,49 +147,57 @@
         base = jnp.where(origin == holder_ref[0, p], p * page, base)
     pos = jnp.where(inside < page, base + inside, 1 << 20)
     sample, token, length = row_lengths(tlen_ref, 1, count)
-    bias_ref[...] = window_bias(pos, plen_ref[0, 1], win, tail, sample, token, length)
-
-
-def moved(size, page, where_ref, q_ref, new_ref, arr_ref, bias_ref, first_ref, res_ref, norm_ref, own_hbm, a1, a2, a3, b1, b2, b3, h1_ref, normed_ref, wown, attn, sem):
-    fetch = pltpu.make_async_copy(own_hbm, wown, sem)
-    fetch.start()
-    wa, wb = (a1, a2, a3), (b1, b2, b3)
-    count = q_ref.shape[2]
-    rows = 2 * count
+    bias = window_bias(pos, plen_ref[0, 1], win, tail, sample, token, length)
+    parts = (bias, load_rows(res_ref, 0), load_rows(res_ref, 1), out, load_rows(q_ref, 1), load_rows(new_ref, 1))
+    out_ref[...] = jnp.concatenate(parts, axis=1)
+
+
+def moved(size, page, arr_ref, norm_ref, *refs):
+    count = len(refs) // 2 - 2
+    hbm, (h1_ref, normed_ref), vmem, (attn, sems) = refs[:count], refs[count : count + 2], refs[count + 2 : -2], refs[-2:]
+    copies = [pltpu.make_async_copy(a, b, sems.at[i]) for i, (a, b) in enumerate(zip(hbm, vmem))]
+    for c in copies:
+        c.start()
+    state, wown, a1, a3, top, bot, b13, btop, bbot = vmem
+    copies[0].wait()
+    n, width = arr_ref.shape[0], attn.shape[1]
+    at = [n + i * width for i in range(5)]
+    bias = state[:, :n]
+    res = jnp.concatenate([state[:, at[0] : at[1]], state[:, at[1] : at[2]]], axis=0)
+    first, q8, fresh = state[:, at[2] : at[3]], state[:, at[3] : at[4]], state[:, at[4] :].astype(BF)
+    rows = state.shape[0]
     r = iota((rows, 1), 0)
-    qh = stack_heads(load_rows(q_ref, 1), size)
-    fresh = load_rows(new_ref, 1).astype(BF)
-    nb = new_bias(r >> 1, r & 1, count)
+    nb = new_bias(r >> 1, r & 1, rows // 2)
     arr = arr_ref[...]
     second = attend(
-        qh,
-        [(arr, arr, bias_ref[...], page), (fresh[:, :size], fresh[:, size:], nb, 0)],
+        stack_heads(q8, size),
+        [(arr, arr, bias, page), (fresh[:, :size], fresh[:, size:], nb, 0)],
         rows,
         size,
     )
-    attn[...] = jnp.concatenate([first_ref[...].astype(F32), second], axis=0).astype(BF)
-    me, core = where_ref[0, 0], where_ref[0, 1]
+    attn[...] = jnp.concatenate([first, second], axis=0).astype(BF)
+    for c in copies[1:]:
+        c.wait()
+    me = lax.axis_index("mlp")
+    low = lax.rem(lax.axis_index("req"), 2) == 0
     block = wown.shape[0]
-    n_mlp = len(wa) + 1
-
-    def piece(k):
+    n_mlp = attn.shape[1] // block
+    part = top.shape[0]
+
+    def piece(k, first=0, count=block):
         rb = lax.rem(me - k + n_mlp, n_mlp)
-        return attn[:, pl.ds(pl.multiple_of(rb * block, 128), block)]
-
-    same = other = None
-    for k in range(1, n_mlp):
-        x = piece(k)
-        s = jnp.dot(x, wa[k - 1][...], preferred_element_type=F32)
-        o = jnp.dot(x, wb[k - 1][...], preferred_element_type=F32)
-        same = s if same is None else same + s
-        other = o if other is None else other + o
-    fetch.wait()
-    own = jnp.dot(piece(0), wown[...], preferred_element_type=F32)
-    low = core == 0
+        return attn[:, pl.ds(pl.multiple_of(rb * block, 128), block)][:, first : first + count]
+
+    def product(x, w):
+        return jnp.dot(x, w[...], preferred_element_type=F32)
+
+    p1, p3, pt, pb = piece(1), piece(n_mlp - 1), piece(2, 0, part), piece(2, part, block - part)
+    same = product(p1, a1) + product(p3, a3) + product(pt, top) + product(pb, bot)
+    other = product(p1, b13.at[0]) + product(p3, b13.at[1]) + product(pt, btop) + product(pb, bbot)
+    own = product(piece(0), wown)
     left = jnp.where(low, same, other)
     right = jnp.where(low, other, same)
     mixed = own + jnp.concatenate([left, right], axis=1)
-    res = jnp.concatenate([load_rows(res_ref, 0), load_rows(res_ref, 1)], axis=0)
     h1 = (res + mixed).astype(BF)
     h1_ref[...] = h1
     f = h1.astype(F32)
@@ -216,41 +230,22 @@
             out_ref[0, q, s] = t.astype(BF)
 
 
-def mlp(x0, x1, x2, x3, wg_hbm, wu_hbm, wd_hbm, y0, y1, y2, y3, wg, wu, wd, sems):
-    cuts = 3
-    kin, kout = wg.shape[0] // cuts, wd.shape[0] // cuts
-    ups, downs = [], []
-    for c in range(cuts):
-        at = pl.ds(c * kin, kin)
-        ups.append(
-            (
-                pltpu.make_async_copy(wg_hbm.at[at], wg.at[at], sems.at[3 * c]),
-                pltpu.make_async_copy(wu_hbm.at[at], wu.at[at], sems.at[3 * c + 1]),
-            )
-        )
-        at = pl.ds(c * kout, kout)
-        downs.append(pltpu.make_async_copy(wd_hbm.at[at], wd.at[at], sems.at[3 * c + 2]))
-    for g, u in ups:
-        g.start()
-        u.start()
-    for d in downs:
-        d.start()
+def load(*refs):
+    count = len(refs) // 2
+    sems = refs[-1]
+    copies = [pltpu.make_async_copy(refs[i], refs[count + i], sems.at[i]) for i in range(count)]
+    for c in copies:
+        c.start()
+    for c in copies:
+        c.wait()
+
+
+def mlp(x0, x1, x2, x3, wg, wu, wd, y0, y1, y2, y3):
     x = jnp.concatenate([x0[...], x1[...], x2[...], x3[...]], axis=0)
-    gate = up = None
-    for c, (g, u) in enumerate(ups):
-        part = x[:, c * kin : (c + 1) * kin]
-        g.wait()
-        t = jnp.dot(part, wg[c * kin : (c + 1) * kin], preferred_element_type=F32)
-        gate = t if gate is None else gate + t
-        u.wait()
-        t = jnp.dot(part, wu[c * kin : (c + 1) * kin], preferred_element_type=F32)
-        up = t if up is None else up + t
+    gate = jnp.dot(x, wg[...], preferred_element_type=F32)
+    up = jnp.dot(x, wu[...], preferred_element_type=F32)
     act = (jax.nn.gelu(gate, approximate=True) * up).astype(BF)
-    y = None
-    for c, d in enumerate(downs):
-        d.wait()
-        t = jnp.dot(act[:, c * kout : (c + 1) * kout], wd[c * kout : (c + 1) * kout], preferred_element_type=F32)
-        y = t if y is None else y + t
+    y = jnp.dot(act, wd[...], preferred_element_type=F32)
     n = x0.shape[0]
     y0[...] = y[:n]
     y1[...] = y[n : 2 * n].astype(BF)
@@ -300,19 +295,27 @@
     win, tail = prompt_kv.shape[1], tail_kv.shape[2]
     slots, page = page_pool.shape[:2]
     rows = 4 * samp
-    me = lax.axis_index("mlp")
-    core = lax.rem(lax.axis_index("req"), 2)
-    place = jnp.stack([me, core]).astype(jnp.int32)[None]
     arrived_rows = n_req * 2 * page
+    block, hid = w_out.shape[0], w_gate.shape[1]
+    half, part = width // 2, block // 2
 
     def shift(x, k):
         return lax.ppermute(x, "mlp", [(i, (i + k) % n_mlp) for i in range(n_mlp)])
 
-    half = width // 2
-    mine = lax.dynamic_slice_in_dim(w_out, core * half, half, 1)
-    slot, mine = lax.optimization_barrier((serve_slot, mine))
-    same = [shift(mine, k) for k in range(1, n_mlp)]
-
+    def swap(x):
+        return lax.ppermute(x, "req", [(i, i ^ 1) for i in range(n_req)])
+
+    mine = call(
+        take_half,
+        jax.ShapeDtypeStruct((block, half), BF),
+        (w_out,),
+        [HBM],
+        [pltpu.SemaphoreType.DMA],
+        nbytes=1_200_000,
+        limit=60,
+    )
+    a1, a3 = shift(mine, 1), shift(mine, -1)
+    slot, _ = lax.optimization_barrier((serve_slot, mine))
     outgoing = call(
         pick_pages,
         jax.ShapeDtypeStruct((arrived_rows, size), BF),
@@ -321,21 +324,25 @@
         [pltpu.VMEM((arrived_rows, size), F32)],
         flops=100_000_000,
         nbytes=1_400_000,
+        limit=60,
     )
     arrived = lax.all_to_all(
         outgoing.reshape(n_req, 2 * page, size), "req", split_axis=0, concat_axis=0, tiled=True
     )
     q_late, outgoing = lax.optimization_barrier((queries, outgoing))
-    first, bias = call(
-        functools.partial(resident, win, tail, size, page),
-        (jax.ShapeDtypeStruct((2 * samp, width), BF), jax.ShapeDtypeStruct((2 * samp, arrived_rows), F32)),
-        (q_late, new_kv, prompt_kv, tail_kv, page_holder, prompt_len, tail_len),
-        [VMEM, VMEM, VMEM, VMEM, SMEM, SMEM, SMEM],
+    span = arrived_rows + 4 * width + 2 * size
+    state = call(
+        functools.partial(resident, win, tail, size, page, arrived_rows),
+        jax.ShapeDtypeStruct((2 * samp, span), F32),
+        (q_late, new_kv, prompt_kv, tail_kv, page_holder, prompt_len, tail_len, residual),
+        [VMEM, VMEM, VMEM, VMEM, SMEM, SMEM, SMEM, VMEM],
         flops=100_000_000,
         nbytes=1_000_000,
-    )
-    *same, first = lax.optimization_barrier((*same, first))
-    other = [lax.ppermute(a, "req", [(i, i ^ 1) for i in range(n_req)]) for a in same]
+        limit=60,
+    )
+    a1, a3, state = lax.optimization_barrier((a1, a3, state))
+    top, bot = shift(a1[:part], 1), shift(a3[part:], -1)
+    b13, btop, bbot = swap(jnp.stack([a1, a3])), swap(top), swap(bot)
     tails_out = call(
         functools.partial(write_tails, win, page),
         jax.ShapeDtypeStruct((1, 2) + tail_kv.shape[1:], BF),
@@ -345,50 +352,38 @@
         flops=1_000_000,
         nbytes=1_500_000,
     )
-    block = w_out.shape[0]
+    pieces = (state, w_out, a1, a3, top, bot, b13, btop, bbot)
+    row_bf = jax.ShapeDtypeStruct((rows, width), BF)
     h1, normed = call(
         functools.partial(moved, size, page),
-        (jax.ShapeDtypeStruct((rows, width), BF), jax.ShapeDtypeStruct((rows, width), BF)),
-        (
-            place,
-            queries,
-            new_kv,
-            arrived.reshape(arrived_rows, size),
-            bias,
-            first,
-            residual,
-            norm_mlp[None],
-            w_out,
-            *same,
-            *other,
-        ),
-        [SMEM] + [VMEM] * 7 + [HBM] + [VMEM] * 6,
-        [
-            pltpu.VMEM((block, width), BF),
-            pltpu.VMEM((rows, width), BF),
-            pltpu.SemaphoreType.DMA,
-        ],
-        limit=14,
+        (row_bf, row_bf),
+        (arrived.reshape(arrived_rows, size), norm_mlp[None], *pieces),
+        [VMEM, VMEM] + [HBM] * len(pieces),
+        [pltpu.VMEM(x.shape, x.dtype) for x in pieces]
+        + [pltpu.VMEM((rows, width), BF), pltpu.SemaphoreType.DMA((len(pieces),))],
         flops=200_000_000,
         nbytes=6_000_000,
+        limit=50,
     )
     others = [shift(normed, k) for k in range(1, n_mlp)]
-    row_bf = jax.ShapeDtypeStruct((rows, width), BF)
-    hid = w_gate.shape[1]
+    w_up, w_down, _ = lax.optimization_barrier((w_up, w_down, normed))
+    w_up, w_down = call(
+        load,
+        (pltpu.VMEM(w_up.shape, BF), pltpu.VMEM(w_down.shape, BF)),
+        (w_up, w_down),
+        [HBM, HBM],
+        [pltpu.SemaphoreType.DMA((2,))],
+        nbytes=14_000_000,
+        limit=50,
+    )
     ys = call(
         mlp,
         (jax.ShapeDtypeStruct((rows, width), F32), row_bf, row_bf, row_bf),
         (normed, *others, w_gate, w_up, w_down),
-        [VMEM] * 4 + [HBM] * 3,
-        [
-            pltpu.VMEM((width, hid), BF),
-            pltpu.VMEM((width, hid), BF),
-            pltpu.VMEM((hid, width), BF),
-            pltpu.SemaphoreType.DMA((9,)),
-        ],
+        [VMEM] * 7,
         flops=700_000_000,
-        nbytes=11_000_000,
-        limit=16,
+        nbytes=1_000_000,
+        limit=14,
     )
     back = [shift(ys[k], -k) for k in range(1, n_mlp)]
     scores, hidden = call(

time: 85.1 us -> 63.6 us (0.75)
  local copies, waits for them, and re-layouts: 12.4 us -> 0.1 us
  waiting for transfers between devices: 30 us -> 17.8 us
  Pallas kernels: 13.6 us -> 17.2 us
  other arithmetic: 0.08 us -> 1.12 us
  starting transfers between devices: 27.3 us -> 26.3 us
    ppermute x9 -> x10, waiting for transfers between devices: 26.6 us -> 15.6 us  [shift(): return lax.ppermute(x, 'mlp', [(i, (i + k) % n_mlp) for i in range(n_mlp)])]
    unnamed x38 -> x18, local copies, waits for them, and re-layouts: 10.4 us -> 0.04 us
    pallas_call x6 -> x8, Pallas kernels: 13.6 us -> 17.2 us  [call(): pl.pallas_call(body, out_shape=outs, in_specs=specs, out_specs=jax.tree.m...]
    dynamic_slice x1 -> x0, local copies, waits for them, and re-layouts: 2.03 us -> none  [on_device(): mine = lax.dynamic_slice_in_dim(w_out, core * half, half, 1)]
    ppermute x3, waiting for transfers between devices: 3.43 us -> 1.56 us  [swap(): return lax.ppermute(x, 'req', [(i, i ^ 1) for i in range(n_req)])]
    another operation x0 -> x1, other arithmetic: none -> 1.12 us  [on_device(): b13, btop, bbot = (swap(jnp.stack([a1, a3])), swap(top), swap(bot))]
    ppermute x9 -> x10, starting transfers between devices: 15 us -> 14.4 us  [shift(): return lax.ppermute(x, 'mlp', [(i, (i + k) % n_mlp) for i in range(n_mlp)])]
  transfers between devices with their start and end apart: 13 -> 14, of which waited for: 9 -> 8; matrix products, arithmetic and copies ran while one was open for 0% -> 2% of each run, Pallas kernels for 3% -> 16%
where the time goes in v2:
time: 63.6 us; the launch traced here: 63.3 us
  starting transfers between devices  26.3 us (41%)
  waiting for transfers between devices  17.8 us (28%)
  Pallas kernels  17.2 us (27%)
  other arithmetic  1.12 us (2%)
  between operations  0.81 us (1%)
    pallas_call x8, Pallas kernels, call(): pl.pallas_call(body, out_shape=outs, in_specs=specs, out_specs=jax.tree.m...  17.2 us
    ppermute x10, waiting for transfers between devices, shift(): return lax.ppermute(x, 'mlp', [(i, (i + k) % n_mlp) for i in range(n_mlp)])  15.6 us
    ppermute x10, starting transfers between devices, shift(): return lax.ppermute(x, 'mlp', [(i, (i + k) % n_mlp) for i in range(n_mlp)])  14.4 us
    all_to_all x1, starting transfers between devices, on_device(): lax.all_to_all(outgoing.reshape(n_req, 2 * page, size), 'req', split_axis...  11.8 us
    ppermute x3, waiting for transfers between devices, swap(): return lax.ppermute(x, 'req', [(i, i ^ 1) for i in range(n_req)])  1.56 us
  transfers between devices with their start and end apart: 14, of which 8 were waited for; matrix products, arithmetic and copies ran while one was open for 2% of the time, Pallas kernels for 16%

profile of v2, /device:TPU:32, one launch (start us, length us, event | category | flops | bytes accessed | tf_op | source)
XLA Modules:
  0.0 63.3 jit_solution(1278967861424053257)
XLA Ops:
  0.6 1.9 %shard_map.184 = bf16[384,768]{1,0:T(8,128)(2,1)} custom-call(bf16[384,1536]{1,0:T(8,128)(2,1)} %refs_1_.1), custom_call_target="tpu_custom_call" | custom-call | bytes 1200000 | tf_op jit(solution)/shard_map/pallas_call | solution.py:19
  2.6 2.8 %collective-permute-start.1 = (bf16[384,768]{1,0:T(8,128)(2,1)}, bf16[384,768]{1,0:T(8,128)(2,1)S(1)}, u32[]{:S(2)}, u32[]{:S(2)}) collective-permute-start(bf16[384,768]{1,0:T(8,128)(2,1)} %shard_map.184), channel_id=1, source_target_pairs={{0,3},{1,0},{2,1},{3,2},{4,7},{5,4},{6,5},{7,6},{8,11},{9,8},{10,9... | collective-permute-start | bytes 1769480 | tf_op jit(solution)/shard_map/ppermute | solution.py:303
  5.4 0.0 collective-permute-start
  5.4 2.4 %shard_map.185 = bf16[2560,128]{1,0:T(8,128)(2,1)} custom-call(bf16[20,64,256]{2,1,0:T(8,128)(2,1)} %bitcast.10, s32[1,64]{1,0:T(1,128)} %slot_ref), custom_call_target="tpu_custom_call" | custom-call | flops 100000000 | bytes 1400000 | tf_op jit(solution)/shard_map/pallas_call | solution.py:19
  7.8 11.8 %all-to-all-start = ((bf16[64,40,128]{2,1,0:T(8,128)(2,1)}), bf16[64,40,128]{2,1,0:T(8,128)(2,1)S(1)}, u32[]{:S(2)}, u32[]{:S(2)}) async-start(bf16[64,40,128]{2,1,0:T(8,128)(2,1)} %bitcast.9), calls=%async_computation | async-start | bytes 1310720 | tf_op jit(solution)/shard_map/all_to_all | solution.py:329
  19.6 2.8 %shard_map.186.refs_0_ = f32[8,8960]{1,0:T(8,128)} custom-call(bf16[1,2,4,2,1536]{4,3,2,1,0:T(2,128)(2,1)} %q_ref, bf16[1,2,4,2,256]{4,3,2,1,0:T(2,128)(2,1)} %new_ref.3, bf16[1,1024,256]{2,1,0:T(8,128)(2,1)} %kv_ref.1, bf16[1,4,64,256]{3,2,1,0:T(8,128)(2,1)} %tails_ref.3, s32[1,64]{1,0:T(1,128)} %holder_ref.3, s32[1,2]{1,0:T(1,128)} %plen_ref.1, ...), custom_call_target="tpu_custom_call" | custom-call | flops 100000000 | bytes 1000000 | tf_op jit(solution)/shard_map/pallas_call | solution.py:19
  22.4 0.0 collective-permute-done.1.refs_3_
  22.4 0.0 collective-permute-done.refs_2_
  22.4 1.1 %pad_maximum_fusion = bf16[2,384,768]{2,1,0:T(8,128)(2,1)} fusion(bf16[1,384,768]{2,1,0:T(8,128)(2,1)S(1)} %bitcast.7, bf16[1,384,768]{2,1,0:T(8,128)(2,1)S(1)} %bitcast.8), kind=kLoop, calls=%fused_computation | loop fusion | flops 589824 | bytes 2359296 | tf_op jit(solution)/shard_map/stack | solution.py:345
  23.6 0.0 copy-start.6
  23.6 0.0 copy-start.1
  23.6 0.2 collective-permute-start.4
  23.7 3.3 %collective-permute-start.3 = (bf16[192,768]{1,0:T(8,128)(2,1)S(1)}, bf16[192,768]{1,0:T(8,128)(2,1)S(1)}, u32[]{:S(2)}, u32[]{:S(2)}) collective-permute-start(bf16[192,768]{1,0:T(8,128)(2,1)S(1)} %slice.7), channel_id=1, source_target_pairs={{0,3},{1,0},{2,1},{3,2},{4,7},{5,4},{6,5},{7,6},{8,11},{9,8},{10,9... | collective-permute-start | bytes 884744 | tf_op jit(solution)/shard_map/ppermute | solution.py:303
  27.1 0.1 collective-permute-start.2
  27.2 6.7 %collective-permute-done.3.refs_5_ = bf16[192,768]{1,0:T(8,128)(2,1)S(1)} collective-permute-done((bf16[192,768]{1,0:T(8,128)(2,1)S(1)}, bf16[192,768]{1,0:T(8,128)(2,1)S(1)}, u32[]{:S(2)}, u32[]{:S(2)}) %collective-permute-start.3) | collective-permute-done | bytes 294944 | tf_op jit(solution)/shard_map/ppermute | solution.py:303
  33.8 0.0 collective-permute-start.6
  33.8 3.5 %collective-permute-done.2.refs_4_ = bf16[192,768]{1,0:T(8,128)(2,1)S(1)} collective-permute-done((bf16[192,768]{1,0:T(8,128)(2,1)S(1)}, bf16[192,768]{1,0:T(8,128)(2,1)S(1)}, u32[]{:S(2)}, u32[]{:S(2)}) %collective-permute-start.2) | collective-permute-done | bytes 294944 | tf_op jit(solution)/shard_map/ppermute | solution.py:303
  37.4 0.0 collective-permute-start.5
  37.4 0.0 copy-done.6
  37.4 0.0 collective-permute-done.6.refs_8_
  37.4 1.6 %collective-permute-done.5.refs_7_ = bf16[192,768]{1,0:T(8,128)(2,1)S(1)} collective-permute-done((bf16[192,768]{1,0:T(8,128)(2,1)S(1)}, bf16[192,768]{1,0:T(8,128)(2,1)S(1)}, u32[]{:S(2)}, u32[]{:S(2)}) %collective-permute-start.5) | collective-permute-done | bytes 294944 | tf_op jit(solution)/shard_map/ppermute | solution.py:306
  38.9 0.6 all-to-all-done.arr_ref
  39.5 0.0 collective-permute-done.4.refs_6_
  39.5 0.0 copy-done.1
  39.5 2.7 %shard_map.187 = (bf16[16,1536]{1,0:T(8,128)(2,1)S(1)}, bf16[16,1536]{1,0:T(8,128)(2,1)S(1)}) custom-call(bf16[2560,128]{1,0:T(8,128)(2,1)S(1)} %bitcast.6, f32[1,1536]{1,0:T(1,128)S(1)} %broadcast_in_dim.9.norm_ref, f32[8,8960]{1,0:T(8,128)S(1)} %copy-done.1, bf16[384,1536]{1,0:T(8,128)(2,1)} %refs_1_.1, bf16[384,768]{1,0:T(8,128)(2,1)S(1)} %collective-permute-done.refs_2_, ...), custom_call_target="tpu_custom_call" | custom-call | flops 200000000 | bytes 6000000 | tf_op jit(solution)/shard_map/pallas_call | solution.py:19
  42.2 3.3 %collective-permute-start.9 = (bf16[16,1536]{1,0:T(8,128)(2,1)S(1)}, bf16[16,1536]{1,0:T(8,128)(2,1)S(1)}, u32[]{:S(2)}, u32[]{:S(2)}) collective-permute-start(bf16[16,1536]{1,0:T(8,128)(2,1)S(1)} %get-tuple-element.26.x0), channel_id=1, source_target_pairs={{0,3},{1,0},{2,1},{3,2},{4,7},{5,4},{6,5},{7,6},{8,11},{9,8},{10,9... | collective-permute-start | bytes 147464 | tf_op jit(solution)/shard_map/ppermute | solution.py:303
  45.5 0.0 collective-permute-start.8
  45.5 1.0 %collective-permute-start.7 = (bf16[16,1536]{1,0:T(8,128)(2,1)S(1)}, bf16[16,1536]{1,0:T(8,128)(2,1)S(1)}, u32[]{:S(2)}, u32[]{:S(2)}) collective-permute-start(bf16[16,1536]{1,0:T(8,128)(2,1)S(1)} %get-tuple-element.26.x0), channel_id=1, source_target_pairs={{0,1},{1,2},{2,3},{3,0},{4,5},{5,6},{6,7},{7,4},{8,9},{9,10},{10,1... | collective-permute-start | bytes 147464 | tf_op jit(solution)/shard_map/ppermute | solution.py:303
  46.5 0.0 copy-start
  46.5 3.2 %shard_map.188 = (bf16[1536,1152]{1,0:T(8,128)(2,1)S(1)}, bf16[1152,1536]{1,0:T(8,128)(2,1)S(1)}) custom-call(bf16[1536,1152]{1,0:T(8,128)(2,1)} %refs_0_, bf16[1152,1536]{1,0:T(8,128)(2,1)} %refs_1_.2), custom_call_target="tpu_custom_call" | custom-call | bytes 14000000 | tf_op jit(solution)/shard_map/pallas_call | solution.py:19
  49.7 0.0 collective-permute-done.9.x3
  49.7 1.4 %collective-permute-done.8.x2 = bf16[16,1536]{1,0:T(8,128)(2,1)S(1)} collective-permute-done((bf16[16,1536]{1,0:T(8,128)(2,1)S(1)}, bf16[16,1536]{1,0:T(8,128)(2,1)S(1)}, u32[]{:S(2)}, u32[]{:S(2)}) %collective-permute-start.8) | collective-permute-done | bytes 49184 | tf_op jit(solution)/shard_map/ppermute | solution.py:303
  51.2 0.2 collective-permute-done.7.x1
  51.4 0.0 copy-done
  51.4 0.0 copy-start.7
  51.4 0.0 copy-start.8
  51.4 0.0 copy-start.2
  51.4 0.0 copy-start.3
  51.4 0.0 copy-start.4
  51.4 0.0 copy-start.5
  51.4 2.0 %shard_map.189 = (f32[16,1536]{1,0:T(8,128)S(1)}, bf16[16,1536]{1,0:T(8,128)(2,1)S(1)}, bf16[16,1536]{1,0:T(8,128)(2,1)S(1)}, bf16[16,1536]{1,0:T(8,128)(2,1)S(1)}) custom-call(bf16[16,1536]{1,0:T(8,128)(2,1)S(1)} %get-tuple-element.26.x0, bf16[16,1536]{1,0:T(8,128)(2,1)S(1)} %collective-permute-done.7.x1, bf16[16,1536]{1,0:T(8,128)(2,1)S(1)} %collective-permute-done.8.x2, ...), custom_call_target="tpu_custom_call" | custom-call | flops 700000000 | bytes 1000000 | tf_op jit(solution)/shard_map/pallas_call | solution.py:19
  53.4 1.5 %collective-permute-start.10 = (bf16[16,1536]{1,0:T(8,128)(2,1)S(1)}, bf16[16,1536]{1,0:T(8,128)(2,1)S(1)}, u32[]{:S(2)}, u32[]{:S(2)}) collective-permute-start(bf16[16,1536]{1,0:T(8,128)(2,1)S(1)} %get-tuple-element.32), channel_id=1, source_target_pairs={{0,3},{1,0},{2,1},{3,2},{4,7},{5,4},{6,5},{7,6},{8,11},{9,8},{10,9... | collective-permute-start | bytes 147464 | tf_op jit(solution)/shard_map/ppermute | solution.py:303
  54.9 2.3 %collective-permute-start.11 = (bf16[16,1536]{1,0:T(8,128)(2,1)S(1)}, bf16[16,1536]{1,0:T(8,128)(2,1)S(1)}, u32[]{:S(2)}, u32[]{:S(2)}) collective-permute-start(bf16[16,1536]{1,0:T(8,128)(2,1)S(1)} %get-tuple-element.33), channel_id=1, source_target_pairs={{0,2},{1,3},{2,0},{3,1},{4,6},{5,7},{6,4},{7,5},{8,10},{9,11},{10,... | collective-permute-start | bytes 147464 | tf_op jit(solution)/shard_map/ppermute | solution.py:303
  57.2 0.0 collective-permute-start.12
  57.2 0.0 copy-done.7
  57.3 0.0 copy-done.8
  57.3 0.0 copy-done.2
  57.3 0.0 copy-done.3
  57.3 0.0 copy-done.4
  57.3 0.0 copy-done.5
  57.3 1.4 %shard_map.191 = bf16[1,2,4,64,256]{4,3,2,1,0:T(8,128)(2,1)} custom-call(bf16[64,40,128]{2,1,0:T(8,128)(2,1)S(1)} %all-to-all-done.arr_ref, bf16[1,4,64,256]{3,2,1,0:T(8,128)(2,1)S(1)} %copy-done.2, bf16[1,2,4,2,256]{4,3,2,1,0:T(2,128)(2,1)S(1)} %copy-done.3, s32[1,64]{1,0:T(1,128)S(1)} %copy-done.5, s32[1,2,4]{2,1,0:T(2,128)S(1)} %copy-done.4), custom_call_target="tpu_custom_call" | custom-call | flops 1000000 | bytes 1500000 | tf_op jit(solution)/shard_map/pallas_call | solution.py:19
  58.7 0.0 collective-permute-done.10.y1
  58.7 1.8 %collective-permute-done.11.y2 = bf16[16,1536]{1,0:T(8,128)(2,1)S(1)} collective-permute-done((bf16[16,1536]{1,0:T(8,128)(2,1)S(1)}, bf16[16,1536]{1,0:T(8,128)(2,1)S(1)}, u32[]{:S(2)}, u32[]{:S(2)}) %collective-permute-start.11) | collective-permute-done | bytes 49184 | tf_op jit(solution)/shard_map/ppermute | solution.py:303
  60.5 2.0 %collective-permute-done.12.y3 = bf16[16,1536]{1,0:T(8,128)(2,1)S(1)} collective-permute-done((bf16[16,1536]{1,0:T(8,128)(2,1)S(1)}, bf16[16,1536]{1,0:T(8,128)(2,1)S(1)}, u32[]{:S(2)}, u32[]{:S(2)}) %collective-permute-start.12) | collective-permute-done | bytes 49184 | tf_op jit(solution)/shard_map/ppermute | solution.py:303
  62.5 0.8 %shard_map.190 = (f32[1,2,2,4]{3,2,1,0:T(2,128)}, bf16[1,2,4,2,1536]{4,3,2,1,0:T(2,128)(2,1)}) custom-call(bf16[16,1536]{1,0:T(8,128)(2,1)S(1)} %get-tuple-element.25.h1_ref, f32[16,1536]{1,0:T(8,128)S(1)} %get-tuple-element.31.y0, bf16[16,1536]{1,0:T(8,128)(2,1)S(1)} %collective-permute-done.10.y1, bf16[16,1536]{1,0:T(8,128)(2,1)S(1)} %collective-permute-done.11.y2, ...), custom_call_target="tpu_custom_call" | custom-call | flops 1000000 | bytes 500000 | tf_op jit(solution)/shard_map/pallas_call | solution.py:19
  (5 shorter events, 0.1 us)
Async XLA Ops:
  2.6 19.9 %collective-permute-start.1 = (bf16[384,768]{1,0:T(8,128)(2,1)}, bf16[384,768]{1,0:T(8,128)(2,1)S(1)}, u32[]{:S(2)}, u32[]{:S(2)}) collective-permute-start(bf16[384,768]{1,0:T(8,128)(2,1)} %shard_map.184), channel_id=1, source_target_pairs={{0,3},{1,0},{2,1},{3,2},{4,7},{5,4},{6,5},{7,6},{8,11},{9,8},{10,9... | collective-permute-start | bytes 1769480 | tf_op jit(solution)/shard_map/ppermute | solution.py:303
  5.4 17.0 %collective-permute-start = (bf16[384,768]{1,0:T(8,128)(2,1)}, bf16[384,768]{1,0:T(8,128)(2,1)S(1)}, u32[]{:S(2)}, u32[]{:S(2)}) collective-permute-start(bf16[384,768]{1,0:T(8,128)(2,1)} %shard_map.184), channel_id=1, source_target_pairs={{0,1},{1,2},{2,3},{3,0},{4,5},{5,6},{6,7},{7,4},{8,9},{9,10},{10,1... | collective-permute-start | bytes 1769480 | tf_op jit(solution)/shard_map/ppermute | solution.py:303
  7.8 31.7 %all-to-all-start = ((bf16[64,40,128]{2,1,0:T(8,128)(2,1)}), bf16[64,40,128]{2,1,0:T(8,128)(2,1)S(1)}, u32[]{:S(2)}, u32[]{:S(2)}) async-start(bf16[64,40,128]{2,1,0:T(8,128)(2,1)} %bitcast.9), calls=%async_computation | async-start | bytes 1310720 | tf_op jit(solution)/shard_map/all_to_all | solution.py:329
  23.6 13.8 %copy-start.6 = (f32[1536]{0:T(1024)S(1)}, f32[1536]{0:T(1024)}, u32[]{:S(2)}) copy-start(f32[1536]{0:T(1024)} %param.28) | copy-start | bytes 18436
  23.6 16.0 %copy-start.1 = (f32[8,8960]{1,0:T(8,128)S(1)}, f32[8,8960]{1,0:T(8,128)}, u32[]{:S(2)}) copy-start(f32[8,8960]{1,0:T(8,128)} %shard_map.186.refs_0_) | copy-start | bytes 860164
  23.6 16.0 %collective-permute-start.4 = (bf16[2,384,768]{2,1,0:T(8,128)(2,1)}, bf16[2,384,768]{2,1,0:T(8,128)(2,1)}, u32[]{:S(2)}, u32[]{:S(2)}) collective-permute-start(bf16[2,384,768]{2,1,0:T(8,128)(2,1)} %pad_maximum_fusion), channel_id=1, source_target_pairs={{0,4},{4,0},{8,12},{12,8},{16,20},{20,16},{24,28},{28,24},{32,36},... | collective-permute-start | bytes 3538952 | tf_op jit(solution)/shard_map/ppermute | solution.py:306
  23.7 10.1 %collective-permute-start.3 = (bf16[192,768]{1,0:T(8,128)(2,1)S(1)}, bf16[192,768]{1,0:T(8,128)(2,1)S(1)}, u32[]{:S(2)}, u32[]{:S(2)}) collective-permute-start(bf16[192,768]{1,0:T(8,128)(2,1)S(1)} %slice.7), channel_id=1, source_target_pairs={{0,3},{1,0},{2,1},{3,2},{4,7},{5,4},{6,5},{7,6},{8,11},{9,8},{10,9... | collective-permute-start | bytes 884744 | tf_op jit(solution)/shard_map/ppermute | solution.py:303
  27.1 10.3 %collective-permute-start.2 = (bf16[192,768]{1,0:T(8,128)(2,1)S(1)}, bf16[192,768]{1,0:T(8,128)(2,1)S(1)}, u32[]{:S(2)}, u32[]{:S(2)}) collective-permute-start(bf16[192,768]{1,0:T(8,128)(2,1)S(1)} %slice.6), channel_id=1, source_target_pairs={{0,1},{1,2},{2,3},{3,0},{4,5},{5,6},{6,7},{7,4},{8,9},{9,10},{10,1... | collective-permute-start | bytes 884744 | tf_op jit(solution)/shard_map/ppermute | solution.py:303
  33.8 3.5 %collective-permute-start.6 = (bf16[192,768]{1,0:T(8,128)(2,1)S(1)}, bf16[192,768]{1,0:T(8,128)(2,1)S(1)}, u32[]{:S(2)}, u32[]{:S(2)}) collective-permute-start(bf16[192,768]{1,0:T(8,128)(2,1)S(1)} %collective-permute-done.3.refs_5_), channel_id=1, source_target_pairs={{0,4},{4,0},{8,12},{12,8},{16,20},{20,16},{24,28},{28,24},{32,36},... | collective-permute-start | bytes 884744 | tf_op jit(solution)/shard_map/ppermute | solution.py:306
  37.4 1.6 %collective-permute-start.5 = (bf16[192,768]{1,0:T(8,128)(2,1)S(1)}, bf16[192,768]{1,0:T(8,128)(2,1)S(1)}, u32[]{:S(2)}, u32[]{:S(2)}) collective-permute-start(bf16[192,768]{1,0:T(8,128)(2,1)S(1)} %collective-permute-done.2.refs_4_), channel_id=1, source_target_pairs={{0,4},{4,0},{8,12},{12,8},{16,20},{20,16},{24,28},{28,24},{32,36},... | collective-permute-start | bytes 884744 | tf_op jit(solution)/shard_map/ppermute | solution.py:306
  42.2 7.5 %collective-permute-start.9 = (bf16[16,1536]{1,0:T(8,128)(2,1)S(1)}, bf16[16,1536]{1,0:T(8,128)(2,1)S(1)}, u32[]{:S(2)}, u32[]{:S(2)}) collective-permute-start(bf16[16,1536]{1,0:T(8,128)(2,1)S(1)} %get-tuple-element.26.x0), channel_id=1, source_target_pairs={{0,3},{1,0},{2,1},{3,2},{4,7},{5,4},{6,5},{7,6},{8,11},{9,8},{10,9... | collective-permute-start | bytes 147464 | tf_op jit(solution)/shard_map/ppermute | solution.py:303
  45.5 5.6 %collective-permute-start.8 = (bf16[16,1536]{1,0:T(8,128)(2,1)S(1)}, bf16[16,1536]{1,0:T(8,128)(2,1)S(1)}, u32[]{:S(2)}, u32[]{:S(2)}) collective-permute-start(bf16[16,1536]{1,0:T(8,128)(2,1)S(1)} %get-tuple-element.26.x0), channel_id=1, source_target_pairs={{0,2},{1,3},{2,0},{3,1},{4,6},{5,7},{6,4},{7,5},{8,10},{9,11},{10,... | collective-permute-start | bytes 147464 | tf_op jit(solution)/shard_map/ppermute | solution.py:303
  45.5 5.8 %collective-permute-start.7 = (bf16[16,1536]{1,0:T(8,128)(2,1)S(1)}, bf16[16,1536]{1,0:T(8,128)(2,1)S(1)}, u32[]{:S(2)}, u32[]{:S(2)}) collective-permute-start(bf16[16,1536]{1,0:T(8,128)(2,1)S(1)} %get-tuple-element.26.x0), channel_id=1, source_target_pairs={{0,1},{1,2},{2,3},{3,0},{4,5},{5,6},{6,7},{7,4},{8,9},{9,10},{10,1... | collective-permute-start | bytes 147464 | tf_op jit(solution)/shard_map/ppermute | solution.py:303
  46.5 4.9 %copy-start = (bf16[1536,1152]{1,0:T(8,128)(2,1)S(1)}, bf16[1536,1152]{1,0:T(8,128)(2,1)}, u32[]{:S(2)}) copy-start(bf16[1536,1152]{1,0:T(8,128)(2,1)} %wg.1) | copy-start | bytes 10616836
  51.4 5.9 %copy-start.7 = (f32[1536]{0:T(1024)S(1)}, f32[1536]{0:T(1024)}, u32[]{:S(2)}) copy-start(f32[1536]{0:T(1024)} %param.32) | copy-start | bytes 18436
  51.4 5.9 %copy-start.8 = (f32[1536]{0:T(1024)S(1)}, f32[1536]{0:T(1024)}, u32[]{:S(2)}) copy-start(f32[1536]{0:T(1024)} %param.33) | copy-start | bytes 18436
  51.4 5.9 %copy-start.2 = (bf16[1,4,64,256]{3,2,1,0:T(8,128)(2,1)S(1)}, bf16[1,4,64,256]{3,2,1,0:T(8,128)(2,1)}, u32[]{:S(2)}) copy-start(bf16[1,4,64,256]{3,2,1,0:T(8,128)(2,1)} %tails_ref.3) | copy-start | bytes 393220
  51.4 5.9 %copy-start.3 = (bf16[1,2,4,2,256]{4,3,2,1,0:T(2,128)(2,1)S(1)}, bf16[1,2,4,2,256]{4,3,2,1,0:T(2,128)(2,1)}, u32[]{:S(2)}) copy-start(bf16[1,2,4,2,256]{4,3,2,1,0:T(2,128)(2,1)} %new_ref.3) | copy-start | bytes 24580
  51.4 5.9 %copy-start.4 = (s32[1,2,4]{2,1,0:T(2,128)S(1)}, s32[1,2,4]{2,1,0:T(2,128)}, u32[]{:S(2)}) copy-start(s32[1,2,4]{2,1,0:T(2,128)} %tlen_ref.3) | copy-start | bytes 100
  51.4 5.9 %copy-start.5 = (s32[1,64]{1,0:T(1,128)S(1)}, s32[1,64]{1,0:T(1,128)}, u32[]{:S(2)}) copy-start(s32[1,64]{1,0:T(1,128)} %holder_ref.3) | copy-start | bytes 772
  53.4 5.3 %collective-permute-start.10 = (bf16[16,1536]{1,0:T(8,128)(2,1)S(1)}, bf16[16,1536]{1,0:T(8,128)(2,1)S(1)}, u32[]{:S(2)}, u32[]{:S(2)}) collective-permute-start(bf16[16,1536]{1,0:T(8,128)(2,1)S(1)} %get-tuple-element.32), channel_id=1, source_target_pairs={{0,3},{1,0},{2,1},{3,2},{4,7},{5,4},{6,5},{7,6},{8,11},{9,8},{10,9... | collective-permute-start | bytes 147464 | tf_op jit(solution)/shard_map/ppermute | solution.py:303
  54.9 5.6 %collective-permute-start.11 = (bf16[16,1536]{1,0:T(8,128)(2,1)S(1)}, bf16[16,1536]{1,0:T(8,128)(2,1)S(1)}, u32[]{:S(2)}, u32[]{:S(2)}) collective-permute-start(bf16[16,1536]{1,0:T(8,128)(2,1)S(1)} %get-tuple-element.33), channel_id=1, source_target_pairs={{0,2},{1,3},{2,0},{3,1},{4,6},{5,7},{6,4},{7,5},{8,10},{9,11},{10,... | collective-permute-start | bytes 147464 | tf_op jit(solution)/shard_map/ppermute | solution.py:303
  57.2 5.3 %collective-permute-start.12 = (bf16[16,1536]{1,0:T(8,128)(2,1)S(1)}, bf16[16,1536]{1,0:T(8,128)(2,1)S(1)}, u32[]{:S(2)}, u32[]{:S(2)}) collective-permute-start(bf16[16,1536]{1,0:T(8,128)(2,1)S(1)} %get-tuple-element.34), channel_id=1, source_target_pairs={{0,1},{1,2},{2,3},{3,0},{4,5},{5,6},{6,7},{7,4},{8,9},{9,10},{10,1... | collective-permute-start | bytes 147464 | tf_op jit(solution)/shard_map/ppermute | solution.py:303

commit v3 on v2

--- a/solution.py
+++ b/solution.py
@@ -15,12 +15,12 @@
 HBM = pl.BlockSpec(memory_space=pltpu.HBM)
 
 
-def call(body, outs, operands, specs, scratch=(), flops=0, nbytes=0, limit=8):
+def call(body, outs, operands, specs, scratch=(), flops=0, nbytes=0, limit=8, out_specs=None):
     return pl.pallas_call(
         body,
         out_shape=outs,
         in_specs=specs,
-        out_specs=jax.tree.map(lambda _: VMEM, outs),
+        out_specs=jax.tree.map(lambda _: VMEM, outs) if out_specs is None else out_specs,
         scratch_shapes=scratch,
         cost_estimate=pl.CostEstimate(flops=flops, bytes_accessed=nbytes, transcendentals=0),
         compiler_params=pltpu.CompilerParams(vmem_limit_bytes=limit << 20),
@@ -41,14 +41,6 @@
         scr[pl.ds(i, dests, stride=2 * rows), :] = got[:, :half]
         scr[pl.ds(rows + i, dests, stride=2 * rows), :] = got[:, half:]
     out_ref[...] = scr[...].astype(BF)
-
-
-def take_half(w_hbm, out_ref, sem):
-    half = out_ref.shape[1]
-    core = lax.rem(lax.axis_index("req"), 2)
-    copy = pltpu.make_async_copy(w_hbm.at[:, pl.ds(pl.multiple_of(core * half, 128), half)], out_ref, sem)
-    copy.start()
-    copy.wait()
 
 
 def load_rows(ref, q):
@@ -148,56 +140,54 @@
     pos = jnp.where(inside < page, base + inside, 1 << 20)
     sample, token, length = row_lengths(tlen_ref, 1, count)
     bias = window_bias(pos, plen_ref[0, 1], win, tail, sample, token, length)
-    parts = (bias, load_rows(res_ref, 0), load_rows(res_ref, 1), out, load_rows(q_ref, 1), load_rows(new_ref, 1))
-    out_ref[...] = jnp.concatenate(parts, axis=1)
-
-
-def moved(size, page, arr_ref, norm_ref, *refs):
+    parts = (bias, load_rows(q_ref, 1), load_rows(new_ref, 1), load_rows(res_ref, 0), load_rows(res_ref, 1), out)
+    out_ref[...] = jnp.concatenate(parts, axis=1).astype(BF)
+
+
+def moved(size, page, arr_ref, state, norm_ref, *refs):
     count = len(refs) // 2 - 2
     hbm, (h1_ref, normed_ref), vmem, (attn, sems) = refs[:count], refs[count : count + 2], refs[count + 2 : -2], refs[-2:]
     copies = [pltpu.make_async_copy(a, b, sems.at[i]) for i, (a, b) in enumerate(zip(hbm, vmem))]
     for c in copies:
         c.start()
-    state, wown, a1, a3, top, bot, b13, btop, bbot = vmem
-    copies[0].wait()
+    wown, near, far, part_a, part_b = vmem
     n, width = arr_ref.shape[0], attn.shape[1]
-    at = [n + i * width for i in range(5)]
-    bias = state[:, :n]
-    res = jnp.concatenate([state[:, at[0] : at[1]], state[:, at[1] : at[2]]], axis=0)
-    first, q8, fresh = state[:, at[2] : at[3]], state[:, at[3] : at[4]], state[:, at[4] :].astype(BF)
     rows = state.shape[0]
+    bias = state[:, :n].astype(F32)
+    at = [n + width + 2 * size + i * width for i in range(4)]
+    q8, fresh = state[:, n : n + width], state[:, n + width : at[0]]
+    res = jnp.concatenate([state[:, at[0] : at[1]], state[:, at[1] : at[2]]], axis=0).astype(F32)
+    first = state[:, at[2] : at[3]].astype(F32)
     r = iota((rows, 1), 0)
     nb = new_bias(r >> 1, r & 1, rows // 2)
     arr = arr_ref[...]
     second = attend(
-        stack_heads(q8, size),
+        stack_heads(q8.astype(F32), size),
         [(arr, arr, bias, page), (fresh[:, :size], fresh[:, size:], nb, 0)],
         rows,
         size,
     )
+    for c in copies:
+        c.wait()
     attn[...] = jnp.concatenate([first, second], axis=0).astype(BF)
-    for c in copies[1:]:
-        c.wait()
     me = lax.axis_index("mlp")
-    low = lax.rem(lax.axis_index("req"), 2) == 0
+    core = lax.rem(lax.axis_index("req"), 2)
     block = wown.shape[0]
-    n_mlp = attn.shape[1] // block
-    part = top.shape[0]
-
-    def piece(k, first=0, count=block):
-        rb = lax.rem(me - k + n_mlp, n_mlp)
-        return attn[:, pl.ds(pl.multiple_of(rb * block, 128), block)][:, first : first + count]
+    n_mlp = width // block
+    part = part_a.shape[0]
+
+    def piece(k):
+        rb = lax.rem(me + k + n_mlp, n_mlp)
+        return attn[:, pl.ds(pl.multiple_of(rb * block, 128), block)]
 
     def product(x, w):
         return jnp.dot(x, w[...], preferred_element_type=F32)
 
-    p1, p3, pt, pb = piece(1), piece(n_mlp - 1), piece(2, 0, part), piece(2, part, block - part)
-    same = product(p1, a1) + product(p3, a3) + product(pt, top) + product(pb, bot)
-    other = product(p1, b13.at[0]) + product(p3, b13.at[1]) + product(pt, btop) + product(pb, bbot)
-    own = product(piece(0), wown)
-    left = jnp.where(low, same, other)
-    right = jnp.where(low, other, same)
-    mixed = own + jnp.concatenate([left, right], axis=1)
+    opposite = piece(2).astype(F32)
+    low, high = opposite[:, :part], opposite[:, part:]
+    mixed = product(piece(0), wown) + product(piece(2 * core - 1), near) + product(piece(1 - 2 * core), far)
+    mixed = mixed + product(jnp.where(core == 0, low, high).astype(BF), part_a)
+    mixed = mixed + product(jnp.where(core == 0, high, low).astype(BF), part_b)
     h1 = (res + mixed).astype(BF)
     h1_ref[...] = h1
     f = h1.astype(F32)
@@ -297,7 +287,7 @@
     rows = 4 * samp
     arrived_rows = n_req * 2 * page
     block, hid = w_out.shape[0], w_gate.shape[1]
-    half, part = width // 2, block // 2
+    part = block // 2
 
     def shift(x, k):
         return lax.ppermute(x, "mlp", [(i, (i + k) % n_mlp) for i in range(n_mlp)])
@@ -305,21 +295,15 @@
     def swap(x):
         return lax.ppermute(x, "req", [(i, i ^ 1) for i in range(n_req)])
 
-    mine = call(
-        take_half,
-        jax.ShapeDtypeStruct((block, half), BF),
-        (w_out,),
-        [HBM],
-        [pltpu.SemaphoreType.DMA],
-        nbytes=1_200_000,
-        limit=60,
-    )
-    a1, a3 = shift(mine, 1), shift(mine, -1)
-    slot, _ = lax.optimization_barrier((serve_slot, mine))
+    def onward(x):
+        to = [(r * n_mlp + m, r * n_mlp + (m + 1 - 2 * (r % 2)) % n_mlp) for r in range(n_req) for m in range(n_mlp)]
+        return lax.ppermute(x, ("req", "mlp"), to)
+
+    near = onward(w_out)
     outgoing = call(
         pick_pages,
         jax.ShapeDtypeStruct((arrived_rows, size), BF),
-        (jnp.transpose(page_pool, (1, 0, 2)), slot),
+        (jnp.transpose(page_pool, (1, 0, 2)), serve_slot),
         [VMEM, VMEM],
         [pltpu.VMEM((arrived_rows, size), F32)],
         flops=100_000_000,
@@ -330,19 +314,18 @@
         outgoing.reshape(n_req, 2 * page, size), "req", split_axis=0, concat_axis=0, tiled=True
     )
     q_late, outgoing = lax.optimization_barrier((queries, outgoing))
-    span = arrived_rows + 4 * width + 2 * size
     state = call(
         functools.partial(resident, win, tail, size, page, arrived_rows),
-        jax.ShapeDtypeStruct((2 * samp, span), F32),
+        jax.ShapeDtypeStruct((2 * samp, arrived_rows + 4 * width + 2 * size), BF),
         (q_late, new_kv, prompt_kv, tail_kv, page_holder, prompt_len, tail_len, residual),
         [VMEM, VMEM, VMEM, VMEM, SMEM, SMEM, SMEM, VMEM],
         flops=100_000_000,
         nbytes=1_000_000,
-        limit=60,
-    )
-    a1, a3, state = lax.optimization_barrier((a1, a3, state))
-    top, bot = shift(a1[:part], 1), shift(a3[part:], -1)
-    b13, btop, bbot = swap(jnp.stack([a1, a3])), swap(top), swap(bot)
+        limit=40,
+    )
+    core = lax.rem(lax.axis_index("req"), 2)
+    part_a = onward(lax.dynamic_slice_in_dim(near, core * part, part, 0))
+    far, part_b = swap(near), swap(part_a)
     tails_out = call(
         functools.partial(write_tails, win, page),
         jax.ShapeDtypeStruct((1, 2) + tail_kv.shape[1:], BF),
@@ -352,13 +335,13 @@
         flops=1_000_000,
         nbytes=1_500_000,
     )
-    pieces = (state, w_out, a1, a3, top, bot, b13, btop, bbot)
+    pieces = (w_out, near, far, part_a, part_b)
     row_bf = jax.ShapeDtypeStruct((rows, width), BF)
     h1, normed = call(
         functools.partial(moved, size, page),
         (row_bf, row_bf),
-        (arrived.reshape(arrived_rows, size), norm_mlp[None], *pieces),
-        [VMEM, VMEM] + [HBM] * len(pieces),
+        (arrived.reshape(arrived_rows, size), state, norm_mlp[None], *pieces),
+        [VMEM] * 3 + [HBM] * len(pieces),
         [pltpu.VMEM(x.shape, x.dtype) for x in pieces]
         + [pltpu.VMEM((rows, width), BF), pltpu.SemaphoreType.DMA((len(pieces),))],
         flops=200_000_000,

time: 63.6 us -> 58.4 us (0.918)
  starting transfers between devices: 26.3 us -> 21.2 us
  Pallas kernels: 17.2 us -> 13.9 us
  waiting for transfers between devices: 17.8 us -> 20 us
  local copies, waits for them, and re-layouts: 0.1 us -> 2.17 us
  other arithmetic: 1.12 us -> 0 us
    ppermute x0 -> x2, waiting for transfers between devices: none -> 11.4 us  [onward(): return lax.ppermute(x, ('req', 'mlp'), to)]
    ppermute x10 -> x6, waiting for transfers between devices: 15.6 us -> 5.09 us  [shift(): return lax.ppermute(x, 'mlp', [(i, (i + k) % n_mlp) for i in range(n_mlp)])]
    ppermute x10 -> x6, starting transfers between devices: 14.4 us -> 6.2 us  [shift(): return lax.ppermute(x, 'mlp', [(i, (i + k) % n_mlp) for i in range(n_mlp)])]
    pallas_call x8 -> x7, Pallas kernels: 17.2 us -> 13.9 us  [call(): pl.pallas_call(body, out_shape=outs, in_specs=specs, out_specs=jax.tree.m...]
    all_to_all x1, waiting for transfers between devices: 0.57 us -> 3.51 us  [on_device(): lax.all_to_all(outgoing.reshape(n_req, 2 * page, size), 'req', split_axis...]
    unnamed x18 -> x28, local copies, waits for them, and re-layouts: 0.04 us -> 2.11 us
    ppermute x0 -> x2, starting transfers between devices: none -> 1.93 us  [onward(): return lax.ppermute(x, ('req', 'mlp'), to)]
    ppermute x3 -> x2, waiting for transfers between devices: 1.56 us -> 0.01 us  [swap(): return lax.ppermute(x, 'req', [(i, i ^ 1) for i in range(n_req)])]
  transfers between devices with their start and end apart: 14 -> 11, of which waited for: 8 -> 8; matrix products, arithmetic and copies ran while one was open for 2% -> 0% of each run, Pallas kernels for 16% -> 14%
where the time goes in v3:
time: 58.4 us; the launch traced here: 58.2 us
  starting transfers between devices  21.2 us (36%)
  waiting for transfers between devices  20 us (34%)
  Pallas kernels  13.9 us (24%)
  local copies, waits for them, and re-layouts  2.17 us (4%)
  between operations  0.88 us (2%)
    pallas_call x7, Pallas kernels, call(): pl.pallas_call(body, out_shape=outs, in_specs=specs, out_specs=jax.tree.m...  13.9 us
    all_to_all x1, starting transfers between devices, on_device(): lax.all_to_all(outgoing.reshape(n_req, 2 * page, size), 'req', split_axis...  12.2 us
    ppermute x2, waiting for transfers between devices, onward(): return lax.ppermute(x, ('req', 'mlp'), to)  11.4 us
    ppermute x6, starting transfers between devices, shift(): return lax.ppermute(x, 'mlp', [(i, (i + k) % n_mlp) for i in range(n_mlp)])  6.2 us
    ppermute x6, waiting for transfers between devices, shift(): return lax.ppermute(x, 'mlp', [(i, (i + k) % n_mlp) for i in range(n_mlp)])  5.09 us
    all_to_all x1, waiting for transfers between devices, on_device(): lax.all_to_all(outgoing.reshape(n_req, 2 * page, size), 'req', split_axis...  3.51 us
    unnamed x28, local copies, waits for them, and re-layouts  2.11 us
    ppermute x2, starting transfers between devices, onward(): return lax.ppermute(x, ('req', 'mlp'), to)  1.93 us
  transfers between devices with their start and end apart: 11, of which 8 were waited for; matrix products, arithmetic and copies ran while one was open for 0% of the time, Pallas kernels for 14%

profile of v3, /device:TPU:32, one launch (start us, length us, event | category | flops | bytes accessed | tf_op | source)
XLA Modules:
  0.0 58.2 jit_solution(1872919986513358166)
XLA Ops:
  0.6 0.0 copy-start.1
  0.6 0.0 copy-start.11
  0.7 0.0 copy-start.4
  0.7 0.0 copy-start.7
  0.7 0.0 copy-start.8
  0.7 0.0 copy-start.2
  0.7 0.0 copy-start.6
  0.7 0.0 copy-start.9
  0.7 0.0 copy-start.5
  0.7 1.6 %collective-permute-start = (bf16[384,1536]{1,0:T(8,128)(2,1)}, bf16[384,1536]{1,0:T(8,128)(2,1)S(1)}, u32[]{:S(2)}, u32[]{:S(2)}) collective-permute-start(bf16[384,1536]{1,0:T(8,128)(2,1)} %refs_0_.1), channel_id=1, source_target_pairs={{0,1},{1,2},{2,3},{3,0},{4,7},{5,4},{6,5},{7,6},{8,9},{9,10},{10,1... | collective-permute-start | bytes 3538952 | tf_op jit(solution)/shard_map/ppermute | solution.py:300
  2.3 2.4 %shard_map.184 = bf16[2560,128]{1,0:T(8,128)(2,1)} custom-call(bf16[20,64,256]{2,1,0:T(8,128)(2,1)} %bitcast.6, s32[1,64]{1,0:T(1,128)} %slot_ref.1), custom_call_target="tpu_custom_call" | custom-call | flops 100000000 | bytes 1400000 | tf_op jit(solution)/shard_map/pallas_call | solution.py:19
  4.7 12.2 %all-to-all-start = ((bf16[64,40,128]{2,1,0:T(8,128)(2,1)}), bf16[64,40,128]{2,1,0:T(8,128)(2,1)S(1)}, u32[]{:S(2)}, u32[]{:S(2)}) async-start(bf16[64,40,128]{2,1,0:T(8,128)(2,1)} %bitcast.5), calls=%async_computation | async-start | bytes 1310720 | tf_op jit(solution)/shard_map/all_to_all | solution.py:313
  16.9 1.5 %collective-permute-done.refs_1_ = bf16[384,1536]{1,0:T(8,128)(2,1)S(1)} collective-permute-done((bf16[384,1536]{1,0:T(8,128)(2,1)}, bf16[384,1536]{1,0:T(8,128)(2,1)S(1)}, u32[]{:S(2)}, u32[]{:S(2)}) %collective-permute-start) | collective-permute-done | bytes 1179680 | tf_op jit(solution)/shard_map/ppermute | solution.py:300
  18.4 0.0 copy-start.10
  18.4 1.0 %copy-done.10 = bf16[384,1536]{1,0:T(8,128)(2,1)} copy-done((bf16[384,1536]{1,0:T(8,128)(2,1)}, bf16[384,1536]{1,0:T(8,128)(2,1)S(1)}, u32[]{:S(2)}) %copy-start.10) | copy-done | bytes 1179672
  19.5 0.4 collective-permute-start.2
  19.9 0.9 %collective-permute-start.1 = (bf16[384,1536]{1,0:T(8,128)(2,1)}, bf16[384,1536]{1,0:T(8,128)(2,1)}, u32[]{:S(2)}, u32[]{:S(2)}) collective-permute-start(bf16[384,1536]{1,0:T(8,128)(2,1)} %copy-done.10), channel_id=1, source_target_pairs={{0,4},{4,0},{8,12},{12,8},{16,20},{20,16},{24,28},{28,24},{32,36},... | collective-permute-start | bytes 3538952 | tf_op jit(solution)/shard_map/ppermute | solution.py:296
  20.7 9.9 %collective-permute-done.2.refs_3_ = bf16[192,1536]{1,0:T(8,128)(2,1)S(1)} collective-permute-done((bf16[192,1536]{1,0:T(8,128)(2,1)S(1)}, bf16[192,1536]{1,0:T(8,128)(2,1)S(1)}, u32[]{:S(2)}, u32[]{:S(2)}) %collective-permute-start.2) | collective-permute-done | bytes 589856 | tf_op jit(solution)/shard_map/ppermute | solution.py:300
  30.7 0.0 collective-permute-start.3
  30.7 0.0 copy-done.11
  30.7 0.0 copy-done.4
  30.7 0.0 copy-done.7
  30.7 0.0 copy-done.8
  30.7 0.0 copy-done.2
  30.7 0.0 copy-done.6
  30.7 0.0 copy-done.9
  30.7 0.0 copy-done.5
  30.8 0.0 copy-start.3
  30.8 1.0 %copy-done.3 = bf16[1,1024,256]{2,1,0:T(8,128)(2,1)S(1)} copy-done((bf16[1,1024,256]{2,1,0:T(8,128)(2,1)S(1)}, bf16[1,1024,256]{2,1,0:T(8,128)(2,1)}, u32[]{:S(2)}) %copy-start.3) | copy-done | bytes 524312
  31.8 1.5 %shard_map.185.state = bf16[8,8960]{1,0:T(8,128)(2,1)S(1)} custom-call(bf16[1,2,4,2,1536]{4,3,2,1,0:T(2,128)(2,1)S(1)} %copy-done.4, bf16[1,2,4,2,256]{4,3,2,1,0:T(2,128)(2,1)S(1)} %copy-done.6, bf16[1,1024,256]{2,1,0:T(8,128)(2,1)S(1)} %copy-done.3, bf16[1,4,64,256]{3,2,1,0:T(8,128)(2,1)S(1)} %copy-done.2, s32[1,64]{1,0:T(1,128)S(1)} %copy-done.8, ...), custom_call_target="tpu_custom_call" | custom-call | flops 100000000 | bytes 1000000 | tf_op jit(solution)/shard_map/pallas_call | solution.py:19
  33.3 3.5 %all-to-all-done.arr_ref = bf16[64,40,128]{2,1,0:T(8,128)(2,1)S(1)} async-done(((bf16[64,40,128]{2,1,0:T(8,128)(2,1)}), bf16[64,40,128]{2,1,0:T(8,128)(2,1)S(1)}, u32[]{:S(2)}, u32[]{:S(2)}) %all-to-all-start) | async-done | bytes 655392 | tf_op jit(solution)/shard_map/all_to_all | solution.py:313
  36.8 0.0 collective-permute-done.3.refs_4_
  36.8 0.0 collective-permute-done.1.refs_2_
  36.8 0.0 copy-done.1
  36.8 2.7 %shard_map.186 = (bf16[16,1536]{1,0:T(8,128)(2,1)S(1)}, bf16[16,1536]{1,0:T(8,128)(2,1)S(1)}) custom-call(bf16[2560,128]{1,0:T(8,128)(2,1)S(1)} %bitcast.4, bf16[8,8960]{1,0:T(8,128)(2,1)S(1)} %shard_map.185.state, f32[1,1536]{1,0:T(1,128)S(1)} %broadcast_in_dim.9.norm_ref, bf16[384,1536]{1,0:T(8,128)(2,1)S(1)} %copy-done.1, bf16[384,1536]{1,0:T(8,128)(2,1)} %copy-done.10, ...), custom_call_target="tpu_custom_call" | custom-call | flops 200000000 | bytes 6000000 | tf_op jit(solution)/shard_map/pallas_call | solution.py:19
  39.6 0.0 copy-start
  39.6 1.4 %collective-permute-start.6 = (bf16[16,1536]{1,0:T(8,128)(2,1)S(1)}, bf16[16,1536]{1,0:T(8,128)(2,1)S(1)}, u32[]{:S(2)}, u32[]{:S(2)}) collective-permute-start(bf16[16,1536]{1,0:T(8,128)(2,1)S(1)} %get-tuple-element.18.x0), channel_id=1, source_target_pairs={{0,3},{1,0},{2,1},{3,2},{4,7},{5,4},{6,5},{7,6},{8,11},{9,8},{10,9... | collective-permute-start | bytes 147464 | tf_op jit(solution)/shard_map/ppermute | solution.py:293
  41.0 1.8 %collective-permute-start.5 = (bf16[16,1536]{1,0:T(8,128)(2,1)S(1)}, bf16[16,1536]{1,0:T(8,128)(2,1)S(1)}, u32[]{:S(2)}, u32[]{:S(2)}) collective-permute-start(bf16[16,1536]{1,0:T(8,128)(2,1)S(1)} %get-tuple-element.18.x0), channel_id=1, source_target_pairs={{0,2},{1,3},{2,0},{3,1},{4,6},{5,7},{6,4},{7,5},{8,10},{9,11},{10,... | collective-permute-start | bytes 147464 | tf_op jit(solution)/shard_map/ppermute | solution.py:293
  42.8 0.6 %collective-permute-start.4 = (bf16[16,1536]{1,0:T(8,128)(2,1)S(1)}, bf16[16,1536]{1,0:T(8,128)(2,1)S(1)}, u32[]{:S(2)}, u32[]{:S(2)}) collective-permute-start(bf16[16,1536]{1,0:T(8,128)(2,1)S(1)} %get-tuple-element.18.x0), channel_id=1, source_target_pairs={{0,1},{1,2},{2,3},{3,0},{4,5},{5,6},{6,7},{7,4},{8,9},{9,10},{10,1... | collective-permute-start | bytes 147464 | tf_op jit(solution)/shard_map/ppermute | solution.py:293
  43.4 3.1 %shard_map.187 = (bf16[1536,1152]{1,0:T(8,128)(2,1)S(1)}, bf16[1152,1536]{1,0:T(8,128)(2,1)S(1)}) custom-call(bf16[1536,1152]{1,0:T(8,128)(2,1)} %refs_0_.2, bf16[1152,1536]{1,0:T(8,128)(2,1)} %refs_1_), custom_call_target="tpu_custom_call" | custom-call | bytes 14000000 | tf_op jit(solution)/shard_map/pallas_call | solution.py:19
  46.5 0.0 collective-permute-done.6.x3
  46.5 0.2 collective-permute-done.5.x2
  46.7 1.4 %collective-permute-done.4.x1 = bf16[16,1536]{1,0:T(8,128)(2,1)S(1)} collective-permute-done((bf16[16,1536]{1,0:T(8,128)(2,1)S(1)}, bf16[16,1536]{1,0:T(8,128)(2,1)S(1)}, u32[]{:S(2)}, u32[]{:S(2)}) %collective-permute-start.4) | collective-permute-done | bytes 49184 | tf_op jit(solution)/shard_map/ppermute | solution.py:293
  48.1 0.0 copy-done
  48.1 0.0 copy-start.12
  48.1 0.0 copy-start.13
  48.1 2.0 %shard_map.188 = (f32[16,1536]{1,0:T(8,128)S(1)}, bf16[16,1536]{1,0:T(8,128)(2,1)S(1)}, bf16[16,1536]{1,0:T(8,128)(2,1)S(1)}, bf16[16,1536]{1,0:T(8,128)(2,1)S(1)}) custom-call(bf16[16,1536]{1,0:T(8,128)(2,1)S(1)} %get-tuple-element.18.x0, bf16[16,1536]{1,0:T(8,128)(2,1)S(1)} %collective-permute-done.4.x1, bf16[16,1536]{1,0:T(8,128)(2,1)S(1)} %collective-permute-done.5.x2, ...), custom_call_target="tpu_custom_call" | custom-call | flops 700000000 | bytes 1000000 | tf_op jit(solution)/shard_map/pallas_call | solution.py:19
  50.1 1.2 %collective-permute-start.7 = (bf16[16,1536]{1,0:T(8,128)(2,1)S(1)}, bf16[16,1536]{1,0:T(8,128)(2,1)S(1)}, u32[]{:S(2)}, u32[]{:S(2)}) collective-permute-start(bf16[16,1536]{1,0:T(8,128)(2,1)S(1)} %get-tuple-element.24), channel_id=1, source_target_pairs={{0,3},{1,0},{2,1},{3,2},{4,7},{5,4},{6,5},{7,6},{8,11},{9,8},{10,9... | collective-permute-start | bytes 147464 | tf_op jit(solution)/shard_map/ppermute | solution.py:293
  51.3 0.5 collective-permute-start.8
  51.8 0.7 %collective-permute-start.9 = (bf16[16,1536]{1,0:T(8,128)(2,1)S(1)}, bf16[16,1536]{1,0:T(8,128)(2,1)S(1)}, u32[]{:S(2)}, u32[]{:S(2)}) collective-permute-start(bf16[16,1536]{1,0:T(8,128)(2,1)S(1)} %get-tuple-element.26), channel_id=1, source_target_pairs={{0,1},{1,2},{2,3},{3,0},{4,5},{5,6},{6,7},{7,4},{8,9},{9,10},{10,1... | collective-permute-start | bytes 147464 | tf_op jit(solution)/shard_map/ppermute | solution.py:293
  52.5 0.0 copy-done.12
  52.5 0.0 copy-done.13
  52.5 1.4 %shard_map.190 = bf16[1,2,4,64,256]{4,3,2,1,0:T(8,128)(2,1)} custom-call(bf16[64,40,128]{2,1,0:T(8,128)(2,1)S(1)} %all-to-all-done.arr_ref, bf16[1,4,64,256]{3,2,1,0:T(8,128)(2,1)S(1)} %copy-done.2, bf16[1,2,4,2,256]{4,3,2,1,0:T(2,128)(2,1)S(1)} %copy-done.6, s32[1,64]{1,0:T(1,128)S(1)} %copy-done.8, s32[1,2,4]{2,1,0:T(2,128)S(1)} %copy-done.7), custom_call_target="tpu_custom_call" | custom-call | flops 1000000 | bytes 1500000 | tf_op jit(solution)/shard_map/pallas_call | solution.py:19
  53.9 0.4 collective-permute-done.7.y1
  54.2 2.6 %collective-permute-done.8.y2 = bf16[16,1536]{1,0:T(8,128)(2,1)S(1)} collective-permute-done((bf16[16,1536]{1,0:T(8,128)(2,1)S(1)}, bf16[16,1536]{1,0:T(8,128)(2,1)S(1)}, u32[]{:S(2)}, u32[]{:S(2)}) %collective-permute-start.8) | collective-permute-done | bytes 49184 | tf_op jit(solution)/shard_map/ppermute | solution.py:293
  56.9 0.5 collective-permute-done.9.y3
  57.4 0.8 %shard_map.189 = (f32[1,2,2,4]{3,2,1,0:T(2,128)}, bf16[1,2,4,2,1536]{4,3,2,1,0:T(2,128)(2,1)}) custom-call(bf16[16,1536]{1,0:T(8,128)(2,1)S(1)} %get-tuple-element.17.h1_ref, f32[16,1536]{1,0:T(8,128)S(1)} %get-tuple-element.23.y0, bf16[16,1536]{1,0:T(8,128)(2,1)S(1)} %collective-permute-done.7.y1, bf16[16,1536]{1,0:T(8,128)(2,1)S(1)} %collective-permute-done.8.y2, ...), custom_call_target="tpu_custom_call" | custom-call | flops 1000000 | bytes 500000 | tf_op jit(solution)/shard_map/pallas_call | solution.py:19
  (4 shorter events, 0.1 us)
Async XLA Ops:
  0.6 36.2 %copy-start.1 = (bf16[384,1536]{1,0:T(8,128)(2,1)S(1)}, bf16[384,1536]{1,0:T(8,128)(2,1)}, u32[]{:S(2)}) copy-start(bf16[384,1536]{1,0:T(8,128)(2,1)} %refs_0_.1) | copy-start | bytes 3538948
  0.6 30.0 %copy-start.11 = (f32[1536]{0:T(1024)S(1)}, f32[1536]{0:T(1024)}, u32[]{:S(2)}) copy-start(f32[1536]{0:T(1024)} %param.28) | copy-start | bytes 18436
  0.7 30.0 %copy-start.4 = (bf16[1,2,4,2,1536]{4,3,2,1,0:T(2,128)(2,1)S(1)}, bf16[1,2,4,2,1536]{4,3,2,1,0:T(2,128)(2,1)}, u32[]{:S(2)}) copy-start(bf16[1,2,4,2,1536]{4,3,2,1,0:T(2,128)(2,1)} %q_ref) | copy-start | bytes 147460
  0.7 30.0 %copy-start.7 = (s32[1,2,4]{2,1,0:T(2,128)S(1)}, s32[1,2,4]{2,1,0:T(2,128)}, u32[]{:S(2)}) copy-start(s32[1,2,4]{2,1,0:T(2,128)} %tlen_ref.3) | copy-start | bytes 100
  0.7 30.0 %copy-start.8 = (s32[1,64]{1,0:T(1,128)S(1)}, s32[1,64]{1,0:T(1,128)}, u32[]{:S(2)}) copy-start(s32[1,64]{1,0:T(1,128)} %holder_ref.3) | copy-start | bytes 772
  0.7 30.0 %copy-start.2 = (bf16[1,4,64,256]{3,2,1,0:T(8,128)(2,1)S(1)}, bf16[1,4,64,256]{3,2,1,0:T(8,128)(2,1)}, u32[]{:S(2)}) copy-start(bf16[1,4,64,256]{3,2,1,0:T(8,128)(2,1)} %tails_ref.3) | copy-start | bytes 393220
  0.7 30.0 %copy-start.6 = (bf16[1,2,4,2,256]{4,3,2,1,0:T(2,128)(2,1)S(1)}, bf16[1,2,4,2,256]{4,3,2,1,0:T(2,128)(2,1)}, u32[]{:S(2)}) copy-start(bf16[1,2,4,2,256]{4,3,2,1,0:T(2,128)(2,1)} %new_ref.3) | copy-start | bytes 24580
  0.7 30.0 %copy-start.9 = (s32[1,2]{1,0:T(1,128)S(1)}, s32[1,2]{1,0:T(1,128)}, u32[]{:S(2)}) copy-start(s32[1,2]{1,0:T(1,128)} %plen_ref.1) | copy-start | bytes 28
  0.7 30.0 %copy-start.5 = (bf16[1,2,4,2,1536]{4,3,2,1,0:T(2,128)(2,1)S(1)}, bf16[1,2,4,2,1536]{4,3,2,1,0:T(2,128)(2,1)}, u32[]{:S(2)}) copy-start(bf16[1,2,4,2,1536]{4,3,2,1,0:T(2,128)(2,1)} %res_ref.1) | copy-start | bytes 147460
  0.7 17.7 %collective-permute-start = (bf16[384,1536]{1,0:T(8,128)(2,1)}, bf16[384,1536]{1,0:T(8,128)(2,1)S(1)}, u32[]{:S(2)}, u32[]{:S(2)}) collective-permute-start(bf16[384,1536]{1,0:T(8,128)(2,1)} %refs_0_.1), channel_id=1, source_target_pairs={{0,1},{1,2},{2,3},{3,0},{4,7},{5,4},{6,5},{7,6},{8,9},{9,10},{10,1... | collective-permute-start | bytes 3538952 | tf_op jit(solution)/shard_map/ppermute | solution.py:300
  4.7 32.1 %all-to-all-start = ((bf16[64,40,128]{2,1,0:T(8,128)(2,1)}), bf16[64,40,128]{2,1,0:T(8,128)(2,1)S(1)}, u32[]{:S(2)}, u32[]{:S(2)}) async-start(bf16[64,40,128]{2,1,0:T(8,128)(2,1)} %bitcast.5), calls=%async_computation | async-start | bytes 1310720 | tf_op jit(solution)/shard_map/all_to_all | solution.py:313
  18.4 1.0 %copy-start.10 = (bf16[384,1536]{1,0:T(8,128)(2,1)}, bf16[384,1536]{1,0:T(8,128)(2,1)S(1)}, u32[]{:S(2)}) copy-start(bf16[384,1536]{1,0:T(8,128)(2,1)S(1)} %collective-permute-done.refs_1_) | copy-start | bytes 3538948
  19.5 11.2 %collective-permute-start.2 = (bf16[192,1536]{1,0:T(8,128)(2,1)S(1)}, bf16[192,1536]{1,0:T(8,128)(2,1)S(1)}, u32[]{:S(2)}, u32[]{:S(2)}) collective-permute-start(bf16[192,1536]{1,0:T(8,128)(2,1)S(1)} %constant_dynamic-slice_fusion), channel_id=1, source_target_pairs={{0,1},{1,2},{2,3},{3,0},{4,7},{5,4},{6,5},{7,6},{8,9},{9,10},{10,1... | collective-permute-start | bytes 1769480 | tf_op jit(solution)/shard_map/ppermute | solution.py:300
  19.9 17.0 %collective-permute-start.1 = (bf16[384,1536]{1,0:T(8,128)(2,1)}, bf16[384,1536]{1,0:T(8,128)(2,1)}, u32[]{:S(2)}, u32[]{:S(2)}) collective-permute-start(bf16[384,1536]{1,0:T(8,128)(2,1)} %copy-done.10), channel_id=1, source_target_pairs={{0,4},{4,0},{8,12},{12,8},{16,20},{20,16},{24,28},{28,24},{32,36},... | collective-permute-start | bytes 3538952 | tf_op jit(solution)/shard_map/ppermute | solution.py:296
  30.7 6.2 %collective-permute-start.3 = (bf16[192,1536]{1,0:T(8,128)(2,1)S(1)}, bf16[192,1536]{1,0:T(8,128)(2,1)S(1)}, u32[]{:S(2)}, u32[]{:S(2)}) collective-permute-start(bf16[192,1536]{1,0:T(8,128)(2,1)S(1)} %collective-permute-done.2.refs_3_), channel_id=1, source_target_pairs={{0,4},{4,0},{8,12},{12,8},{16,20},{20,16},{24,28},{28,24},{32,36},... | collective-permute-start | bytes 1769480 | tf_op jit(solution)/shard_map/ppermute | solution.py:296
  30.8 1.0 %copy-start.3 = (bf16[1,1024,256]{2,1,0:T(8,128)(2,1)S(1)}, bf16[1,1024,256]{2,1,0:T(8,128)(2,1)}, u32[]{:S(2)}) copy-start(bf16[1,1024,256]{2,1,0:T(8,128)(2,1)} %kv_ref.1) | copy-start | bytes 1572868
  39.6 8.5 %copy-start = (bf16[1536,1152]{1,0:T(8,128)(2,1)S(1)}, bf16[1536,1152]{1,0:T(8,128)(2,1)}, u32[]{:S(2)}) copy-start(bf16[1536,1152]{1,0:T(8,128)(2,1)} %wg.1) | copy-start | bytes 10616836
  39.6 6.9 %collective-permute-start.6 = (bf16[16,1536]{1,0:T(8,128)(2,1)S(1)}, bf16[16,1536]{1,0:T(8,128)(2,1)S(1)}, u32[]{:S(2)}, u32[]{:S(2)}) collective-permute-start(bf16[16,1536]{1,0:T(8,128)(2,1)S(1)} %get-tuple-element.18.x0), channel_id=1, source_target_pairs={{0,3},{1,0},{2,1},{3,2},{4,7},{5,4},{6,5},{7,6},{8,11},{9,8},{10,9... | collective-permute-start | bytes 147464 | tf_op jit(solution)/shard_map/ppermute | solution.py:293
  41.0 5.7 %collective-permute-start.5 = (bf16[16,1536]{1,0:T(8,128)(2,1)S(1)}, bf16[16,1536]{1,0:T(8,128)(2,1)S(1)}, u32[]{:S(2)}, u32[]{:S(2)}) collective-permute-start(bf16[16,1536]{1,0:T(8,128)(2,1)S(1)} %get-tuple-element.18.x0), channel_id=1, source_target_pairs={{0,2},{1,3},{2,0},{3,1},{4,6},{5,7},{6,4},{7,5},{8,10},{9,11},{10,... | collective-permute-start | bytes 147464 | tf_op jit(solution)/shard_map/ppermute | solution.py:293
  42.8 5.3 %collective-permute-start.4 = (bf16[16,1536]{1,0:T(8,128)(2,1)S(1)}, bf16[16,1536]{1,0:T(8,128)(2,1)S(1)}, u32[]{:S(2)}, u32[]{:S(2)}) collective-permute-start(bf16[16,1536]{1,0:T(8,128)(2,1)S(1)} %get-tuple-element.18.x0), channel_id=1, source_target_pairs={{0,1},{1,2},{2,3},{3,0},{4,5},{5,6},{6,7},{7,4},{8,9},{9,10},{10,1... | collective-permute-start | bytes 147464 | tf_op jit(solution)/shard_map/ppermute | solution.py:293
  48.1 4.4 %copy-start.12 = (f32[1536]{0:T(1024)S(1)}, f32[1536]{0:T(1024)}, u32[]{:S(2)}) copy-start(f32[1536]{0:T(1024)} %param.32) | copy-start | bytes 18436
  48.1 4.4 %copy-start.13 = (f32[1536]{0:T(1024)S(1)}, f32[1536]{0:T(1024)}, u32[]{:S(2)}) copy-start(f32[1536]{0:T(1024)} %param.33) | copy-start | bytes 18436
  50.1 4.2 %collective-permute-start.7 = (bf16[16,1536]{1,0:T(8,128)(2,1)S(1)}, bf16[16,1536]{1,0:T(8,128)(2,1)S(1)}, u32[]{:S(2)}, u32[]{:S(2)}) collective-permute-start(bf16[16,1536]{1,0:T(8,128)(2,1)S(1)} %get-tuple-element.24), channel_id=1, source_target_pairs={{0,3},{1,0},{2,1},{3,2},{4,7},{5,4},{6,5},{7,6},{8,11},{9,8},{10,9... | collective-permute-start | bytes 147464 | tf_op jit(solution)/shard_map/ppermute | solution.py:293
  51.3 5.6 %collective-permute-start.8 = (bf16[16,1536]{1,0:T(8,128)(2,1)S(1)}, bf16[16,1536]{1,0:T(8,128)(2,1)S(1)}, u32[]{:S(2)}, u32[]{:S(2)}) collective-permute-start(bf16[16,1536]{1,0:T(8,128)(2,1)S(1)} %get-tuple-element.25), channel_id=1, source_target_pairs={{0,2},{1,3},{2,0},{3,1},{4,6},{5,7},{6,4},{7,5},{8,10},{9,11},{10,... | collective-permute-start | bytes 147464 | tf_op jit(solution)/shard_map/ppermute | solution.py:293
  51.8 5.6 %collective-permute-start.9 = (bf16[16,1536]{1,0:T(8,128)(2,1)S(1)}, bf16[16,1536]{1,0:T(8,128)(2,1)S(1)}, u32[]{:S(2)}, u32[]{:S(2)}) collective-permute-start(bf16[16,1536]{1,0:T(8,128)(2,1)S(1)} %get-tuple-element.26), channel_id=1, source_target_pairs={{0,1},{1,2},{2,3},{3,0},{4,5},{5,6},{6,7},{7,4},{8,9},{9,10},{10,1... | collective-permute-start | bytes 147464 | tf_op jit(solution)/shard_map/ppermute | solution.py:293

commit v4 on v3

--- a/solution.py
+++ b/solution.py
@@ -144,13 +144,13 @@
     out_ref[...] = jnp.concatenate(parts, axis=1).astype(BF)
 
 
-def moved(size, page, arr_ref, state, norm_ref, *refs):
+def moved(size, page, arr_ref, state, norm_ref, wown, *refs):
     count = len(refs) // 2 - 2
     hbm, (h1_ref, normed_ref), vmem, (attn, sems) = refs[:count], refs[count : count + 2], refs[count + 2 : -2], refs[-2:]
     copies = [pltpu.make_async_copy(a, b, sems.at[i]) for i, (a, b) in enumerate(zip(hbm, vmem))]
     for c in copies:
         c.start()
-    wown, near, far, part_a, part_b = vmem
+    near, far, part_a, part_b = vmem
     n, width = arr_ref.shape[0], attn.shape[1]
     rows = state.shape[0]
     bias = state[:, :n].astype(F32)
@@ -335,13 +335,13 @@
         flops=1_000_000,
         nbytes=1_500_000,
     )
-    pieces = (w_out, near, far, part_a, part_b)
+    pieces = (near, far, part_a, part_b)
     row_bf = jax.ShapeDtypeStruct((rows, width), BF)
     h1, normed = call(
         functools.partial(moved, size, page),
         (row_bf, row_bf),
-        (arrived.reshape(arrived_rows, size), state, norm_mlp[None], *pieces),
-        [VMEM] * 3 + [HBM] * len(pieces),
+        (arrived.reshape(arrived_rows, size), state, norm_mlp[None], w_out, *pieces),
+        [VMEM] * 4 + [HBM] * len(pieces),
         [pltpu.VMEM(x.shape, x.dtype) for x in pieces]
         + [pltpu.VMEM((rows, width), BF), pltpu.SemaphoreType.DMA((len(pieces),))],
         flops=200_000_000,

time: 58.4 us -> 58.2 us (level)
  transfers between devices with their start and end apart: 11 -> 11, of which waited for: 8 -> 8; matrix products, arithmetic and copies ran while one was open for 0% -> 0% of each run, Pallas kernels for 14% -> 15%
where the time goes in v4:
time: 58.2 us; the launch traced here: 57.9 us
  starting transfers between devices  21.2 us (36%)
  waiting for transfers between devices  20 us (34%)
  Pallas kernels  13.7 us (24%)
  local copies, waits for them, and re-layouts  2.17 us (4%)
  between operations  0.88 us (2%)
    pallas_call x7, Pallas kernels, call(): pl.pallas_call(body, out_shape=outs, in_specs=specs, out_specs=jax.tree.m...  13.7 us
    all_to_all x1, starting transfers between devices, on_device(): lax.all_to_all(outgoing.reshape(n_req, 2 * page, size), 'req', split_axis...  12.2 us
    ppermute x2, waiting for transfers between devices, onward(): return lax.ppermute(x, ('req', 'mlp'), to)  11.4 us
    ppermute x6, starting transfers between devices, shift(): return lax.ppermute(x, 'mlp', [(i, (i + k) % n_mlp) for i in range(n_mlp)])  6.19 us
    ppermute x6, waiting for transfers between devices, shift(): return lax.ppermute(x, 'mlp', [(i, (i + k) % n_mlp) for i in range(n_mlp)])  5.09 us
    all_to_all x1, waiting for transfers between devices, on_device(): lax.all_to_all(outgoing.reshape(n_req, 2 * page, size), 'req', split_axis...  3.51 us
    unnamed x28, local copies, waits for them, and re-layouts  2.11 us
    ppermute x2, starting transfers between devices, onward(): return lax.ppermute(x, ('req', 'mlp'), to)  1.93 us
  transfers between devices with their start and end apart: 11, of which 8 were waited for; matrix products, arithmetic and copies ran while one was open for 0% of the time, Pallas kernels for 15%

profile of v4, /device:TPU:32, one launch (start us, length us, event | category | flops | bytes accessed | tf_op | source)
XLA Modules:
  0.0 57.9 jit_solution(9758992452832004425)
XLA Ops:
  0.6 0.0 copy-start.1
  0.6 0.0 copy-start.11
  0.7 0.0 copy-start.4
  0.7 0.0 copy-start.7
  0.7 0.0 copy-start.8
  0.7 0.0 copy-start.2
  0.7 0.0 copy-start.6
  0.7 0.0 copy-start.9
  0.7 0.0 copy-start.5
  0.7 1.6 %collective-permute-start = (bf16[384,1536]{1,0:T(8,128)(2,1)}, bf16[384,1536]{1,0:T(8,128)(2,1)S(1)}, u32[]{:S(2)}, u32[]{:S(2)}) collective-permute-start(bf16[384,1536]{1,0:T(8,128)(2,1)} %wown.1), channel_id=1, source_target_pairs={{0,1},{1,2},{2,3},{3,0},{4,7},{5,4},{6,5},{7,6},{8,9},{9,10},{10,1... | collective-permute-start | bytes 3538952 | tf_op jit(solution)/shard_map/ppermute | solution.py:300
  2.3 2.4 %shard_map.184 = bf16[2560,128]{1,0:T(8,128)(2,1)} custom-call(bf16[20,64,256]{2,1,0:T(8,128)(2,1)} %bitcast.6, s32[1,64]{1,0:T(1,128)} %slot_ref.1), custom_call_target="tpu_custom_call" | custom-call | flops 100000000 | bytes 1400000 | tf_op jit(solution)/shard_map/pallas_call | solution.py:19
  4.7 12.2 %all-to-all-start = ((bf16[64,40,128]{2,1,0:T(8,128)(2,1)}), bf16[64,40,128]{2,1,0:T(8,128)(2,1)S(1)}, u32[]{:S(2)}, u32[]{:S(2)}) async-start(bf16[64,40,128]{2,1,0:T(8,128)(2,1)} %bitcast.5), calls=%async_computation | async-start | bytes 1310720 | tf_op jit(solution)/shard_map/all_to_all | solution.py:313
  16.9 1.5 %collective-permute-done.refs_0_ = bf16[384,1536]{1,0:T(8,128)(2,1)S(1)} collective-permute-done((bf16[384,1536]{1,0:T(8,128)(2,1)}, bf16[384,1536]{1,0:T(8,128)(2,1)S(1)}, u32[]{:S(2)}, u32[]{:S(2)}) %collective-permute-start) | collective-permute-done | bytes 1179680 | tf_op jit(solution)/shard_map/ppermute | solution.py:300
  18.4 0.0 copy-start.10
  18.4 1.0 %copy-done.10 = bf16[384,1536]{1,0:T(8,128)(2,1)} copy-done((bf16[384,1536]{1,0:T(8,128)(2,1)}, bf16[384,1536]{1,0:T(8,128)(2,1)S(1)}, u32[]{:S(2)}) %copy-start.10) | copy-done | bytes 1179672
  19.5 0.4 collective-permute-start.2
  19.9 0.9 %collective-permute-start.1 = (bf16[384,1536]{1,0:T(8,128)(2,1)}, bf16[384,1536]{1,0:T(8,128)(2,1)}, u32[]{:S(2)}, u32[]{:S(2)}) collective-permute-start(bf16[384,1536]{1,0:T(8,128)(2,1)} %copy-done.10), channel_id=1, source_target_pairs={{0,4},{4,0},{8,12},{12,8},{16,20},{20,16},{24,28},{28,24},{32,36},... | collective-permute-start | bytes 3538952 | tf_op jit(solution)/shard_map/ppermute | solution.py:296
  20.7 9.9 %collective-permute-done.2.refs_2_ = bf16[192,1536]{1,0:T(8,128)(2,1)S(1)} collective-permute-done((bf16[192,1536]{1,0:T(8,128)(2,1)S(1)}, bf16[192,1536]{1,0:T(8,128)(2,1)S(1)}, u32[]{:S(2)}, u32[]{:S(2)}) %collective-permute-start.2) | collective-permute-done | bytes 589856 | tf_op jit(solution)/shard_map/ppermute | solution.py:300
  30.7 0.0 collective-permute-start.3
  30.7 0.0 copy-done.11
  30.7 0.0 copy-done.4
  30.7 0.0 copy-done.7
  30.7 0.0 copy-done.8
  30.7 0.0 copy-done.2
  30.7 0.0 copy-done.6
  30.7 0.0 copy-done.9
  30.7 0.0 copy-done.5
  30.8 0.0 copy-start.3
  30.8 1.0 %copy-done.3 = bf16[1,1024,256]{2,1,0:T(8,128)(2,1)S(1)} copy-done((bf16[1,1024,256]{2,1,0:T(8,128)(2,1)S(1)}, bf16[1,1024,256]{2,1,0:T(8,128)(2,1)}, u32[]{:S(2)}) %copy-start.3) | copy-done | bytes 524312
  31.8 1.5 %shard_map.185.state = bf16[8,8960]{1,0:T(8,128)(2,1)S(1)} custom-call(bf16[1,2,4,2,1536]{4,3,2,1,0:T(2,128)(2,1)S(1)} %copy-done.4, bf16[1,2,4,2,256]{4,3,2,1,0:T(2,128)(2,1)S(1)} %copy-done.6, bf16[1,1024,256]{2,1,0:T(8,128)(2,1)S(1)} %copy-done.3, bf16[1,4,64,256]{3,2,1,0:T(8,128)(2,1)S(1)} %copy-done.2, s32[1,64]{1,0:T(1,128)S(1)} %copy-done.8, ...), custom_call_target="tpu_custom_call" | custom-call | flops 100000000 | bytes 1000000 | tf_op jit(solution)/shard_map/pallas_call | solution.py:19
  33.3 3.5 %all-to-all-done.arr_ref = bf16[64,40,128]{2,1,0:T(8,128)(2,1)S(1)} async-done(((bf16[64,40,128]{2,1,0:T(8,128)(2,1)}), bf16[64,40,128]{2,1,0:T(8,128)(2,1)S(1)}, u32[]{:S(2)}, u32[]{:S(2)}) %all-to-all-start) | async-done | bytes 655392 | tf_op jit(solution)/shard_map/all_to_all | solution.py:313
  36.8 0.0 collective-permute-done.3.refs_3_
  36.8 0.0 collective-permute-done.1.refs_1_
  36.8 0.0 copy-done.1
  36.8 2.5 %shard_map.186 = (bf16[16,1536]{1,0:T(8,128)(2,1)S(1)}, bf16[16,1536]{1,0:T(8,128)(2,1)S(1)}) custom-call(bf16[2560,128]{1,0:T(8,128)(2,1)S(1)} %bitcast.4, bf16[8,8960]{1,0:T(8,128)(2,1)S(1)} %shard_map.185.state, f32[1,1536]{1,0:T(1,128)S(1)} %broadcast_in_dim.9.norm_ref, bf16[384,1536]{1,0:T(8,128)(2,1)S(1)} %copy-done.1, bf16[384,1536]{1,0:T(8,128)(2,1)} %copy-done.10, ...), custom_call_target="tpu_custom_call" | custom-call | flops 200000000 | bytes 6000000 | tf_op jit(solution)/shard_map/pallas_call | solution.py:19
  39.3 0.0 copy-start
  39.3 1.4 %collective-permute-start.6 = (bf16[16,1536]{1,0:T(8,128)(2,1)S(1)}, bf16[16,1536]{1,0:T(8,128)(2,1)S(1)}, u32[]{:S(2)}, u32[]{:S(2)}) collective-permute-start(bf16[16,1536]{1,0:T(8,128)(2,1)S(1)} %get-tuple-element.18.x0), channel_id=1, source_target_pairs={{0,3},{1,0},{2,1},{3,2},{4,7},{5,4},{6,5},{7,6},{8,11},{9,8},{10,9... | collective-permute-start | bytes 147464 | tf_op jit(solution)/shard_map/ppermute | solution.py:293
  40.7 1.8 %collective-permute-start.5 = (bf16[16,1536]{1,0:T(8,128)(2,1)S(1)}, bf16[16,1536]{1,0:T(8,128)(2,1)S(1)}, u32[]{:S(2)}, u32[]{:S(2)}) collective-permute-start(bf16[16,1536]{1,0:T(8,128)(2,1)S(1)} %get-tuple-element.18.x0), channel_id=1, source_target_pairs={{0,2},{1,3},{2,0},{3,1},{4,6},{5,7},{6,4},{7,5},{8,10},{9,11},{10,... | collective-permute-start | bytes 147464 | tf_op jit(solution)/shard_map/ppermute | solution.py:293
  42.6 0.6 %collective-permute-start.4 = (bf16[16,1536]{1,0:T(8,128)(2,1)S(1)}, bf16[16,1536]{1,0:T(8,128)(2,1)S(1)}, u32[]{:S(2)}, u32[]{:S(2)}) collective-permute-start(bf16[16,1536]{1,0:T(8,128)(2,1)S(1)} %get-tuple-element.18.x0), channel_id=1, source_target_pairs={{0,1},{1,2},{2,3},{3,0},{4,5},{5,6},{6,7},{7,4},{8,9},{9,10},{10,1... | collective-permute-start | bytes 147464 | tf_op jit(solution)/shard_map/ppermute | solution.py:293
  43.1 3.1 %shard_map.187 = (bf16[1536,1152]{1,0:T(8,128)(2,1)S(1)}, bf16[1152,1536]{1,0:T(8,128)(2,1)S(1)}) custom-call(bf16[1536,1152]{1,0:T(8,128)(2,1)} %refs_0_, bf16[1152,1536]{1,0:T(8,128)(2,1)} %refs_1_), custom_call_target="tpu_custom_call" | custom-call | bytes 14000000 | tf_op jit(solution)/shard_map/pallas_call | solution.py:19
  46.2 0.0 collective-permute-done.6.x3
  46.3 0.2 collective-permute-done.5.x2
  46.4 1.4 %collective-permute-done.4.x1 = bf16[16,1536]{1,0:T(8,128)(2,1)S(1)} collective-permute-done((bf16[16,1536]{1,0:T(8,128)(2,1)S(1)}, bf16[16,1536]{1,0:T(8,128)(2,1)S(1)}, u32[]{:S(2)}, u32[]{:S(2)}) %collective-permute-start.4) | collective-permute-done | bytes 49184 | tf_op jit(solution)/shard_map/ppermute | solution.py:293
  47.9 0.0 copy-done
  47.9 0.0 copy-start.12
  47.9 0.0 copy-start.13
  47.9 2.0 %shard_map.188 = (f32[16,1536]{1,0:T(8,128)S(1)}, bf16[16,1536]{1,0:T(8,128)(2,1)S(1)}, bf16[16,1536]{1,0:T(8,128)(2,1)S(1)}, bf16[16,1536]{1,0:T(8,128)(2,1)S(1)}) custom-call(bf16[16,1536]{1,0:T(8,128)(2,1)S(1)} %get-tuple-element.18.x0, bf16[16,1536]{1,0:T(8,128)(2,1)S(1)} %collective-permute-done.4.x1, bf16[16,1536]{1,0:T(8,128)(2,1)S(1)} %collective-permute-done.5.x2, ...), custom_call_target="tpu_custom_call" | custom-call | flops 700000000 | bytes 1000000 | tf_op jit(solution)/shard_map/pallas_call | solution.py:19
  49.8 1.2 %collective-permute-start.7 = (bf16[16,1536]{1,0:T(8,128)(2,1)S(1)}, bf16[16,1536]{1,0:T(8,128)(2,1)S(1)}, u32[]{:S(2)}, u32[]{:S(2)}) collective-permute-start(bf16[16,1536]{1,0:T(8,128)(2,1)S(1)} %get-tuple-element.24), channel_id=1, source_target_pairs={{0,3},{1,0},{2,1},{3,2},{4,7},{5,4},{6,5},{7,6},{8,11},{9,8},{10,9... | collective-permute-start | bytes 147464 | tf_op jit(solution)/shard_map/ppermute | solution.py:293
  51.0 0.5 collective-permute-start.8
  51.5 0.7 %collective-permute-start.9 = (bf16[16,1536]{1,0:T(8,128)(2,1)S(1)}, bf16[16,1536]{1,0:T(8,128)(2,1)S(1)}, u32[]{:S(2)}, u32[]{:S(2)}) collective-permute-start(bf16[16,1536]{1,0:T(8,128)(2,1)S(1)} %get-tuple-element.26), channel_id=1, source_target_pairs={{0,1},{1,2},{2,3},{3,0},{4,5},{5,6},{6,7},{7,4},{8,9},{9,10},{10,1... | collective-permute-start | bytes 147464 | tf_op jit(solution)/shard_map/ppermute | solution.py:293
  52.2 0.0 copy-done.12
  52.2 0.0 copy-done.13
  52.3 1.4 %shard_map.190 = bf16[1,2,4,64,256]{4,3,2,1,0:T(8,128)(2,1)} custom-call(bf16[64,40,128]{2,1,0:T(8,128)(2,1)S(1)} %all-to-all-done.arr_ref, bf16[1,4,64,256]{3,2,1,0:T(8,128)(2,1)S(1)} %copy-done.2, bf16[1,2,4,2,256]{4,3,2,1,0:T(2,128)(2,1)S(1)} %copy-done.6, s32[1,64]{1,0:T(1,128)S(1)} %copy-done.8, s32[1,2,4]{2,1,0:T(2,128)S(1)} %copy-done.7), custom_call_target="tpu_custom_call" | custom-call | flops 1000000 | bytes 1500000 | tf_op jit(solution)/shard_map/pallas_call | solution.py:19
  53.6 0.4 collective-permute-done.7.y1
  54.0 2.6 %collective-permute-done.8.y2 = bf16[16,1536]{1,0:T(8,128)(2,1)S(1)} collective-permute-done((bf16[16,1536]{1,0:T(8,128)(2,1)S(1)}, bf16[16,1536]{1,0:T(8,128)(2,1)S(1)}, u32[]{:S(2)}, u32[]{:S(2)}) %collective-permute-start.8) | collective-permute-done | bytes 49184 | tf_op jit(solution)/shard_map/ppermute | solution.py:293
  56.6 0.5 collective-permute-done.9.y3
  57.1 0.8 %shard_map.189 = (f32[1,2,2,4]{3,2,1,0:T(2,128)}, bf16[1,2,4,2,1536]{4,3,2,1,0:T(2,128)(2,1)}) custom-call(bf16[16,1536]{1,0:T(8,128)(2,1)S(1)} %get-tuple-element.17.h1_ref, f32[16,1536]{1,0:T(8,128)S(1)} %get-tuple-element.23.y0, bf16[16,1536]{1,0:T(8,128)(2,1)S(1)} %collective-permute-done.7.y1, bf16[16,1536]{1,0:T(8,128)(2,1)S(1)} %collective-permute-done.8.y2, ...), custom_call_target="tpu_custom_call" | custom-call | flops 1000000 | bytes 500000 | tf_op jit(solution)/shard_map/pallas_call | solution.py:19
  (4 shorter events, 0.1 us)
Async XLA Ops:
  0.6 36.2 %copy-start.1 = (bf16[384,1536]{1,0:T(8,128)(2,1)S(1)}, bf16[384,1536]{1,0:T(8,128)(2,1)}, u32[]{:S(2)}) copy-start(bf16[384,1536]{1,0:T(8,128)(2,1)} %wown.1) | copy-start | bytes 3538948
  0.6 30.0 %copy-start.11 = (f32[1536]{0:T(1024)S(1)}, f32[1536]{0:T(1024)}, u32[]{:S(2)}) copy-start(f32[1536]{0:T(1024)} %param.28) | copy-start | bytes 18436
  0.7 30.0 %copy-start.4 = (bf16[1,2,4,2,1536]{4,3,2,1,0:T(2,128)(2,1)S(1)}, bf16[1,2,4,2,1536]{4,3,2,1,0:T(2,128)(2,1)}, u32[]{:S(2)}) copy-start(bf16[1,2,4,2,1536]{4,3,2,1,0:T(2,128)(2,1)} %q_ref) | copy-start | bytes 147460
  0.7 30.0 %copy-start.7 = (s32[1,2,4]{2,1,0:T(2,128)S(1)}, s32[1,2,4]{2,1,0:T(2,128)}, u32[]{:S(2)}) copy-start(s32[1,2,4]{2,1,0:T(2,128)} %tlen_ref.3) | copy-start | bytes 100
  0.7 30.0 %copy-start.8 = (s32[1,64]{1,0:T(1,128)S(1)}, s32[1,64]{1,0:T(1,128)}, u32[]{:S(2)}) copy-start(s32[1,64]{1,0:T(1,128)} %holder_ref.3) | copy-start | bytes 772
  0.7 30.0 %copy-start.2 = (bf16[1,4,64,256]{3,2,1,0:T(8,128)(2,1)S(1)}, bf16[1,4,64,256]{3,2,1,0:T(8,128)(2,1)}, u32[]{:S(2)}) copy-start(bf16[1,4,64,256]{3,2,1,0:T(8,128)(2,1)} %tails_ref.3) | copy-start | bytes 393220
  0.7 30.0 %copy-start.6 = (bf16[1,2,4,2,256]{4,3,2,1,0:T(2,128)(2,1)S(1)}, bf16[1,2,4,2,256]{4,3,2,1,0:T(2,128)(2,1)}, u32[]{:S(2)}) copy-start(bf16[1,2,4,2,256]{4,3,2,1,0:T(2,128)(2,1)} %new_ref.3) | copy-start | bytes 24580
  0.7 30.0 %copy-start.9 = (s32[1,2]{1,0:T(1,128)S(1)}, s32[1,2]{1,0:T(1,128)}, u32[]{:S(2)}) copy-start(s32[1,2]{1,0:T(1,128)} %plen_ref.1) | copy-start | bytes 28
  0.7 30.0 %copy-start.5 = (bf16[1,2,4,2,1536]{4,3,2,1,0:T(2,128)(2,1)S(1)}, bf16[1,2,4,2,1536]{4,3,2,1,0:T(2,128)(2,1)}, u32[]{:S(2)}) copy-start(bf16[1,2,4,2,1536]{4,3,2,1,0:T(2,128)(2,1)} %res_ref.1) | copy-start | bytes 147460
  0.7 17.7 %collective-permute-start = (bf16[384,1536]{1,0:T(8,128)(2,1)}, bf16[384,1536]{1,0:T(8,128)(2,1)S(1)}, u32[]{:S(2)}, u32[]{:S(2)}) collective-permute-start(bf16[384,1536]{1,0:T(8,128)(2,1)} %wown.1), channel_id=1, source_target_pairs={{0,1},{1,2},{2,3},{3,0},{4,7},{5,4},{6,5},{7,6},{8,9},{9,10},{10,1... | collective-permute-start | bytes 3538952 | tf_op jit(solution)/shard_map/ppermute | solution.py:300
  4.7 32.1 %all-to-all-start = ((bf16[64,40,128]{2,1,0:T(8,128)(2,1)}), bf16[64,40,128]{2,1,0:T(8,128)(2,1)S(1)}, u32[]{:S(2)}, u32[]{:S(2)}) async-start(bf16[64,40,128]{2,1,0:T(8,128)(2,1)} %bitcast.5), calls=%async_computation | async-start | bytes 1310720 | tf_op jit(solution)/shard_map/all_to_all | solution.py:313
  18.4 1.0 %copy-start.10 = (bf16[384,1536]{1,0:T(8,128)(2,1)}, bf16[384,1536]{1,0:T(8,128)(2,1)S(1)}, u32[]{:S(2)}) copy-start(bf16[384,1536]{1,0:T(8,128)(2,1)S(1)} %collective-permute-done.refs_0_) | copy-start | bytes 3538948
  19.5 11.2 %collective-permute-start.2 = (bf16[192,1536]{1,0:T(8,128)(2,1)S(1)}, bf16[192,1536]{1,0:T(8,128)(2,1)S(1)}, u32[]{:S(2)}, u32[]{:S(2)}) collective-permute-start(bf16[192,1536]{1,0:T(8,128)(2,1)S(1)} %constant_dynamic-slice_fusion), channel_id=1, source_target_pairs={{0,1},{1,2},{2,3},{3,0},{4,7},{5,4},{6,5},{7,6},{8,9},{9,10},{10,1... | collective-permute-start | bytes 1769480 | tf_op jit(solution)/shard_map/ppermute | solution.py:300
  19.9 17.0 %collective-permute-start.1 = (bf16[384,1536]{1,0:T(8,128)(2,1)}, bf16[384,1536]{1,0:T(8,128)(2,1)}, u32[]{:S(2)}, u32[]{:S(2)}) collective-permute-start(bf16[384,1536]{1,0:T(8,128)(2,1)} %copy-done.10), channel_id=1, source_target_pairs={{0,4},{4,0},{8,12},{12,8},{16,20},{20,16},{24,28},{28,24},{32,36},... | collective-permute-start | bytes 3538952 | tf_op jit(solution)/shard_map/ppermute | solution.py:296
  30.7 6.2 %collective-permute-start.3 = (bf16[192,1536]{1,0:T(8,128)(2,1)S(1)}, bf16[192,1536]{1,0:T(8,128)(2,1)S(1)}, u32[]{:S(2)}, u32[]{:S(2)}) collective-permute-start(bf16[192,1536]{1,0:T(8,128)(2,1)S(1)} %collective-permute-done.2.refs_2_), channel_id=1, source_target_pairs={{0,4},{4,0},{8,12},{12,8},{16,20},{20,16},{24,28},{28,24},{32,36},... | collective-permute-start | bytes 1769480 | tf_op jit(solution)/shard_map/ppermute | solution.py:296
  30.8 1.0 %copy-start.3 = (bf16[1,1024,256]{2,1,0:T(8,128)(2,1)S(1)}, bf16[1,1024,256]{2,1,0:T(8,128)(2,1)}, u32[]{:S(2)}) copy-start(bf16[1,1024,256]{2,1,0:T(8,128)(2,1)} %kv_ref.1) | copy-start | bytes 1572868
  39.3 8.5 %copy-start = (bf16[1536,1152]{1,0:T(8,128)(2,1)S(1)}, bf16[1536,1152]{1,0:T(8,128)(2,1)}, u32[]{:S(2)}) copy-start(bf16[1536,1152]{1,0:T(8,128)(2,1)} %wg.1) | copy-start | bytes 10616836
  39.3 6.9 %collective-permute-start.6 = (bf16[16,1536]{1,0:T(8,128)(2,1)S(1)}, bf16[16,1536]{1,0:T(8,128)(2,1)S(1)}, u32[]{:S(2)}, u32[]{:S(2)}) collective-permute-start(bf16[16,1536]{1,0:T(8,128)(2,1)S(1)} %get-tuple-element.18.x0), channel_id=1, source_target_pairs={{0,3},{1,0},{2,1},{3,2},{4,7},{5,4},{6,5},{7,6},{8,11},{9,8},{10,9... | collective-permute-start | bytes 147464 | tf_op jit(solution)/shard_map/ppermute | solution.py:293
  40.7 5.7 %collective-permute-start.5 = (bf16[16,1536]{1,0:T(8,128)(2,1)S(1)}, bf16[16,1536]{1,0:T(8,128)(2,1)S(1)}, u32[]{:S(2)}, u32[]{:S(2)}) collective-permute-start(bf16[16,1536]{1,0:T(8,128)(2,1)S(1)} %get-tuple-element.18.x0), channel_id=1, source_target_pairs={{0,2},{1,3},{2,0},{3,1},{4,6},{5,7},{6,4},{7,5},{8,10},{9,11},{10,... | collective-permute-start | bytes 147464 | tf_op jit(solution)/shard_map/ppermute | solution.py:293
  42.6 5.3 %collective-permute-start.4 = (bf16[16,1536]{1,0:T(8,128)(2,1)S(1)}, bf16[16,1536]{1,0:T(8,128)(2,1)S(1)}, u32[]{:S(2)}, u32[]{:S(2)}) collective-permute-start(bf16[16,1536]{1,0:T(8,128)(2,1)S(1)} %get-tuple-element.18.x0), channel_id=1, source_target_pairs={{0,1},{1,2},{2,3},{3,0},{4,5},{5,6},{6,7},{7,4},{8,9},{9,10},{10,1... | collective-permute-start | bytes 147464 | tf_op jit(solution)/shard_map/ppermute | solution.py:293
  47.9 4.4 %copy-start.12 = (f32[1536]{0:T(1024)S(1)}, f32[1536]{0:T(1024)}, u32[]{:S(2)}) copy-start(f32[1536]{0:T(1024)} %param.32) | copy-start | bytes 18436
  47.9 4.4 %copy-start.13 = (f32[1536]{0:T(1024)S(1)}, f32[1536]{0:T(1024)}, u32[]{:S(2)}) copy-start(f32[1536]{0:T(1024)} %param.33) | copy-start | bytes 18436
  49.8 4.2 %collective-permute-start.7 = (bf16[16,1536]{1,0:T(8,128)(2,1)S(1)}, bf16[16,1536]{1,0:T(8,128)(2,1)S(1)}, u32[]{:S(2)}, u32[]{:S(2)}) collective-permute-start(bf16[16,1536]{1,0:T(8,128)(2,1)S(1)} %get-tuple-element.24), channel_id=1, source_target_pairs={{0,3},{1,0},{2,1},{3,2},{4,7},{5,4},{6,5},{7,6},{8,11},{9,8},{10,9... | collective-permute-start | bytes 147464 | tf_op jit(solution)/shard_map/ppermute | solution.py:293
  51.0 5.6 %collective-permute-start.8 = (bf16[16,1536]{1,0:T(8,128)(2,1)S(1)}, bf16[16,1536]{1,0:T(8,128)(2,1)S(1)}, u32[]{:S(2)}, u32[]{:S(2)}) collective-permute-start(bf16[16,1536]{1,0:T(8,128)(2,1)S(1)} %get-tuple-element.25), channel_id=1, source_target_pairs={{0,2},{1,3},{2,0},{3,1},{4,6},{5,7},{6,4},{7,5},{8,10},{9,11},{10,... | collective-permute-start | bytes 147464 | tf_op jit(solution)/shard_map/ppermute | solution.py:293
  51.5 5.6 %collective-permute-start.9 = (bf16[16,1536]{1,0:T(8,128)(2,1)S(1)}, bf16[16,1536]{1,0:T(8,128)(2,1)S(1)}, u32[]{:S(2)}, u32[]{:S(2)}) collective-permute-start(bf16[16,1536]{1,0:T(8,128)(2,1)S(1)} %get-tuple-element.26), channel_id=1, source_target_pairs={{0,1},{1,2},{2,3},{3,0},{4,5},{5,6},{6,7},{7,4},{8,9},{9,10},{10,1... | collective-permute-start | bytes 147464 | tf_op jit(solution)/shard_map/ppermute | solution.py:293

commit v5 on v4

--- a/solution.py
+++ b/solution.py
@@ -1,4 +1,5 @@
 import functools
+import math
 
 import jax
 import jax.numpy as jnp
@@ -81,7 +82,7 @@
 
 
 def attend(qh, segments, rows, size):
-    scale = 1.0 / jnp.sqrt(F32(size))
+    scale = F32(math.log2(math.e) / math.sqrt(size))
     heads = qh.shape[0] // rows
     scored = []
     top = None
@@ -96,7 +97,7 @@
     total = None
     acc = None
     for s, (_, values, _, shift) in zip(scored, segments):
-        e = jnp.exp(s - top)
+        e = jnp.exp2(s - top)
         t = e.sum(axis=1, keepdims=True)
         if shift:
             e = pltpu.roll(e, shift, axis=1)

time: 58.2 us -> 58.2 us (level)
  no operation moved by 1% of the time
where the time goes in v5:
time: 58.2 us; the launch traced here: 57.9 us
  starting transfers between devices  21.2 us (36%)
  waiting for transfers between devices  20 us (34%)
  Pallas kernels  13.7 us (24%)
  local copies, waits for them, and re-layouts  2.17 us (4%)
  between operations  0.88 us (2%)
    pallas_call x7, Pallas kernels, call(): pl.pallas_call(body, out_shape=outs, in_specs=specs, out_specs=jax.tree.m...  13.7 us
    all_to_all x1, starting transfers between devices, on_device(): lax.all_to_all(outgoing.reshape(n_req, 2 * page, size), 'req', split_axis...  12.2 us
    ppermute x2, waiting for transfers between devices, onward(): return lax.ppermute(x, ('req', 'mlp'), to)  11.4 us
    ppermute x6, starting transfers between devices, shift(): return lax.ppermute(x, 'mlp', [(i, (i + k) % n_mlp) for i in range(n_mlp)])  6.19 us
    ppermute x6, waiting for transfers between devices, shift(): return lax.ppermute(x, 'mlp', [(i, (i + k) % n_mlp) for i in range(n_mlp)])  5.09 us
    all_to_all x1, waiting for transfers between devices, on_device(): lax.all_to_all(outgoing.reshape(n_req, 2 * page, size), 'req', split_axis...  3.5 us
    unnamed x28, local copies, waits for them, and re-layouts  2.11 us
    ppermute x2, starting transfers between devices, onward(): return lax.ppermute(x, ('req', 'mlp'), to)  1.93 us
  transfers between devices with their start and end apart: 11, of which 8 were waited for; matrix products, arithmetic and copies ran while one was open for 0% of the time, Pallas kernels for 15%

profile of v5, /device:TPU:32, one launch (start us, length us, event | category | flops | bytes accessed | tf_op | source)
XLA Modules:
  0.0 57.9 jit_solution(1680434995033688386)
XLA Ops:
  0.6 0.0 copy-start.1
  0.6 0.0 copy-start.11
  0.7 0.0 copy-start.4
  0.7 0.0 copy-start.7
  0.7 0.0 copy-start.8
  0.7 0.0 copy-start.2
  0.7 0.0 copy-start.6
  0.7 0.0 copy-start.9
  0.7 0.0 copy-start.5
  0.7 1.6 %collective-permute-start = (bf16[384,1536]{1,0:T(8,128)(2,1)}, bf16[384,1536]{1,0:T(8,128)(2,1)S(1)}, u32[]{:S(2)}, u32[]{:S(2)}) collective-permute-start(bf16[384,1536]{1,0:T(8,128)(2,1)} %wown.1), channel_id=1, source_target_pairs={{0,1},{1,2},{2,3},{3,0},{4,7},{5,4},{6,5},{7,6},{8,9},{9,10},{10,1... | collective-permute-start | bytes 3538952 | tf_op jit(solution)/shard_map/ppermute | solution.py:301
  2.3 2.4 %shard_map.184 = bf16[2560,128]{1,0:T(8,128)(2,1)} custom-call(bf16[20,64,256]{2,1,0:T(8,128)(2,1)} %bitcast.6, s32[1,64]{1,0:T(1,128)} %slot_ref.1), custom_call_target="tpu_custom_call" | custom-call | flops 100000000 | bytes 1400000 | tf_op jit(solution)/shard_map/pallas_call | solution.py:20
  4.7 12.2 %all-to-all-start = ((bf16[64,40,128]{2,1,0:T(8,128)(2,1)}), bf16[64,40,128]{2,1,0:T(8,128)(2,1)S(1)}, u32[]{:S(2)}, u32[]{:S(2)}) async-start(bf16[64,40,128]{2,1,0:T(8,128)(2,1)} %bitcast.5), calls=%async_computation | async-start | bytes 1310720 | tf_op jit(solution)/shard_map/all_to_all | solution.py:314
  16.9 1.5 %collective-permute-done.refs_0_ = bf16[384,1536]{1,0:T(8,128)(2,1)S(1)} collective-permute-done((bf16[384,1536]{1,0:T(8,128)(2,1)}, bf16[384,1536]{1,0:T(8,128)(2,1)S(1)}, u32[]{:S(2)}, u32[]{:S(2)}) %collective-permute-start) | collective-permute-done | bytes 1179680 | tf_op jit(solution)/shard_map/ppermute | solution.py:301
  18.4 0.0 copy-start.10
  18.4 1.0 %copy-done.10 = bf16[384,1536]{1,0:T(8,128)(2,1)} copy-done((bf16[384,1536]{1,0:T(8,128)(2,1)}, bf16[384,1536]{1,0:T(8,128)(2,1)S(1)}, u32[]{:S(2)}) %copy-start.10) | copy-done | bytes 1179672
  19.5 0.4 collective-permute-start.2
  19.9 0.9 %collective-permute-start.1 = (bf16[384,1536]{1,0:T(8,128)(2,1)}, bf16[384,1536]{1,0:T(8,128)(2,1)}, u32[]{:S(2)}, u32[]{:S(2)}) collective-permute-start(bf16[384,1536]{1,0:T(8,128)(2,1)} %copy-done.10), channel_id=1, source_target_pairs={{0,4},{4,0},{8,12},{12,8},{16,20},{20,16},{24,28},{28,24},{32,36},... | collective-permute-start | bytes 3538952 | tf_op jit(solution)/shard_map/ppermute | solution.py:297
  20.7 9.9 %collective-permute-done.2.refs_2_ = bf16[192,1536]{1,0:T(8,128)(2,1)S(1)} collective-permute-done((bf16[192,1536]{1,0:T(8,128)(2,1)S(1)}, bf16[192,1536]{1,0:T(8,128)(2,1)S(1)}, u32[]{:S(2)}, u32[]{:S(2)}) %collective-permute-start.2) | collective-permute-done | bytes 589856 | tf_op jit(solution)/shard_map/ppermute | solution.py:301
  30.7 0.0 collective-permute-start.3
  30.7 0.0 copy-done.11
  30.7 0.0 copy-done.4
  30.7 0.0 copy-done.7
  30.7 0.0 copy-done.8
  30.7 0.0 copy-done.2
  30.7 0.0 copy-done.6
  30.7 0.0 copy-done.9
  30.7 0.0 copy-done.5
  30.8 0.0 copy-start.3
  30.8 1.0 %copy-done.3 = bf16[1,1024,256]{2,1,0:T(8,128)(2,1)S(1)} copy-done((bf16[1,1024,256]{2,1,0:T(8,128)(2,1)S(1)}, bf16[1,1024,256]{2,1,0:T(8,128)(2,1)}, u32[]{:S(2)}) %copy-start.3) | copy-done | bytes 524312
  31.8 1.5 %shard_map.185.state = bf16[8,8960]{1,0:T(8,128)(2,1)S(1)} custom-call(bf16[1,2,4,2,1536]{4,3,2,1,0:T(2,128)(2,1)S(1)} %copy-done.4, bf16[1,2,4,2,256]{4,3,2,1,0:T(2,128)(2,1)S(1)} %copy-done.6, bf16[1,1024,256]{2,1,0:T(8,128)(2,1)S(1)} %copy-done.3, bf16[1,4,64,256]{3,2,1,0:T(8,128)(2,1)S(1)} %copy-done.2, s32[1,64]{1,0:T(1,128)S(1)} %copy-done.8, ...), custom_call_target="tpu_custom_call" | custom-call | flops 100000000 | bytes 1000000 | tf_op jit(solution)/shard_map/pallas_call | solution.py:20
  33.3 3.5 %all-to-all-done.arr_ref = bf16[64,40,128]{2,1,0:T(8,128)(2,1)S(1)} async-done(((bf16[64,40,128]{2,1,0:T(8,128)(2,1)}), bf16[64,40,128]{2,1,0:T(8,128)(2,1)S(1)}, u32[]{:S(2)}, u32[]{:S(2)}) %all-to-all-start) | async-done | bytes 655392 | tf_op jit(solution)/shard_map/all_to_all | solution.py:314
  36.8 0.0 collective-permute-done.3.refs_3_
  36.8 0.0 collective-permute-done.1.refs_1_
  36.8 0.0 copy-done.1
  36.8 2.5 %shard_map.186 = (bf16[16,1536]{1,0:T(8,128)(2,1)S(1)}, bf16[16,1536]{1,0:T(8,128)(2,1)S(1)}) custom-call(bf16[2560,128]{1,0:T(8,128)(2,1)S(1)} %bitcast.4, bf16[8,8960]{1,0:T(8,128)(2,1)S(1)} %shard_map.185.state, f32[1,1536]{1,0:T(1,128)S(1)} %broadcast_in_dim.9.norm_ref, bf16[384,1536]{1,0:T(8,128)(2,1)S(1)} %copy-done.1, bf16[384,1536]{1,0:T(8,128)(2,1)} %copy-done.10, ...), custom_call_target="tpu_custom_call" | custom-call | flops 200000000 | bytes 6000000 | tf_op jit(solution)/shard_map/pallas_call | solution.py:20
  39.3 0.0 copy-start
  39.3 1.4 %collective-permute-start.6 = (bf16[16,1536]{1,0:T(8,128)(2,1)S(1)}, bf16[16,1536]{1,0:T(8,128)(2,1)S(1)}, u32[]{:S(2)}, u32[]{:S(2)}) collective-permute-start(bf16[16,1536]{1,0:T(8,128)(2,1)S(1)} %get-tuple-element.18.x0), channel_id=1, source_target_pairs={{0,3},{1,0},{2,1},{3,2},{4,7},{5,4},{6,5},{7,6},{8,11},{9,8},{10,9... | collective-permute-start | bytes 147464 | tf_op jit(solution)/shard_map/ppermute | solution.py:294
  40.7 1.8 %collective-permute-start.5 = (bf16[16,1536]{1,0:T(8,128)(2,1)S(1)}, bf16[16,1536]{1,0:T(8,128)(2,1)S(1)}, u32[]{:S(2)}, u32[]{:S(2)}) collective-permute-start(bf16[16,1536]{1,0:T(8,128)(2,1)S(1)} %get-tuple-element.18.x0), channel_id=1, source_target_pairs={{0,2},{1,3},{2,0},{3,1},{4,6},{5,7},{6,4},{7,5},{8,10},{9,11},{10,... | collective-permute-start | bytes 147464 | tf_op jit(solution)/shard_map/ppermute | solution.py:294
  42.6 0.6 %collective-permute-start.4 = (bf16[16,1536]{1,0:T(8,128)(2,1)S(1)}, bf16[16,1536]{1,0:T(8,128)(2,1)S(1)}, u32[]{:S(2)}, u32[]{:S(2)}) collective-permute-start(bf16[16,1536]{1,0:T(8,128)(2,1)S(1)} %get-tuple-element.18.x0), channel_id=1, source_target_pairs={{0,1},{1,2},{2,3},{3,0},{4,5},{5,6},{6,7},{7,4},{8,9},{9,10},{10,1... | collective-permute-start | bytes 147464 | tf_op jit(solution)/shard_map/ppermute | solution.py:294
  43.1 3.1 %shard_map.187 = (bf16[1536,1152]{1,0:T(8,128)(2,1)S(1)}, bf16[1152,1536]{1,0:T(8,128)(2,1)S(1)}) custom-call(bf16[1536,1152]{1,0:T(8,128)(2,1)} %refs_0_, bf16[1152,1536]{1,0:T(8,128)(2,1)} %refs_1_), custom_call_target="tpu_custom_call" | custom-call | bytes 14000000 | tf_op jit(solution)/shard_map/pallas_call | solution.py:20
  46.2 0.0 collective-permute-done.6.x3
  46.3 0.2 collective-permute-done.5.x2
  46.4 1.4 %collective-permute-done.4.x1 = bf16[16,1536]{1,0:T(8,128)(2,1)S(1)} collective-permute-done((bf16[16,1536]{1,0:T(8,128)(2,1)S(1)}, bf16[16,1536]{1,0:T(8,128)(2,1)S(1)}, u32[]{:S(2)}, u32[]{:S(2)}) %collective-permute-start.4) | collective-permute-done | bytes 49184 | tf_op jit(solution)/shard_map/ppermute | solution.py:294
  47.9 0.0 copy-done
  47.9 0.0 copy-start.12
  47.9 0.0 copy-start.13
  47.9 2.0 %shard_map.188 = (f32[16,1536]{1,0:T(8,128)S(1)}, bf16[16,1536]{1,0:T(8,128)(2,1)S(1)}, bf16[16,1536]{1,0:T(8,128)(2,1)S(1)}, bf16[16,1536]{1,0:T(8,128)(2,1)S(1)}) custom-call(bf16[16,1536]{1,0:T(8,128)(2,1)S(1)} %get-tuple-element.18.x0, bf16[16,1536]{1,0:T(8,128)(2,1)S(1)} %collective-permute-done.4.x1, bf16[16,1536]{1,0:T(8,128)(2,1)S(1)} %collective-permute-done.5.x2, ...), custom_call_target="tpu_custom_call" | custom-call | flops 700000000 | bytes 1000000 | tf_op jit(solution)/shard_map/pallas_call | solution.py:20
  49.8 1.2 %collective-permute-start.7 = (bf16[16,1536]{1,0:T(8,128)(2,1)S(1)}, bf16[16,1536]{1,0:T(8,128)(2,1)S(1)}, u32[]{:S(2)}, u32[]{:S(2)}) collective-permute-start(bf16[16,1536]{1,0:T(8,128)(2,1)S(1)} %get-tuple-element.24), channel_id=1, source_target_pairs={{0,3},{1,0},{2,1},{3,2},{4,7},{5,4},{6,5},{7,6},{8,11},{9,8},{10,9... | collective-permute-start | bytes 147464 | tf_op jit(solution)/shard_map/ppermute | solution.py:294
  51.0 0.5 collective-permute-start.8
  51.5 0.7 %collective-permute-start.9 = (bf16[16,1536]{1,0:T(8,128)(2,1)S(1)}, bf16[16,1536]{1,0:T(8,128)(2,1)S(1)}, u32[]{:S(2)}, u32[]{:S(2)}) collective-permute-start(bf16[16,1536]{1,0:T(8,128)(2,1)S(1)} %get-tuple-element.26), channel_id=1, source_target_pairs={{0,1},{1,2},{2,3},{3,0},{4,5},{5,6},{6,7},{7,4},{8,9},{9,10},{10,1... | collective-permute-start | bytes 147464 | tf_op jit(solution)/shard_map/ppermute | solution.py:294
  52.2 0.0 copy-done.12
  52.2 0.0 copy-done.13
  52.3 1.4 %shard_map.190 = bf16[1,2,4,64,256]{4,3,2,1,0:T(8,128)(2,1)} custom-call(bf16[64,40,128]{2,1,0:T(8,128)(2,1)S(1)} %all-to-all-done.arr_ref, bf16[1,4,64,256]{3,2,1,0:T(8,128)(2,1)S(1)} %copy-done.2, bf16[1,2,4,2,256]{4,3,2,1,0:T(2,128)(2,1)S(1)} %copy-done.6, s32[1,64]{1,0:T(1,128)S(1)} %copy-done.8, s32[1,2,4]{2,1,0:T(2,128)S(1)} %copy-done.7), custom_call_target="tpu_custom_call" | custom-call | flops 1000000 | bytes 1500000 | tf_op jit(solution)/shard_map/pallas_call | solution.py:20
  53.6 0.4 collective-permute-done.7.y1
  54.0 2.6 %collective-permute-done.8.y2 = bf16[16,1536]{1,0:T(8,128)(2,1)S(1)} collective-permute-done((bf16[16,1536]{1,0:T(8,128)(2,1)S(1)}, bf16[16,1536]{1,0:T(8,128)(2,1)S(1)}, u32[]{:S(2)}, u32[]{:S(2)}) %collective-permute-start.8) | collective-permute-done | bytes 49184 | tf_op jit(solution)/shard_map/ppermute | solution.py:294
  56.6 0.5 collective-permute-done.9.y3
  57.1 0.8 %shard_map.189 = (f32[1,2,2,4]{3,2,1,0:T(2,128)}, bf16[1,2,4,2,1536]{4,3,2,1,0:T(2,128)(2,1)}) custom-call(bf16[16,1536]{1,0:T(8,128)(2,1)S(1)} %get-tuple-element.17.h1_ref, f32[16,1536]{1,0:T(8,128)S(1)} %get-tuple-element.23.y0, bf16[16,1536]{1,0:T(8,128)(2,1)S(1)} %collective-permute-done.7.y1, bf16[16,1536]{1,0:T(8,128)(2,1)S(1)} %collective-permute-done.8.y2, ...), custom_call_target="tpu_custom_call" | custom-call | flops 1000000 | bytes 500000 | tf_op jit(solution)/shard_map/pallas_call | solution.py:20
  (4 shorter events, 0.1 us)
Async XLA Ops:
  0.6 36.2 %copy-start.1 = (bf16[384,1536]{1,0:T(8,128)(2,1)S(1)}, bf16[384,1536]{1,0:T(8,128)(2,1)}, u32[]{:S(2)}) copy-start(bf16[384,1536]{1,0:T(8,128)(2,1)} %wown.1) | copy-start | bytes 3538948
  0.6 30.0 %copy-start.11 = (f32[1536]{0:T(1024)S(1)}, f32[1536]{0:T(1024)}, u32[]{:S(2)}) copy-start(f32[1536]{0:T(1024)} %param.28) | copy-start | bytes 18436
  0.7 30.0 %copy-start.4 = (bf16[1,2,4,2,1536]{4,3,2,1,0:T(2,128)(2,1)S(1)}, bf16[1,2,4,2,1536]{4,3,2,1,0:T(2,128)(2,1)}, u32[]{:S(2)}) copy-start(bf16[1,2,4,2,1536]{4,3,2,1,0:T(2,128)(2,1)} %q_ref) | copy-start | bytes 147460
  0.7 30.0 %copy-start.7 = (s32[1,2,4]{2,1,0:T(2,128)S(1)}, s32[1,2,4]{2,1,0:T(2,128)}, u32[]{:S(2)}) copy-start(s32[1,2,4]{2,1,0:T(2,128)} %tlen_ref.3) | copy-start | bytes 100
  0.7 30.0 %copy-start.8 = (s32[1,64]{1,0:T(1,128)S(1)}, s32[1,64]{1,0:T(1,128)}, u32[]{:S(2)}) copy-start(s32[1,64]{1,0:T(1,128)} %holder_ref.3) | copy-start | bytes 772
  0.7 30.0 %copy-start.2 = (bf16[1,4,64,256]{3,2,1,0:T(8,128)(2,1)S(1)}, bf16[1,4,64,256]{3,2,1,0:T(8,128)(2,1)}, u32[]{:S(2)}) copy-start(bf16[1,4,64,256]{3,2,1,0:T(8,128)(2,1)} %tails_ref.3) | copy-start | bytes 393220
  0.7 30.0 %copy-start.6 = (bf16[1,2,4,2,256]{4,3,2,1,0:T(2,128)(2,1)S(1)}, bf16[1,2,4,2,256]{4,3,2,1,0:T(2,128)(2,1)}, u32[]{:S(2)}) copy-start(bf16[1,2,4,2,256]{4,3,2,1,0:T(2,128)(2,1)} %new_ref.3) | copy-start | bytes 24580
  0.7 30.0 %copy-start.9 = (s32[1,2]{1,0:T(1,128)S(1)}, s32[1,2]{1,0:T(1,128)}, u32[]{:S(2)}) copy-start(s32[1,2]{1,0:T(1,128)} %plen_ref.1) | copy-start | bytes 28
  0.7 30.0 %copy-start.5 = (bf16[1,2,4,2,1536]{4,3,2,1,0:T(2,128)(2,1)S(1)}, bf16[1,2,4,2,1536]{4,3,2,1,0:T(2,128)(2,1)}, u32[]{:S(2)}) copy-start(bf16[1,2,4,2,1536]{4,3,2,1,0:T(2,128)(2,1)} %res_ref.1) | copy-start | bytes 147460
  0.7 17.7 %collective-permute-start = (bf16[384,1536]{1,0:T(8,128)(2,1)}, bf16[384,1536]{1,0:T(8,128)(2,1)S(1)}, u32[]{:S(2)}, u32[]{:S(2)}) collective-permute-start(bf16[384,1536]{1,0:T(8,128)(2,1)} %wown.1), channel_id=1, source_target_pairs={{0,1},{1,2},{2,3},{3,0},{4,7},{5,4},{6,5},{7,6},{8,9},{9,10},{10,1... | collective-permute-start | bytes 3538952 | tf_op jit(solution)/shard_map/ppermute | solution.py:301
  4.7 32.1 %all-to-all-start = ((bf16[64,40,128]{2,1,0:T(8,128)(2,1)}), bf16[64,40,128]{2,1,0:T(8,128)(2,1)S(1)}, u32[]{:S(2)}, u32[]{:S(2)}) async-start(bf16[64,40,128]{2,1,0:T(8,128)(2,1)} %bitcast.5), calls=%async_computation | async-start | bytes 1310720 | tf_op jit(solution)/shard_map/all_to_all | solution.py:314
  18.4 1.0 %copy-start.10 = (bf16[384,1536]{1,0:T(8,128)(2,1)}, bf16[384,1536]{1,0:T(8,128)(2,1)S(1)}, u32[]{:S(2)}) copy-start(bf16[384,1536]{1,0:T(8,128)(2,1)S(1)} %collective-permute-done.refs_0_) | copy-start | bytes 3538948
  19.5 11.2 %collective-permute-start.2 = (bf16[192,1536]{1,0:T(8,128)(2,1)S(1)}, bf16[192,1536]{1,0:T(8,128)(2,1)S(1)}, u32[]{:S(2)}, u32[]{:S(2)}) collective-permute-start(bf16[192,1536]{1,0:T(8,128)(2,1)S(1)} %constant_dynamic-slice_fusion), channel_id=1, source_target_pairs={{0,1},{1,2},{2,3},{3,0},{4,7},{5,4},{6,5},{7,6},{8,9},{9,10},{10,1... | collective-permute-start | bytes 1769480 | tf_op jit(solution)/shard_map/ppermute | solution.py:301
  19.9 17.0 %collective-permute-start.1 = (bf16[384,1536]{1,0:T(8,128)(2,1)}, bf16[384,1536]{1,0:T(8,128)(2,1)}, u32[]{:S(2)}, u32[]{:S(2)}) collective-permute-start(bf16[384,1536]{1,0:T(8,128)(2,1)} %copy-done.10), channel_id=1, source_target_pairs={{0,4},{4,0},{8,12},{12,8},{16,20},{20,16},{24,28},{28,24},{32,36},... | collective-permute-start | bytes 3538952 | tf_op jit(solution)/shard_map/ppermute | solution.py:297
  30.7 6.2 %collective-permute-start.3 = (bf16[192,1536]{1,0:T(8,128)(2,1)S(1)}, bf16[192,1536]{1,0:T(8,128)(2,1)S(1)}, u32[]{:S(2)}, u32[]{:S(2)}) collective-permute-start(bf16[192,1536]{1,0:T(8,128)(2,1)S(1)} %collective-permute-done.2.refs_2_), channel_id=1, source_target_pairs={{0,4},{4,0},{8,12},{12,8},{16,20},{20,16},{24,28},{28,24},{32,36},... | collective-permute-start | bytes 1769480 | tf_op jit(solution)/shard_map/ppermute | solution.py:297
  30.8 1.0 %copy-start.3 = (bf16[1,1024,256]{2,1,0:T(8,128)(2,1)S(1)}, bf16[1,1024,256]{2,1,0:T(8,128)(2,1)}, u32[]{:S(2)}) copy-start(bf16[1,1024,256]{2,1,0:T(8,128)(2,1)} %kv_ref.1) | copy-start | bytes 1572868
  39.3 8.5 %copy-start = (bf16[1536,1152]{1,0:T(8,128)(2,1)S(1)}, bf16[1536,1152]{1,0:T(8,128)(2,1)}, u32[]{:S(2)}) copy-start(bf16[1536,1152]{1,0:T(8,128)(2,1)} %wg.1) | copy-start | bytes 10616836
  39.3 6.9 %collective-permute-start.6 = (bf16[16,1536]{1,0:T(8,128)(2,1)S(1)}, bf16[16,1536]{1,0:T(8,128)(2,1)S(1)}, u32[]{:S(2)}, u32[]{:S(2)}) collective-permute-start(bf16[16,1536]{1,0:T(8,128)(2,1)S(1)} %get-tuple-element.18.x0), channel_id=1, source_target_pairs={{0,3},{1,0},{2,1},{3,2},{4,7},{5,4},{6,5},{7,6},{8,11},{9,8},{10,9... | collective-permute-start | bytes 147464 | tf_op jit(solution)/shard_map/ppermute | solution.py:294
  40.7 5.7 %collective-permute-start.5 = (bf16[16,1536]{1,0:T(8,128)(2,1)S(1)}, bf16[16,1536]{1,0:T(8,128)(2,1)S(1)}, u32[]{:S(2)}, u32[]{:S(2)}) collective-permute-start(bf16[16,1536]{1,0:T(8,128)(2,1)S(1)} %get-tuple-element.18.x0), channel_id=1, source_target_pairs={{0,2},{1,3},{2,0},{3,1},{4,6},{5,7},{6,4},{7,5},{8,10},{9,11},{10,... | collective-permute-start | bytes 147464 | tf_op jit(solution)/shard_map/ppermute | solution.py:294
  42.6 5.3 %collective-permute-start.4 = (bf16[16,1536]{1,0:T(8,128)(2,1)S(1)}, bf16[16,1536]{1,0:T(8,128)(2,1)S(1)}, u32[]{:S(2)}, u32[]{:S(2)}) collective-permute-start(bf16[16,1536]{1,0:T(8,128)(2,1)S(1)} %get-tuple-element.18.x0), channel_id=1, source_target_pairs={{0,1},{1,2},{2,3},{3,0},{4,5},{5,6},{6,7},{7,4},{8,9},{9,10},{10,1... | collective-permute-start | bytes 147464 | tf_op jit(solution)/shard_map/ppermute | solution.py:294
  47.9 4.4 %copy-start.12 = (f32[1536]{0:T(1024)S(1)}, f32[1536]{0:T(1024)}, u32[]{:S(2)}) copy-start(f32[1536]{0:T(1024)} %param.32) | copy-start | bytes 18436
  47.9 4.4 %copy-start.13 = (f32[1536]{0:T(1024)S(1)}, f32[1536]{0:T(1024)}, u32[]{:S(2)}) copy-start(f32[1536]{0:T(1024)} %param.33) | copy-start | bytes 18436
  49.8 4.2 %collective-permute-start.7 = (bf16[16,1536]{1,0:T(8,128)(2,1)S(1)}, bf16[16,1536]{1,0:T(8,128)(2,1)S(1)}, u32[]{:S(2)}, u32[]{:S(2)}) collective-permute-start(bf16[16,1536]{1,0:T(8,128)(2,1)S(1)} %get-tuple-element.24), channel_id=1, source_target_pairs={{0,3},{1,0},{2,1},{3,2},{4,7},{5,4},{6,5},{7,6},{8,11},{9,8},{10,9... | collective-permute-start | bytes 147464 | tf_op jit(solution)/shard_map/ppermute | solution.py:294
  51.0 5.6 %collective-permute-start.8 = (bf16[16,1536]{1,0:T(8,128)(2,1)S(1)}, bf16[16,1536]{1,0:T(8,128)(2,1)S(1)}, u32[]{:S(2)}, u32[]{:S(2)}) collective-permute-start(bf16[16,1536]{1,0:T(8,128)(2,1)S(1)} %get-tuple-element.25), channel_id=1, source_target_pairs={{0,2},{1,3},{2,0},{3,1},{4,6},{5,7},{6,4},{7,5},{8,10},{9,11},{10,... | collective-permute-start | bytes 147464 | tf_op jit(solution)/shard_map/ppermute | solution.py:294
  51.5 5.6 %collective-permute-start.9 = (bf16[16,1536]{1,0:T(8,128)(2,1)S(1)}, bf16[16,1536]{1,0:T(8,128)(2,1)S(1)}, u32[]{:S(2)}, u32[]{:S(2)}) collective-permute-start(bf16[16,1536]{1,0:T(8,128)(2,1)S(1)} %get-tuple-element.26), channel_id=1, source_target_pairs={{0,1},{1,2},{2,3},{3,0},{4,5},{5,6},{6,7},{7,4},{8,9},{9,10},{10,1... | collective-permute-start | bytes 147464 | tf_op jit(solution)/shard_map/ppermute | solution.py:294
